TPU v7x, 32 devices: a whole 2x2x4 slice. The times are simulated.
32 devices in a mesh: grp: 4 (over x, core), shard: 8 (over z, y).
Axes of the slice: x: 2, y: 2, z: 4, core: 2. Of those that a mesh axis runs over, the one named last changes fastest.
Arguments:
- tokens: bfloat16 [8, 512, 2048], P('grp', 'shard'), may hold values from -6 to 6
- lengths: int32 [8], P('grp'), may hold values from 128 to 512, as said below
- prenorm_gain: bfloat16 [2048], P('shard'), may hold values from 0.099609375 to 1.8984375
- query_weight: bfloat16 [2048, 2048], P('shard'), may hold values from -0.125 to 0.125
- key_weight: bfloat16 [1024, 2048], P('shard'), may hold values from -0.125 to 0.125
- value_weight: bfloat16 [1024, 2048], P('shard'), may hold values from -0.125 to 0.125
- out_weight: bfloat16 [2048, 2048], P('shard'), may hold values from -2 to 2
- midnorm_gain: bfloat16 [2048], P('shard'), may hold values from 0.099609375 to 1.8984375
- gate_weight: bfloat16 [8192, 2048], P('shard'), may hold values from -0.125 to 0.125
- up_weight: bfloat16 [8192, 2048], P('shard'), may hold values from -0.125 to 0.125
- down_weight: bfloat16 [8192, 2048], P('shard'), may hold values from -0.0625 to 0.0625
- cotangent: bfloat16 [8, 512, 2048], P('grp', 'shard'), may hold values from -6 to 6
Outputs:
- mixed: bfloat16 [8, 512, 2048], P('grp', 'shard')
- input_gradient: bfloat16 [8, 512, 2048], P('grp', 'shard')
- prenorm_gradient: float32 [2048], P('shard')
- query_gradient: float32 [2048, 2048], P('shard')
- key_gradient: float32 [1024, 2048], P('shard')
- value_gradient: float32 [1024, 2048], P('shard')
- out_gradient: float32 [2048, 2048], P('shard')
- midnorm_gradient: float32 [2048], P('shard')
- gate_gradient: float32 [8192, 2048], P('shard')
- up_gradient: float32 [8192, 2048], P('shard')
- down_gradient: float32 [8192, 2048], P('shard')
Inputs may be any that keep to these rules, and one draw needn't show every extreme that they name: Each sequence's valid slots are its first lengths[n] slots; in every draw some sequence has all 512 slots valid.
All inputs are finite; a program needn't handle non-finite values.
Results may differ from a plain program's by a relative error of at most 0.02.
Values may be sent and summed in bfloat16 or wider, within the bound.
A program may use at most 448 MiB of HBM per device.

v0:
```python
import math

import jax
import jax.numpy as jnp
from jax import lax
from jax.sharding import PartitionSpec as P

NH = 8
KVH = 4
HD = 256


epsilon = 1e-06
theta_base = 1000042.0
masked_value = -1e30


def turned(source):
    half_width = source.shape[-1] // 2
    return jnp.concatenate([-source[..., half_width:], source[..., :half_width]], -1)


def rotate(source, cosine_table, sine_table):
    return source * cosine_table + turned(source) * sine_table


def unrotate(source, cosine_table, sine_table):
    return source * cosine_table - turned(source) * sine_table


def norm_forward(source, norm_gain):
    inverse = lax.rsqrt(jnp.mean(source * source, -1, keepdims=True) + epsilon)
    return (source * inverse * norm_gain, inverse)


def norm_backward(source, inverse, norm_gain, grad_out):
    weighted = grad_out * norm_gain
    inner_sum = jnp.sum(weighted * source, -1, keepdims=True)
    grad_in = (
        inverse * weighted - source * inverse * inverse * inverse * inner_sum / source.shape[-1]
    )
    return (grad_in, jnp.sum(grad_out * source * inverse, 0))


def weight_terms(normed, query_grad, key_grad, value_grad, attended, branch_grad, shard_count):
    token_count, model_width = normed.shape
    query_share = query_grad.shape[1] // shard_count
    kv_share = key_grad.shape[1] // shard_count
    shard_rows = 2 * query_share + 2 * kv_share

    def weight_term(first_row, row_count):
        blocks = row_count // shard_rows

        def columns(matrix, share_cols):
            return matrix.reshape(token_count, blocks, share_cols)

        part_query = jnp.einsum(
            "tmr,td->mrd",
            columns(query_grad, query_share),
            normed,
            preferred_element_type=jnp.float32,
        )
        part_key = jnp.einsum(
            "tmr,td->mrd", columns(key_grad, kv_share), normed, preferred_element_type=jnp.float32
        )
        part_value = jnp.einsum(
            "tmr,td->mrd", columns(value_grad, kv_share), normed, preferred_element_type=jnp.float32
        )
        part_out = jnp.einsum(
            "tmr,td->mrd",
            columns(attended, query_share),
            branch_grad,
            preferred_element_type=jnp.float32,
        )
        return jnp.concatenate([part_query, part_key, part_value, part_out], 1).reshape(
            row_count, model_width
        )

    return (weight_term, shard_rows)


def local(
    tokens,
    lengths,
    prenorm_gain,
    query_weight,
    key_weight,
    value_weight,
    out_weight,
    midnorm_gain,
    gate_weight,
    up_weight,
    down_weight,
    cotangent,
):
    shard_count = lax.axis_size("shard")
    shard_rank = lax.axis_index("shard")
    micro_count, seq_dev, model_width = tokens.shape
    slot_count = seq_dev * shard_count
    repeat_heads = NH // KVH
    query_width = NH * HD
    kv_width = KVH * HD
    score_scale = 1.0 / math.sqrt(HD)
    local_pos = shard_rank * seq_dev + jnp.arange(seq_dev, dtype=jnp.int32)
    key_pos = jnp.arange(slot_count, dtype=jnp.int32)
    inverse_freq = theta_base ** (-(jnp.arange(0, HD, 2).astype(jnp.float32) / HD))
    angles = local_pos.astype(jnp.float32)[:, None] * inverse_freq[None, :]
    cosine_table = jnp.concatenate([jnp.cos(angles), jnp.cos(angles)], -1)[:, None, :]
    sine_table = jnp.concatenate([jnp.sin(angles), jnp.sin(angles)], -1)[:, None, :]
    gate_total = jnp.zeros(gate_weight.shape, jnp.float32)
    up_total = jnp.zeros(up_weight.shape, jnp.float32)
    down_total = jnp.zeros(down_weight.shape, jnp.float32)
    prenorm_total = jnp.zeros((model_width,), jnp.float32)
    midnorm_total = jnp.zeros((model_width,), jnp.float32)
    attn_total = None
    mixed_rows = []
    input_rows = []
    for micro_index in range(micro_count):
        gathered = (
            lax.all_gather(query_weight, "shard", axis=0, tiled=True),
            lax.all_gather(key_weight, "shard", axis=0, tiled=True),
            lax.all_gather(value_weight, "shard", axis=0, tiled=True),
            lax.all_gather(prenorm_gain, "shard", axis=0, tiled=True),
            lax.all_gather(midnorm_gain, "shard", axis=0, tiled=True),
        )
        query_full, key_full, value_full, prenorm_full, midnorm_full = gathered
        prenorm_f = prenorm_full.astype(jnp.float32)
        midnorm_f = midnorm_full.astype(jnp.float32)
        source = tokens[micro_index].astype(jnp.float32)
        length_now = lengths[micro_index]
        valid_rows = local_pos < length_now
        scaled_first, inverse_first = norm_forward(source, prenorm_f)
        normed_first = scaled_first.astype(jnp.bfloat16)
        query_pre = jnp.einsum(
            "sd,qd->sq", normed_first, query_full, preferred_element_type=jnp.float32
        ).reshape(seq_dev, NH, HD)
        key_pre = jnp.einsum(
            "sd,qd->sq", normed_first, key_full, preferred_element_type=jnp.float32
        ).reshape(seq_dev, KVH, HD)
        value_pre = jnp.einsum(
            "sd,qd->sq", normed_first, value_full, preferred_element_type=jnp.float32
        )
        query_rot = rotate(query_pre, cosine_table, sine_table).astype(jnp.bfloat16)
        key_rot = rotate(key_pre, cosine_table, sine_table).astype(jnp.bfloat16)
        key_value = jnp.concatenate(
            [key_rot.reshape(seq_dev, kv_width), value_pre.astype(jnp.bfloat16)], 1
        )
        kv_all = lax.all_gather(key_value, "shard", axis=0, tiled=True)
        keys_all = kv_all[:, :kv_width].reshape(slot_count, KVH, HD)
        values_all = kv_all[:, kv_width:].reshape(slot_count, KVH, HD)
        query_group = query_rot.reshape(seq_dev, KVH, repeat_heads, HD)
        scores = (
            jnp.einsum("skrd,tkd->krst", query_group, keys_all, preferred_element_type=jnp.float32)
            * score_scale
        )
        allowed = (key_pos[None, :] <= local_pos[:, None]) & (key_pos[None, :] < length_now)
        scores = jnp.where(allowed, scores, masked_value)
        row_max = jnp.max(scores, -1, keepdims=True)
        exp_scores = jnp.exp(scores - row_max)
        attention_probs = exp_scores / jnp.sum(exp_scores, -1, keepdims=True)
        probs_low = attention_probs.astype(jnp.bfloat16)
        attended = (
            jnp.einsum("krst,tkd->skrd", probs_low, values_all, preferred_element_type=jnp.float32)
            .astype(jnp.bfloat16)
            .reshape(seq_dev, query_width)
        )
        branch = jnp.dot(
            attended,
            lax.all_gather(out_weight, "shard", axis=0, tiled=True),
            preferred_element_type=jnp.float32,
        )
        middle = source + branch
        scaled_second, inverse_second = norm_forward(middle, midnorm_f)
        normed_second = scaled_second.astype(jnp.bfloat16)
        normed_all = lax.all_gather(normed_second, "shard", axis=0, tiled=True)
        gate_pre = jnp.einsum(
            "sd,fd->sf", normed_all, gate_weight, preferred_element_type=jnp.float32
        )
        up_pre = jnp.einsum("sd,fd->sf", normed_all, up_weight, preferred_element_type=jnp.float32)
        sigmoid_gate = jax.nn.sigmoid(gate_pre)
        silu_gate = gate_pre * sigmoid_gate
        hidden = (silu_gate * up_pre).astype(jnp.bfloat16)
        ffn_part = lax.psum_scatter(
            jnp.dot(hidden, down_weight, preferred_element_type=jnp.float32).astype(jnp.bfloat16),
            "shard",
            scatter_dimension=0,
            tiled=True,
        ).astype(jnp.float32)
        mixed_rows.append(
            jnp.where(valid_rows[:, None], middle + ffn_part, 0.0).astype(jnp.bfloat16)
        )
        cot_low = jnp.where(
            valid_rows[:, None], cotangent[micro_index], jnp.zeros_like(cotangent[micro_index])
        )
        cot_all = lax.all_gather(cot_low, "shard", axis=0, tiled=True)
        hidden_grad = jnp.einsum(
            "sd,fd->sf", cot_all, down_weight, preferred_element_type=jnp.float32
        )
        down_total = down_total + jnp.einsum(
            "sf,sd->fd", hidden, cot_all, preferred_element_type=jnp.float32
        )
        gate_grad = (
            hidden_grad * up_pre * sigmoid_gate * (1.0 + gate_pre * (1.0 - sigmoid_gate))
        ).astype(jnp.bfloat16)
        up_grad = (hidden_grad * silu_gate).astype(jnp.bfloat16)
        gate_total = gate_total + jnp.einsum(
            "sf,sd->fd", gate_grad, normed_all, preferred_element_type=jnp.float32
        )
        up_total = up_total + jnp.einsum(
            "sf,sd->fd", up_grad, normed_all, preferred_element_type=jnp.float32
        )
        second_grad = lax.psum_scatter(
            jnp.dot(gate_grad, gate_weight, preferred_element_type=jnp.float32)
            + jnp.dot(up_grad, up_weight, preferred_element_type=jnp.float32),
            "shard",
            scatter_dimension=0,
            tiled=True,
        )
        middle_part, midnorm_part = norm_backward(middle, inverse_second, midnorm_f, second_grad)
        middle_grad = cot_low.astype(jnp.float32) + middle_part
        midnorm_total = midnorm_total + midnorm_part
        branch_grad = middle_grad.astype(jnp.bfloat16)
        attended_grad = jnp.einsum(
            "sd,qd->sq",
            branch_grad,
            lax.all_gather(out_weight, "shard", axis=0, tiled=True),
            preferred_element_type=jnp.float32,
        ).astype(jnp.bfloat16)
        attended_group = attended_grad.reshape(seq_dev, KVH, repeat_heads, HD)
        probs_grad = jnp.einsum(
            "skrd,tkd->krst", attended_group, values_all, preferred_element_type=jnp.float32
        )
        inner_sum = jnp.sum(attention_probs * probs_grad, -1, keepdims=True)
        scores_grad = (attention_probs * (probs_grad - inner_sum)).astype(jnp.bfloat16)
        query_rot_grad = (
            jnp.einsum(
                "krst,tkd->skrd", scores_grad, keys_all, preferred_element_type=jnp.float32
            ).reshape(seq_dev, NH, HD)
            * score_scale
        )
        query_grad = (
            unrotate(query_rot_grad, cosine_table, sine_table)
            .astype(jnp.bfloat16)
            .reshape(seq_dev, query_width)
        )
        row_count = lax.axis_size("shard") * seq_dev
        key_part = (
            jnp.einsum(
                "krst,skrd->tkd", scores_grad, query_group, preferred_element_type=jnp.float32
            )
            * score_scale
        )
        value_part = jnp.einsum(
            "krst,skrd->tkd", probs_low, attended_group, preferred_element_type=jnp.float32
        )
        kv_grad = lax.psum_scatter(
            jnp.concatenate(
                [key_part.reshape(row_count, kv_width), value_part.reshape(row_count, kv_width)], 1
            ).astype(jnp.bfloat16),
            "shard",
            scatter_dimension=0,
            tiled=True,
        ).astype(jnp.float32)
        key_grad = (
            unrotate(kv_grad[:, :kv_width].reshape(seq_dev, KVH, HD), cosine_table, sine_table)
            .astype(jnp.bfloat16)
            .reshape(seq_dev, kv_width)
        )
        value_grad = kv_grad[:, kv_width:].astype(jnp.bfloat16)
        first_grad = jnp.einsum(
            "sq,qd->sd", query_grad, query_full, preferred_element_type=jnp.float32
        )
        first_grad = first_grad + jnp.einsum(
            "sq,qd->sd", key_grad, key_full, preferred_element_type=jnp.float32
        )
        first_grad = first_grad + jnp.einsum(
            "sq,qd->sd", value_grad, value_full, preferred_element_type=jnp.float32
        )
        source_part, prenorm_part = norm_backward(source, inverse_first, prenorm_f, first_grad)
        input_rows.append((middle_grad + source_part).astype(jnp.bfloat16))
        prenorm_total = prenorm_total + prenorm_part
        saved = (normed_first, query_grad, key_grad, value_grad, attended, branch_grad)
        weight_term, shard_rows = weight_terms(*saved, shard_count)
        reduced = lax.psum_scatter(
            weight_term(jnp.int32(0), lax.axis_size("shard") * shard_rows).astype(jnp.bfloat16),
            "shard",
            scatter_dimension=0,
            tiled=True,
        ).astype(jnp.float32)
        attn_total = reduced if attn_total is None else attn_total + reduced
    gain_sums = lax.psum((prenorm_total, midnorm_total), ("grp", "shard"))
    gain_share = model_width // shard_count
    prenorm_gradient = lax.dynamic_slice_in_dim(
        gain_sums[0], shard_rank * gain_share, gain_share, 0
    )
    midnorm_gradient = lax.dynamic_slice_in_dim(
        gain_sums[1], shard_rank * gain_share, gain_share, 0
    )
    summed = (
        lax.psum(attn_total.astype(jnp.bfloat16), "grp").astype(jnp.float32),
        lax.psum(gate_total.astype(jnp.bfloat16), "grp").astype(jnp.float32),
        lax.psum(up_total.astype(jnp.bfloat16), "grp").astype(jnp.float32),
        lax.psum(down_total.astype(jnp.bfloat16), "grp").astype(jnp.float32),
    )
    attn_rows = summed[0]
    query_share = query_width // shard_count
    kv_share = kv_width // shard_count
    query_gradient = attn_rows[:query_share]
    key_gradient = attn_rows[query_share : query_share + kv_share]
    value_gradient = attn_rows[query_share + kv_share : query_share + 2 * kv_share]
    out_gradient = attn_rows[query_share + 2 * kv_share :]
    return (
        jnp.stack(mixed_rows),
        jnp.stack(input_rows),
        prenorm_gradient,
        query_gradient,
        key_gradient,
        value_gradient,
        out_gradient,
        midnorm_gradient,
        summed[1],
        summed[2],
        summed[3],
    )


def solution(mesh):
    in_specs = (
        P("grp", "shard", None),
        P("grp"),
        P("shard"),
        P("shard", None),
        P("shard", None),
        P("shard", None),
        P("shard", None),
        P("shard"),
        P("shard", None),
        P("shard", None),
        P("shard", None),
        P("grp", "shard", None),
    )
    out_specs = (
        P("grp", "shard", None),
        P("grp", "shard", None),
        P("shard"),
        P("shard", None),
        P("shard", None),
        P("shard", None),
        P("shard", None),
        P("shard"),
        P("shard", None),
        P("shard", None),
        P("shard", None),
    )
    return jax.shard_map(local, mesh=mesh, in_specs=in_specs, out_specs=out_specs, check_vma=False)
```

profile of v0, /device:TPU:0, one launch (start us, length us, event | category | flops | bytes accessed | tf_op | source)
XLA Modules:
  0.0 2343.5 jit_solution(3952414453735895625)
XLA Ops:
  9.4 22.4 all-gather
  33.9 52.4 %all-gather.13.cloned.1.call-done = bf16[1024,2048]{1,0:T(8,128)(2,1)} async-done(((bf16[128,2048]{1,0:T(8,128)(2,1)}), bf16[1024,2048]{1,0:T(8,128)(2,1)}) %all-gather.13.cloned.1.call-update) | async-done | bytes 4194320 | tf_op jit(solution)/shard_map/all_gather | solution.py:121
  92.4 67.8 %all-gather.15.cloned.1.call-done = bf16[1024,2048]{1,0:T(8,128)(2,1)} async-done(((bf16[128,2048]{1,0:T(8,128)(2,1)}), bf16[1024,2048]{1,0:T(8,128)(2,1)}) %all-gather.15.cloned.1.call-update) | async-done | bytes 4194320 | tf_op jit(solution)/shard_map/all_gather | solution.py:122
  165.7 18.3 all-gather.1
  186.6 25.5 %all-gather.17.cloned.1.call-done = bf16[512,2048]{1,0:T(8,128)(2,1)} async-done(((bf16[64,2048]{1,0:T(8,128)(2,1)}), bf16[512,2048]{1,0:T(8,128)(2,1)}) %all-gather.17.cloned.1.call-update) | async-done | bytes 2097168 | tf_op jit(solution)/shard_map/all_gather | solution.py:148
  216.3 121.3 %all-gather.19.cloned.1.call-done = bf16[2048,2048]{1,0:T(8,128)(2,1)} async-done(((bf16[256,2048]{1,0:T(8,128)(2,1)}), bf16[2048,2048]{1,0:T(8,128)(2,1)}) %all-gather.19.cloned.1.call-update) | async-done | bytes 8388624 | tf_op jit(solution)/shard_map/all_gather | solution.py:120
  353.4 109.6 %all-gather.21.cloned.1.call-done = bf16[2048,2048]{1,0:T(8,128)(2,1)} async-done(((bf16[256,2048]{1,0:T(8,128)(2,1)}), bf16[2048,2048]{1,0:T(8,128)(2,1)}) %all-gather.21.cloned.1.call-update) | async-done | bytes 8388624 | tf_op jit(solution)/shard_map/all_gather | solution.py:169
  476.2 40.3 %all-gather.23.cloned.1.call-done = bf16[512,2048]{1,0:T(8,128)(2,1)} async-done(((bf16[64,2048]{1,0:T(8,128)(2,1)}), bf16[512,2048]{1,0:T(8,128)(2,1)}) %all-gather.23.cloned.1.call-update) | async-done | bytes 2097168 | tf_op jit(solution)/shard_map/all_gather | solution.py:175
  526.9 40.1 %all-gather.29.cloned.1.call-done = bf16[512,2048]{1,0:T(8,128)(2,1)} async-done(((bf16[64,2048]{1,0:T(8,128)(2,1)}), bf16[512,2048]{1,0:T(8,128)(2,1)}) %all-gather.29.cloned.1.call-update) | async-done | bytes 2097168 | tf_op jit(solution)/shard_map/all_gather | solution.py:195
  588.4 29.2 %all-gather.25.cloned.1.call-done = bf16[512,2048]{1,0:T(8,128)(2,1)} async-done(((bf16[64,2048]{1,0:T(8,128)(2,1)}), bf16[512,2048]{1,0:T(8,128)(2,1)}) %all-gather.25.cloned.1.call-update) | async-done | bytes 2097168 | tf_op jit(solution)/shard_map/all_gather | solution.py:148
  636.6 71.7 %reduce-scatter.13.cloned.1.call-done = f32[64,2048]{1,0:T(8,128)} async-done(((f32[512,2048]{1,0:T(8,128)}), f32[64,2048]{1,0:T(8,128)}) %reduce-scatter.13.cloned.1.call-update) | async-done | bytes 524304 | tf_op jit(solution)/shard_map/reduce_scatter | solution.py:212
  710.2 70.0 %reduce-scatter.9.cloned.1.call-done = bf16[64,2048]{1,0:T(8,128)(2,1)} async-done(((bf16[512,2048]{1,0:T(8,128)(2,1)}), bf16[64,2048]{1,0:T(8,128)(2,1)}) %reduce-scatter.9.cloned.1.call-update) | async-done | bytes 262160 | tf_op jit(solution)/shard_map/reduce_scatter | solution.py:183
  783.0 48.4 %all-gather.27.cloned.1.call-done = bf16[512,2048]{1,0:T(8,128)(2,1)} async-done(((bf16[64,2048]{1,0:T(8,128)(2,1)}), bf16[512,2048]{1,0:T(8,128)(2,1)}) %all-gather.27.cloned.1.call-update) | async-done | bytes 2097168 | tf_op jit(solution)/shard_map/all_gather | solution.py:175
  841.8 40.2 %all-gather.31.cloned.1.call-done = bf16[512,2048]{1,0:T(8,128)(2,1)} async-done(((bf16[64,2048]{1,0:T(8,128)(2,1)}), bf16[512,2048]{1,0:T(8,128)(2,1)}) %all-gather.31.cloned.1.call-update) | async-done | bytes 2097168 | tf_op jit(solution)/shard_map/all_gather | solution.py:195
  926.9 57.4 %reduce-scatter.17.cloned.1.call-done = f32[64,2048]{1,0:T(8,128)} async-done(((f32[512,2048]{1,0:T(8,128)}), f32[64,2048]{1,0:T(8,128)}) %reduce-scatter.17.cloned.1.call-update) | async-done | bytes 524304 | tf_op jit(solution)/shard_map/reduce_scatter | solution.py:212
  986.0 69.8 %reduce-scatter.11.cloned.1.call-done = bf16[64,2048]{1,0:T(8,128)(2,1)} async-done(((bf16[512,2048]{1,0:T(8,128)(2,1)}), bf16[64,2048]{1,0:T(8,128)(2,1)}) %reduce-scatter.11.cloned.1.call-update) | async-done | bytes 262160 | tf_op jit(solution)/shard_map/reduce_scatter | solution.py:183
  1084.3 42.1 %reduce-scatter.15.cloned.1.call-done = bf16[64,2048]{1,0:T(8,128)(2,1)} async-done(((bf16[512,2048]{1,0:T(8,128)(2,1)}), bf16[64,2048]{1,0:T(8,128)(2,1)}) %reduce-scatter.15.cloned.1.call-update) | async-done | bytes 262160 | tf_op jit(solution)/shard_map/reduce_scatter | solution.py:256
  1143.7 53.3 %reduce-scatter.19.cloned.1.call-done = bf16[64,2048]{1,0:T(8,128)(2,1)} async-done(((bf16[512,2048]{1,0:T(8,128)(2,1)}), bf16[64,2048]{1,0:T(8,128)(2,1)}) %reduce-scatter.19.cloned.1.call-update) | async-done | bytes 262160 | tf_op jit(solution)/shard_map/reduce_scatter | solution.py:256
  1209.7 17.3 pad_maximum_fusion.1
  1246.4 17.7 pad_maximum_fusion
  1294.7 335.3 %reduce-scatter.23.cloned.1.call-done = bf16[768,2048]{1,0:T(8,128)(2,1)} async-done(((bf16[6144,2048]{1,0:T(8,128)(2,1)}), bf16[768,2048]{1,0:T(8,128)(2,1)}) %reduce-scatter.23.cloned.1.call-update) | async-done | bytes 3145744 | tf_op jit(solution)/shard_map/reduce_scatter | solution.py:284
  1629.9 406.5 %reduce-scatter.21.cloned.1.call-done = bf16[768,2048]{1,0:T(8,128)(2,1)} async-done(((bf16[6144,2048]{1,0:T(8,128)(2,1)}), bf16[768,2048]{1,0:T(8,128)(2,1)}) %reduce-scatter.21.cloned.1.call-update) | async-done | bytes 3145744 | tf_op jit(solution)/shard_map/reduce_scatter | solution.py:284
  2071.2 41.1 %all-reduce = (f32[2048]{0:T(1024)S(1)}, f32[2048]{0:T(1024)S(1)}) all-reduce(f32[2048]{0:T(1024)S(1)} %add.195, f32[2048]{0:T(1024)S(1)} %add.198), channel_id=1, replica_groups=mesh['grp'=4,'shard'=8] {'grp','shard'}, use_global_device_ids=true, to_apply=%region_22.23 | all-reduce | flops 4096 | bytes 32768 | tf_op jit(solution)/shard_map/psum | solution.py:291
  2114.8 201.1 %all-reduce.4.cloned.1.call-done = (bf16[768,2048]{1,0:T(8,128)(2,1)}, bf16[1024,2048]{1,0:T(8,128)(2,1)}, bf16[1024,2048]{1,0:T(8,128)(2,1)}, bf16[1024,2048]{1,0:T(8,128)(2,1)}) async-done(((bf16[768,2048]{1,0:T(8,128)(2,1)}, bf16[1024,2048]{1,0:T(8,128)(2,1)}, bf16[1024,2048]{1,0:T(8,128)(2,1)}, bf16[1024,2048]{1,0:T(8,128)(2,1)}), (bf16[768,2048]{1,0:T(8,128)(2,1)}, bf16[1024,2048]{1,0:T(8,128)(2,1)}, ...) | async-done | bytes 15728656 | tf_op jit(solution)/shard_map/psum | solution.py:300
  (348 shorter events, 328.9 us)
Async XLA Ops:
  7.2 79.1 %all-gather.13.cloned.1.call-start = ((), (), s32[]{:S(2)}) async-start(), calls=%async_computation.8 | async-start | bytes 4718592 | tf_op jit(solution)/shard_map/all_gather | solution.py:121
  7.9 152.2 %all-gather.15.cloned.1.call-start = ((), (), s32[]{:S(2)}) async-start(), calls=%async_computation.9 | async-start | bytes 4718592 | tf_op jit(solution)/shard_map/all_gather | solution.py:122
  8.7 203.5 %all-gather.17.cloned.1.call-start = ((), (), s32[]{:S(2)}) async-start(), calls=%async_computation.10 | async-start | bytes 2359296 | tf_op jit(solution)/shard_map/all_gather | solution.py:148
  33.9 303.7 %copy-start.43 = (f32[64]{0:T(128)}, f32[64]{0:T(128)S(1)}, u32[]{:S(2)}) copy-start(f32[64]{0:T(128)S(1)} %get-tuple-element.114) | copy-start | bytes 772
  33.9 310.0 %copy-start.40 = (f32[64]{0:T(128)}, f32[64]{0:T(128)S(1)}, u32[]{:S(2)}) copy-start(f32[64]{0:T(128)S(1)} %get-tuple-element.113) | copy-start | bytes 772
  164.5 173.1 %all-gather.19.cloned.1.call-start = ((), (), s32[]{:S(2)}) async-start(), calls=%async_computation.11 | async-start | bytes 9437184 | tf_op jit(solution)/shard_map/all_gather | solution.py:120
  165.0 298.0 %all-gather.21.cloned.1.call-start = ((), (), s32[]{:S(2)}) async-start(), calls=%async_computation.12 | async-start | bytes 9437184 | tf_op jit(solution)/shard_map/all_gather | solution.py:169
  165.6 350.9 %all-gather.23.cloned.1.call-start = ((), (), s32[]{:S(2)}) async-start(), calls=%async_computation.13 | async-start | bytes 2359296 | tf_op jit(solution)/shard_map/all_gather | solution.py:175
  349.5 566.9 %copy-start.10 = (f32[4,2,64,512]{3,2,1,0:T(8,128)}, f32[4,2,64,512]{3,2,1,0:T(8,128)S(1)}, u32[]{:S(2)}) copy-start(f32[4,2,64,512]{3,2,1,0:T(8,128)S(1)} %get-tuple-element.93) | copy-start | bytes 3145732
  469.0 98.1 %all-gather.29.cloned.1.call-start = ((), (), s32[]{:S(2)}) async-start(), calls=%async_computation.18 | async-start | bytes 2359296 | tf_op jit(solution)/shard_map/all_gather | solution.py:195
  471.3 146.3 %all-gather.25.cloned.1.call-start = ((), (), s32[]{:S(2)}) async-start(), calls=%async_computation.15 | async-start | bytes 2359296 | tf_op jit(solution)/shard_map/all_gather | solution.py:148
  475.7 232.7 %reduce-scatter.13.cloned.1.call-start = ((), (), s32[]{:S(2)}) async-start(), calls=%async_computation.19 | async-start | bytes 4718592 | tf_op jit(solution)/shard_map/reduce_scatter | solution.py:212
  582.3 197.9 %reduce-scatter.9.cloned.1.call-start = ((), (), s32[]{:S(2)}) async-start(), calls=%async_computation.14 | async-start | bytes 2359296 | tf_op jit(solution)/shard_map/reduce_scatter | solution.py:183
  588.2 243.2 %all-gather.27.cloned.1.call-start = ((), (), s32[]{:S(2)}) async-start(), calls=%async_computation.16 | async-start | bytes 2359296 | tf_op jit(solution)/shard_map/all_gather | solution.py:175
  630.9 149.3 %copy-start.13 = (bf16[64,2048]{1,0:T(8,128)(2,1)S(1)}, bf16[64,2048]{1,0:T(8,128)(2,1)}, u32[]{:S(2)}) copy-start(bf16[64,2048]{1,0:T(8,128)(2,1)} %get-tuple-element.51) | copy-start | bytes 786436
  782.4 99.6 %all-gather.31.cloned.1.call-start = ((), (), s32[]{:S(2)}) async-start(), calls=%async_computation.21 | async-start | bytes 2359296 | tf_op jit(solution)/shard_map/all_gather | solution.py:195
  783.0 201.2 %reduce-scatter.17.cloned.1.call-start = ((), (), s32[]{:S(2)}) async-start(), calls=%async_computation.22 | async-start | bytes 4718592 | tf_op jit(solution)/shard_map/reduce_scatter | solution.py:212
  897.7 158.1 %reduce-scatter.11.cloned.1.call-start = ((), (), s32[]{:S(2)}) async-start(), calls=%async_computation.17 | async-start | bytes 2359296 | tf_op jit(solution)/shard_map/reduce_scatter | solution.py:183
  903.9 222.5 %reduce-scatter.15.cloned.1.call-start = ((), (), s32[]{:S(2)}) async-start(), calls=%async_computation.20 | async-start | bytes 2359296 | tf_op jit(solution)/shard_map/reduce_scatter | solution.py:256
  923.5 132.3 %copy-start.51 = (pred[64]{0:T(512)(128)(4,1)S(1)}, pred[64]{0:T(512)(128)(4,1)}, u32[]{:S(2)}) copy-start(pred[64]{0:T(512)(128)(4,1)} %copy-done.50) | copy-start | bytes 196
  926.8 270.3 %reduce-scatter.19.cloned.1.call-start = ((), (), s32[]{:S(2)}) async-start(), calls=%async_computation.23 | async-start | bytes 2359296 | tf_op jit(solution)/shard_map/reduce_scatter | solution.py:256
  1080.7 549.3 %reduce-scatter.23.cloned.1.call-start = ((), (), s32[]{:S(2)}) async-start(), calls=%async_computation.25 | async-start | bytes 28311552 | tf_op jit(solution)/shard_map/reduce_scatter | solution.py:284
  1227.1 809.3 %reduce-scatter.21.cloned.1.call-start = ((), (), s32[]{:S(2)}) async-start(), calls=%async_computation.24 | async-start | bytes 28311552 | tf_op jit(solution)/shard_map/reduce_scatter | solution.py:284
  1264.1 1051.8 %all-reduce.4.cloned.1.call-start = ((), (), s32[]{:S(2)}) async-start(), calls=%async_computation.26 | async-start | bytes 31457280 | tf_op jit(solution)/shard_map/psum | solution.py:300
  (75 other events, 1678.7 us)
Sparse Core Ops, SparseCore 0:
  10.1 76.1 all-gather.12
  88.4 71.6 all-gather.14
  164.6 47.5 all-gather.16
  214.1 123.4 all-gather.18
  339.6 123.3 all-gather.20
  469.1 47.4 all-gather.22
  519.3 47.7 all-gather.28
  569.8 47.7 all-gather.24
  621.8 86.5 reduce-scatter.12
  712.7 67.3 reduce-scatter.8
  783.1 48.2 all-gather.26
  834.2 47.7 all-gather.30
  897.8 86.3 reduce-scatter.16
  988.2 67.5 reduce-scatter.10
  1059.8 66.5 reduce-scatter.14
  1130.4 66.6 reduce-scatter.18
  1227.2 402.6 reduce-scatter.22
  1633.7 402.7 reduce-scatter.20
  2042.8 273.1 all-reduce.3
where the time goes:
time: 2350 us; the launch traced here: 2340 us
  waiting for transfers between devices  1890 us (80%)
  matrix products  213 us (9%)
  other arithmetic  99.2 us (4%)
  blocking collectives  81.7 us (3%)
  local copies, waits for them, and re-layouts  45.9 us (2%)
    reduce_scatter x2, waiting for transfers between devices, local(): lax.psum_scatter(weight_term(jnp.int32(0), lax.axis_size('shard') * shard...  742 us
    psum x1, waiting for transfers between devices, local(): lax.psum(attn_total.astype(jnp.bfloat16), 'grp').astype(jnp.float32)  201 us
    reduce_scatter x2, waiting for transfers between devices, local(): lax.psum_scatter(jnp.dot(hidden, down_weight, preferred_element_type=jnp....  140 us
    reduce_scatter x2, waiting for transfers between devices, local(): lax.psum_scatter(jnp.dot(gate_grad, gate_weight, preferred_element_type=j...  129 us
    all_gather x1, waiting for transfers between devices, local(): lax.all_gather(query_weight, 'shard', axis=0, tiled=True)  121 us
    all_gather x1, waiting for transfers between devices, local(): lax.all_gather(out_weight, 'shard', axis=0, tiled=True)  110 us
    reduce_scatter x2, waiting for transfers between devices, local(): lax.psum_scatter(jnp.concatenate([key_part.reshape(row_count, kv_width),...  95.5 us
    all_gather x2, waiting for transfers between devices, local(): normed_all = lax.all_gather(normed_second, 'shard', axis=0, tiled=True)  88.7 us
  transfers between devices with their start and end apart: 19, of which 19 were waited for; matrix products, arithmetic and copies ran while one was open for 12% of the time, Pallas kernels for 0%

commit v1 on v0

--- a/solution.py
+++ b/solution.py
@@ -79,7 +79,7 @@
     return (weight_term, shard_rows)
 
 
-def local(
+def local_rows(
     tokens,
     lengths,
     prenorm_gain,
@@ -324,7 +324,194 @@
     )
 
 
+def local_heads(
+    tokens,
+    lengths,
+    prenorm_gain,
+    query_weight,
+    key_weight,
+    value_weight,
+    out_weight,
+    midnorm_gain,
+    gate_weight,
+    up_weight,
+    down_weight,
+    cotangent,
+):
+    low = jnp.bfloat16
+    shard_count = lax.axis_size("shard")
+    shard_rank = lax.axis_index("shard")
+    seqs, seq_dev, model_width = tokens.shape
+    slot_count = seq_dev * shard_count
+    own_rows = seqs * seq_dev
+    score_scale = 1.0 / math.sqrt(HD)
+    pairs = [[2 * pair, 2 * pair + 1] for pair in range(shard_count // 2)]
+    half = HD // 2
+    upper = shard_rank % 2
+
+    def gather(rows):
+        width = rows.shape[-1]
+        return lax.all_gather(rows.reshape(seqs, seq_dev, width), "shard", axis=1, tiled=True)
+
+    def scatter(partial):
+        return lax.psum_scatter(
+            partial.astype(low), "shard", scatter_dimension=1, tiled=True
+        ).reshape(own_rows, partial.shape[-1])
+
+    def times(rows, weight):
+        return jnp.einsum("sta,ba->stb", rows, weight, preferred_element_type=jnp.float32)
+
+    def into(rows, weight):
+        return jnp.einsum("stb,ba->sta", rows, weight, preferred_element_type=jnp.float32)
+
+    def outer(left, right):
+        return jnp.einsum("stb,sta->ba", left, right, preferred_element_type=jnp.float32)
+
+    key_pos = jnp.arange(slot_count, dtype=jnp.int32)
+    local_pos = shard_rank * seq_dev + jnp.arange(seq_dev, dtype=jnp.int32)
+    inverse_freq = theta_base ** (-(jnp.arange(0, HD, 2).astype(jnp.float32) / HD))
+    angles = key_pos.astype(jnp.float32)[:, None] * inverse_freq[None, :]
+    cosine_table = jnp.concatenate([jnp.cos(angles), jnp.cos(angles)], -1)
+    sine_table = jnp.concatenate([jnp.sin(angles), jnp.sin(angles)], -1)
+
+    prenorm_f = lax.all_gather(prenorm_gain, "shard", axis=0, tiled=True).astype(jnp.float32)
+    midnorm_f = lax.all_gather(midnorm_gain, "shard", axis=0, tiled=True).astype(jnp.float32)
+    valid_rows = (local_pos[None, :] < lengths[:, None]).reshape(own_rows, 1)
+    cot_low = jnp.where(valid_rows, cotangent.reshape(own_rows, model_width), jnp.zeros((), low))
+
+    key_head = lax.all_gather(
+        key_weight, "shard", axis=0, tiled=True, axis_index_groups=pairs
+    )
+    value_head = lax.all_gather(
+        value_weight, "shard", axis=0, tiled=True, axis_index_groups=pairs
+    )
+
+    source = tokens.reshape(own_rows, model_width).astype(jnp.float32)
+    scaled_first, inverse_first = norm_forward(source, prenorm_f)
+    normed_first = gather(scaled_first.astype(low))
+    cot_all = gather(cot_low)
+
+    queries = rotate(times(normed_first, query_weight), cosine_table, sine_table).astype(low)
+    keys = rotate(times(normed_first, key_head), cosine_table, sine_table).astype(low)
+    values = times(normed_first, value_head).astype(low)
+    scores = (
+        jnp.einsum("sqd,skd->sqk", queries, keys, preferred_element_type=jnp.float32) * score_scale
+    )
+    allowed = (key_pos[None, None, :] <= key_pos[None, :, None]) & (
+        key_pos[None, None, :] < lengths[:, None, None]
+    )
+    scores = jnp.where(allowed, scores, masked_value)
+    exp_scores = jnp.exp(scores - jnp.max(scores, -1, keepdims=True))
+    probs = exp_scores / jnp.sum(exp_scores, -1, keepdims=True)
+    probs_low = probs.astype(low)
+    attended = jnp.einsum(
+        "sqk,skd->sqd", probs_low, values, preferred_element_type=jnp.float32
+    ).astype(low)
+    middle = source + scatter(into(attended, out_weight)).astype(jnp.float32)
+    scaled_second, inverse_second = norm_forward(middle, midnorm_f)
+    normed_second = gather(scaled_second.astype(low))
+
+    gate_pre = times(normed_second, gate_weight)
+    up_pre = times(normed_second, up_weight)
+    sigmoid_gate = jax.nn.sigmoid(gate_pre)
+    silu_gate = gate_pre * sigmoid_gate
+    hidden = (silu_gate * up_pre).astype(low)
+    hidden_grad = times(cot_all, down_weight)
+    gate_grad = (
+        hidden_grad * up_pre * sigmoid_gate * (1.0 + gate_pre * (1.0 - sigmoid_gate))
+    ).astype(low)
+    up_grad = (hidden_grad * silu_gate).astype(low)
+    second_grad = scatter(into(gate_grad, gate_weight) + into(up_grad, up_weight)).astype(
+        jnp.float32
+    )
+    ffn_part = scatter(into(hidden, down_weight)).astype(jnp.float32)
+    mixed = jnp.where(valid_rows, middle + ffn_part, 0.0).astype(low)
+    gate_total = lax.psum(outer(gate_grad, normed_second).astype(low), "grp")
+    up_total = lax.psum(outer(up_grad, normed_second).astype(low), "grp")
+    down_total = lax.psum(outer(hidden, cot_all).astype(low), "grp")
+
+    middle_part, midnorm_part = norm_backward(middle, inverse_second, midnorm_f, second_grad)
+    middle_grad = cot_low.astype(jnp.float32) + middle_part
+    branch_grad = gather(middle_grad.astype(low))
+    attended_grad = times(branch_grad, out_weight).astype(low)
+    out_total = outer(attended, branch_grad)
+    probs_grad = jnp.einsum(
+        "sqd,skd->sqk", attended_grad, values, preferred_element_type=jnp.float32
+    )
+    inner_sum = jnp.sum(probs * probs_grad, -1, keepdims=True)
+    scores_grad = (probs * (probs_grad - inner_sum)).astype(low)
+    query_grad = unrotate(
+        jnp.einsum("sqk,skd->sqd", scores_grad, keys, preferred_element_type=jnp.float32)
+        * score_scale,
+        cosine_table,
+        sine_table,
+    ).astype(low)
+    key_grad = unrotate(
+        jnp.einsum("sqk,sqd->skd", scores_grad, queries, preferred_element_type=jnp.float32)
+        * score_scale,
+        cosine_table,
+        sine_table,
+    ).astype(low)
+    value_grad = jnp.einsum(
+        "sqk,sqd->skd", probs_low, attended_grad, preferred_element_type=jnp.float32
+    ).astype(low)
+    first_grad = scatter(
+        into(query_grad, query_weight) + into(key_grad, key_head) + into(value_grad, value_head)
+    ).astype(jnp.float32)
+
+    def halves(grad):
+        first, second = grad[..., :half], grad[..., half:]
+        return (
+            jnp.where(upper == 0, first, second),
+            jnp.where(upper == 0, second, first),
+        )
+
+    key_own, key_other = halves(key_grad)
+    value_own, value_other = halves(value_grad)
+    swaps = [(rank, rank ^ 1) for rank in range(shard_count)]
+    swapped = lax.ppermute(jnp.concatenate([key_other, value_other], -1), "shard", swaps)
+    key_own = (key_own.astype(jnp.float32) + swapped[..., :half].astype(jnp.float32)).astype(low)
+    value_own = (value_own.astype(jnp.float32) + swapped[..., half:].astype(jnp.float32)).astype(
+        low
+    )
+    attn_total = lax.psum(
+        jnp.concatenate(
+            [
+                outer(query_grad, normed_first),
+                outer(key_own, normed_first),
+                outer(value_own, normed_first),
+                out_total,
+            ],
+            0,
+        ).astype(low),
+        "grp",
+    )
+    source_part, prenorm_part = norm_backward(source, inverse_first, prenorm_f, first_grad)
+    input_gradient = (middle_grad + source_part).astype(low)
+
+    gain_sums = lax.psum(jnp.stack([prenorm_part, midnorm_part]), ("grp", "shard"))
+    gain_share = model_width // shard_count
+    gain_own = lax.dynamic_slice_in_dim(gain_sums, shard_rank * gain_share, gain_share, 1)
+    f32 = jnp.float32
+    share = query_weight.shape[0]
+    kv_share = key_weight.shape[0]
+    return (
+        mixed.reshape(tokens.shape),
+        input_gradient.reshape(tokens.shape),
+        gain_own[0],
+        attn_total[:share].astype(f32),
+        attn_total[share : share + kv_share].astype(f32),
+        attn_total[share + kv_share : share + 2 * kv_share].astype(f32),
+        attn_total[share + 2 * kv_share :].astype(f32),
+        gain_own[1],
+        gate_total.astype(f32),
+        up_total.astype(f32),
+        down_total.astype(f32),
+    )
+
+
 def solution(mesh):
+    local = local_heads if mesh.shape["shard"] == NH else local_rows
     in_specs = (
         P("grp", "shard", None),
         P("grp"),

time: 2350 us -> 1140 us (0.49)
  waiting for transfers between devices: 1890 us -> 860 us
  matrix products: 213 us -> 120 us
  other arithmetic: 99.2 us -> 44.1 us
  local copies, waits for them, and re-layouts: 45.9 us -> 3.36 us
    reduce_scatter x8 -> x4, waiting for transfers between devices: 1110 us -> 327 us  [scatter(): lax.psum_scatter(partial.astype(low), 'shard', scatter_dimension=1, tiled...]
    all_gather x10 -> x6, waiting for transfers between devices: 575 us -> 268 us  [the longest x4 256 us: gather(): lax.all_gather(rows.reshape(seqs, seq_dev, width), 'shard', axis=1, tiled...]
    dot_general x54 -> x26, matrix products: 213 us -> 117 us  [the longest x7 46.7 us: times(): jnp.einsum('sta,ba->stb', rows, weight, preferred_element_type=jnp.float32)]
    psum x1, waiting for transfers between devices: 201 us -> 255 us  [local_heads(): lax.psum(jnp.concatenate([outer(query_grad, normed_first), outer(key_own,...]
    concatenate x7 -> x2, other arithmetic: 42.7 us -> 2 us  [the longest x1 1.97 us: local_heads(): jnp.concatenate([outer(query_grad, normed_first), outer(key_own, normed_f...]
  transfers between devices with their start and end apart: 19 -> 12, of which waited for: 19 -> 11; matrix products, arithmetic and copies ran while one was open for 12% -> 8% of each run, Pallas kernels for 0% -> 0%
where the time goes in v1:
time: 1140 us; the launch traced here: 1130 us
  waiting for transfers between devices  860 us (75%)
  matrix products  120 us (11%)
  blocking collectives  82.6 us (7%)
  other arithmetic  44.1 us (4%)
  between operations  14.8 us (1%)
    reduce_scatter x4, waiting for transfers between devices, scatter(): lax.psum_scatter(partial.astype(low), 'shard', scatter_dimension=1, tiled...  327 us
    all_gather x4, waiting for transfers between devices, gather(): lax.all_gather(rows.reshape(seqs, seq_dev, width), 'shard', axis=1, tiled...  256 us
    psum x1, waiting for transfers between devices, local_heads(): lax.psum(jnp.concatenate([outer(query_grad, normed_first), outer(key_own,...  255 us
    dot_general x7, matrix products, times(): jnp.einsum('sta,ba->stb', rows, weight, preferred_element_type=jnp.float32)  46.7 us
    psum x1, blocking collectives, local_heads(): lax.psum(jnp.stack([prenorm_part, midnorm_part]), ('grp', 'shard'))  40.4 us
    dot_general x7, matrix products, into(): jnp.einsum('stb,ba->sta', rows, weight, preferred_element_type=jnp.float32)  36 us
    dot_general x7, matrix products, outer(): jnp.einsum('stb,sta->ba', left, right, preferred_element_type=jnp.float32)  26.3 us
  transfers between devices with their start and end apart: 12, of which 11 were waited for; matrix products, arithmetic and copies ran while one was open for 8% of the time, Pallas kernels for 0%

profile of v1, /device:TPU:0, one launch (start us, length us, event | category | flops | bytes accessed | tf_op | source)
XLA Modules:
  0.0 1131.0 jit_solution(13568092393736963254)
XLA Ops:
  8.6 22.3 %all-gather = bf16[8,1,256]{2,1,0:T(2,128)(2,1)S(1)} all-gather(bf16[1,1,256]{2,1,0:T(2,128)(2,1)S(1)} %reshape.279), channel_id=1, replica_groups=mesh['grp'=4,'shard'=8] {'shard'}, dimensions={0}, use_global_device_ids=true | all-gather | bytes 4608 | tf_op jit(solution)/shard_map/all_gather | solution.py:377
  37.8 72.0 %all-gather.9.cloned.1.call-done = bf16[2,512,2048]{2,1,0:T(8,128)(2,1)} async-done(((bf16[2,64,2048]{2,1,0:T(8,128)(2,1)}), bf16[2,512,2048]{2,1,0:T(8,128)(2,1)}) %all-gather.9.cloned.1.call-update) | async-done | bytes 4194320 | tf_op jit(solution)/shard_map/all_gather | solution.py:354
  119.2 11.8 %all-gather.13.cloned.1.call-done = bf16[256,2048]{1,0:T(8,128)(2,1)} async-done(((bf16[128,2048]{1,0:T(8,128)(2,1)}), bf16[256,2048]{1,0:T(8,128)(2,1)}) %all-gather.13.cloned.1.call-update) | async-done | bytes 1048592 | tf_op jit(solution)/shard_map/all_gather | solution.py:385
  145.0 19.9 %all-gather.1 = bf16[8,1,256]{2,1,0:T(2,128)(2,1)S(1)} all-gather(bf16[1,1,256]{2,1,0:T(2,128)(2,1)S(1)} %reshape.281), channel_id=1, replica_groups=mesh['grp'=4,'shard'=8] {'shard'}, dimensions={0}, use_global_device_ids=true | all-gather | bytes 4608 | tf_op jit(solution)/shard_map/all_gather | solution.py:378
  164.9 67.0 %reduce-scatter.5.cloned.1.call-done = bf16[2,64,2048]{2,1,0:T(8,128)(2,1)} async-done(((bf16[2,512,2048]{2,1,0:T(8,128)(2,1)}), bf16[2,64,2048]{2,1,0:T(8,128)(2,1)}) %reduce-scatter.5.cloned.1.call-update) | async-done | bytes 524304 | tf_op jit(solution)/shard_map/reduce_scatter | solution.py:357
  235.7 72.3 %all-gather.17.cloned.1.call-done = bf16[2,512,2048]{2,1,0:T(8,128)(2,1)} async-done(((bf16[2,64,2048]{2,1,0:T(8,128)(2,1)}), bf16[2,512,2048]{2,1,0:T(8,128)(2,1)}) %all-gather.17.cloned.1.call-update) | async-done | bytes 4194320 | tf_op jit(solution)/shard_map/all_gather | solution.py:354
  307.9 10.0 fusion.3
  317.9 64.5 %all-gather.15.cloned.1.call-done = bf16[2,512,2048]{2,1,0:T(8,128)(2,1)} async-done(((bf16[2,64,2048]{2,1,0:T(8,128)(2,1)}), bf16[2,512,2048]{2,1,0:T(8,128)(2,1)}) %all-gather.15.cloned.1.call-update) | async-done | bytes 4194320 | tf_op jit(solution)/shard_map/all_gather | solution.py:354
  382.5 10.1 fusion.9
  392.6 11.0 multiply_convert_fusion.1
  403.7 6.7 fusion.7
  410.4 8.2 add_convert_fusion.1
  418.7 86.4 %reduce-scatter.9.cloned.1.call-done = bf16[2,64,2048]{2,1,0:T(8,128)(2,1)} async-done(((bf16[2,512,2048]{2,1,0:T(8,128)(2,1)}), bf16[2,64,2048]{2,1,0:T(8,128)(2,1)}) %reduce-scatter.9.cloned.1.call-update) | async-done | bytes 524304 | tf_op jit(solution)/shard_map/reduce_scatter | solution.py:357
  512.1 9.6 bitcast_convert_fusion.2
  528.0 6.5 bitcast_convert_fusion
  534.5 47.3 %all-gather.19.cloned.1.call-done = bf16[2,512,2048]{2,1,0:T(8,128)(2,1)} async-done(((bf16[2,64,2048]{2,1,0:T(8,128)(2,1)}), bf16[2,512,2048]{2,1,0:T(8,128)(2,1)}) %all-gather.19.cloned.1.call-update) | async-done | bytes 4194320 | tf_op jit(solution)/shard_map/all_gather | solution.py:354
  598.8 8.4 collective-permute-done
  610.7 9.3 fusion.16
  627.6 255.4 %all-reduce.3.cloned.1.call-done = (bf16[768,2048]{1,0:T(8,128)(2,1)}, bf16[1024,2048]{1,0:T(8,128)(2,1)}, bf16[1024,2048]{1,0:T(8,128)(2,1)}, bf16[1024,2048]{1,0:T(8,128)(2,1)}) async-done(((bf16[768,2048]{1,0:T(8,128)(2,1)}, bf16[1024,2048]{1,0:T(8,128)(2,1)}, bf16[1024,2048]{1,0:T(8,128)(2,1)}, bf16[1024,2048]{1,0:T(8,128)(2,1)}), (bf16[768,2048]{1,0:T(8,128)(2,1)}, bf16[1024,2048]{1,0:T(8,128)(2,1)}, ...) | async-done | bytes 15728656 | tf_op jit(solution)/shard_map/psum | solution.py:477
  883.0 6.8 convert_element_type.241
  893.9 81.3 %reduce-scatter.7.cloned.1.call-done = bf16[2,64,2048]{2,1,0:T(8,128)(2,1)} async-done(((bf16[2,512,2048]{2,1,0:T(8,128)(2,1)}), bf16[2,64,2048]{2,1,0:T(8,128)(2,1)}) %reduce-scatter.7.cloned.1.call-update) | async-done | bytes 524304 | tf_op jit(solution)/shard_map/reduce_scatter | solution.py:357
  975.3 92.4 %reduce-scatter.11.cloned.1.call-done = bf16[2,64,2048]{2,1,0:T(8,128)(2,1)} async-done(((bf16[2,512,2048]{2,1,0:T(8,128)(2,1)}), bf16[2,64,2048]{2,1,0:T(8,128)(2,1)}) %reduce-scatter.11.cloned.1.call-update) | async-done | bytes 524304 | tf_op jit(solution)/shard_map/reduce_scatter | solution.py:357
  1070.3 40.4 %psum.35 = f32[2,2048]{1,0:T(2,128)S(1)} all-reduce(f32[2,2048]{1,0:T(2,128)S(1)} %pad_maximum_fusion.4), channel_id=1, replica_groups=mesh['grp'=4,'shard'=8] {'grp','shard'}, use_global_device_ids=true, to_apply=%region_13.14 | all-reduce | flops 4096 | bytes 32768 | tf_op jit(solution)/shard_map/psum | solution.py:492
  1110.7 6.8 convert_element_type.243
  (150 shorter events, 89.5 us)
Async XLA Ops:
  7.2 132.0 %copy-start = (bf16[256,2048]{1,0:T(8,128)(2,1)S(1)}, bf16[256,2048]{1,0:T(8,128)(2,1)}, u32[]{:S(2)}) copy-start(bf16[256,2048]{1,0:T(8,128)(2,1)} %param.18) | copy-start | bytes 3145732
  7.2 30.6 %all-gather.11.cloned.1.call-start = ((), (), s32[]{:S(2)}) async-start(), calls=%async_computation.5 | async-start | bytes 1572864 | tf_op jit(solution)/shard_map/all_gather | solution.py:382
  7.9 101.9 %all-gather.9.cloned.1.call-start = ((), (), s32[]{:S(2)}) async-start(), calls=%async_computation.4 | async-start | bytes 4718592 | tf_op jit(solution)/shard_map/all_gather | solution.py:354
  34.2 96.8 %all-gather.13.cloned.1.call-start = ((), (), s32[]{:S(2)}) async-start(), calls=%async_computation.6 | async-start | bytes 1572864 | tf_op jit(solution)/shard_map/all_gather | solution.py:385
  34.9 197.0 %reduce-scatter.5.cloned.1.call-start = ((), (), s32[]{:S(2)}) async-start(), calls=%async_computation.7 | async-start | bytes 4718592 | tf_op jit(solution)/shard_map/reduce_scatter | solution.py:357
  117.2 18.5 %copy-start.13 = (bf16[2,512,256]{1,2,0:T(8,128)(2,1)}, bf16[2,512,256]{1,2,0:T(8,128)(2,1)S(1)}, u32[]{:S(2)}) copy-start(bf16[2,512,256]{1,2,0:T(8,128)(2,1)S(1)} %get-tuple-element.31) | copy-start | bytes 1572868
  117.2 391.4 %copy-start.11 = (bf16[2,512,256]{1,2,0:T(8,128)(2,1)}, bf16[2,512,256]{1,2,0:T(8,128)(2,1)S(1)}, u32[]{:S(2)}) copy-start(bf16[2,512,256]{1,2,0:T(8,128)(2,1)S(1)} %get-tuple-element.32) | copy-start | bytes 1572868
  143.8 88.1 %copy-start.4 = (bf16[2,64,2048]{2,1,0:T(8,128)(2,1)S(1)}, bf16[2,64,2048]{2,1,0:T(8,128)(2,1)}, u32[]{:S(2)}) copy-start(bf16[2,64,2048]{2,1,0:T(8,128)(2,1)} %param.12) | copy-start | bytes 1572868
  143.8 164.1 %all-gather.17.cloned.1.call-start = ((), (), s32[]{:S(2)}) async-start(), calls=%async_computation.10 | async-start | bytes 4718592 | tf_op jit(solution)/shard_map/all_gather | solution.py:354
  144.9 237.6 %all-gather.15.cloned.1.call-start = ((), (), s32[]{:S(2)}) async-start(), calls=%async_computation.8 | async-start | bytes 4718592 | tf_op jit(solution)/shard_map/all_gather | solution.py:354
  235.3 269.9 %reduce-scatter.9.cloned.1.call-start = ((), (), s32[]{:S(2)}) async-start(), calls=%async_computation.11 | async-start | bytes 4718592 | tf_op jit(solution)/shard_map/reduce_scatter | solution.py:357
  382.5 10.1 copy-start.24
  382.5 10.1 copy-start.26
  392.6 11.1 copy-start.23
  418.6 86.5 %copy-start.6 = (bf16[2,64,2048]{2,1,0:T(8,128)(2,1)S(1)}, bf16[2,64,2048]{2,1,0:T(8,128)(2,1)}, u32[]{:S(2)}) copy-start(bf16[2,64,2048]{2,1,0:T(8,128)(2,1)} %reduce-scatter.5.cloned.1.call-done) | copy-start | bytes 1572868
  418.7 163.1 %all-gather.19.cloned.1.call-start = ((), (), s32[]{:S(2)}) async-start(), calls=%async_computation.12 | async-start | bytes 4718592 | tf_op jit(solution)/shard_map/all_gather | solution.py:354
  508.4 374.6 %all-reduce.3.cloned.1.call-start = ((), (), s32[]{:S(2)}) async-start(), calls=%async_computation.14 | async-start | bytes 31457280 | tf_op jit(solution)/shard_map/psum | solution.py:477
  512.1 9.6 copy-start.27
  512.1 9.6 copy-start.32
  594.7 12.5 %collective-permute-start = (bf16[2,512,256]{1,2,0:T(8,128)(2,1)S(1)}, bf16[2,512,256]{1,2,0:T(8,128)(2,1)S(1)}, u32[]{:S(2)}, u32[]{:S(2)}) collective-permute-start(bf16[2,512,256]{1,2,0:T(8,128)(2,1)S(1)} %pad_maximum_fusion.3), channel_id=1, source_target_pairs={{0,1},{1,0},{2,3},{3,2},{4,5},{5,4},{6,7},{7,6},{8,9},{9,8},{10,11... | collective-permute-start | bytes 1572872 | tf_op jit(solution)/shard_map/ppermute | solution.py:472
  610.7 364.6 %reduce-scatter.7.cloned.1.call-start = ((), (), s32[]{:S(2)}) async-start(), calls=%async_computation.9 | async-start | bytes 4718592 | tf_op jit(solution)/shard_map/reduce_scatter | solution.py:357
  620.1 447.6 %reduce-scatter.11.cloned.1.call-start = ((), (), s32[]{:S(2)}) async-start(), calls=%async_computation.13 | async-start | bytes 4718592 | tf_op jit(solution)/shard_map/reduce_scatter | solution.py:357
  889.9 177.8 %copy-start.20 = (bf16[2,64,2048]{2,1,0:T(8,128)(2,1)S(1)}, bf16[2,64,2048]{2,1,0:T(8,128)(2,1)}, u32[]{:S(2)}) copy-start(bf16[2,64,2048]{2,1,0:T(8,128)(2,1)} %reduce-scatter.9.cloned.1.call-done) | copy-start | bytes 1572868
  1110.7 6.8 copy-start.7
  (22 other events, 84.5 us)
Sparse Core Ops, SparseCore 0:
  9.6 24.0 all-gather.10
  36.4 73.3 all-gather.8
  111.4 19.5 all-gather.12
  143.9 87.9 reduce-scatter.4
  234.8 73.1 all-gather.16
  310.8 71.6 all-gather.14
  418.8 86.3 reduce-scatter.8
  508.6 73.1 all-gather.18
  610.8 272.2 all-reduce.2
  887.1 88.1 reduce-scatter.6
  979.9 87.6 reduce-scatter.10

commit v2 on v1

--- a/solution.py
+++ b/solution.py
@@ -1,13 +1,387 @@
+import functools
 import math
 
 import jax
 import jax.numpy as jnp
 from jax import lax
+from jax.experimental import pallas as pl
+from jax.experimental.pallas import tpu as pltpu
 from jax.sharding import PartitionSpec as P
+
+MESH = pl.DeviceIdType.MESH
+DEPTH = 2
 
 NH = 8
 KVH = 4
 HD = 256
+
+
+def greet(me, line, cross):
+    z = me // 2
+    barrier = pltpu.get_barrier_semaphore()
+    def signal(peer):
+        pl.semaphore_signal(barrier, inc=1, device_id={"shard": peer}, device_id_type=MESH)
+    signal(cross)
+    @pl.when(z > 0)
+    def _(): signal(me - 2)
+    @pl.when(z < line - 1)
+    def _(): signal(me + 2)
+    ends = jnp.where(z > 0, 1, 0) + jnp.where(z < line - 1, 1, 0)
+    pl.semaphore_wait(barrier, 1 + ends)
+
+
+def gather_kernel(line, split, own_ref, out_ref, local_sem, send_sem, recv_sem):
+    me = lax.axis_index("shard")
+    z, y = me // 2, lax.rem(me, 2)
+    cross = me + 1 - 2 * y
+    rows = own_ref.shape[0]
+    parts = [pl.ds(0, split), pl.ds(split, rows - split)] if split < rows else [pl.ds(0, rows)]
+    greet(me, line, cross)
+    keep = pltpu.make_async_copy(own_ref, out_ref.at[me], local_sem)
+    keep.start()
+    UP, DOWN, CROSS = 0, 1, 2
+    def copy(way, origin, part, own=False):
+        peer = {UP: me + 2, DOWN: me - 2, CROSS: cross}[way]
+        return pltpu.make_async_remote_copy(
+            src_ref=own_ref.at[parts[part]] if own else out_ref.at[origin, parts[part]],
+            dst_ref=out_ref.at[origin, parts[part]],
+            send_sem=send_sem.at[way, origin, part],
+            recv_sem=recv_sem.at[origin, part],
+            device_id={"shard": peer}, device_id_type=MESH)
+    def arrived(origin, part):
+        copy(CROSS, origin, part).wait_recv()
+    sent = []
+    def send(cond, way, origin, part, own=False):
+        c = copy(way, origin, part, own)
+        if cond is None:
+            c.start()
+        else:
+            pl.when(cond)(c.start)
+        sent.append((cond, way, origin, part, own))
+    has_b = len(parts) > 1
+    if has_b:
+        send(None, CROSS, me, 1, True)
+    send(None, CROSS, me, 0, True)
+    send(z < line - 1, UP, me, 0, True)
+    send(z > 0, DOWN, me, 0, True)
+    if has_b:
+        send(z < line - 1, UP, me, 1, True)
+        send(z > 0, DOWN, me, 1, True)
+        arrived(cross, 1)
+        send(z < line - 1, UP, cross, 1)
+        send(z > 0, DOWN, cross, 1)
+    for k in range(1, line):
+        for part in range(len(parts)):
+            for other in ([False] if part == 0 else [False, True]):
+                for sign in (-1, 1):
+                    origin = me + 2 * k * sign + (1 - 2 * y if other else 0)
+                    there = z >= k if sign < 0 else z + k < line
+                    way = UP if sign < 0 else DOWN
+                    more = (there & (z < line - 1)) if sign < 0 else (there & (z > 0))
+                    pl.when(there)(functools.partial(arrived, origin, part))
+                    send(more, way, origin, part)
+                    if part == 0:
+                        send(there, CROSS, origin, 0)
+    for k in range(line):
+        arrived(2 * k + 1 - y, 0)
+    for cond, way, origin, part, own in sent:
+        c = copy(way, origin, part, own)
+        if cond is None:
+            c.wait_send()
+        else:
+            pl.when(cond)(c.wait_send)
+    keep.wait()
+
+def gather(own, count, ident, space=pltpu.VMEM, split=112):
+    rows, width = own.shape
+    return pl.pallas_call(
+        functools.partial(gather_kernel, count // 2, split),
+        out_shape=jax.ShapeDtypeStruct((count, rows, width), own.dtype),
+        in_specs=[pl.BlockSpec(memory_space=space)],
+        out_specs=pl.BlockSpec(memory_space=space),
+        scratch_shapes=[pltpu.SemaphoreType.DMA, pltpu.SemaphoreType.DMA((3, count, 2)), pltpu.SemaphoreType.DMA((count, 2))],
+        compiler_params=pltpu.CompilerParams(collective_id=ident, has_side_effects=True),
+        name=f"gather{ident}")(own)
+
+def total_into(dst, *srcs):
+    rows = dst.shape[0]
+    step = 16
+    @pl.loop(0, rows // step)
+    def _(i):
+        at = pl.ds(pl.multiple_of(i * step, step), step)
+        v = srcs[0][at].astype(jnp.float32)
+        for s in srcs[1:]:
+            v = v + s[at].astype(jnp.float32)
+        dst[at] = v.astype(dst.dtype)
+
+def reduce_kernel(line, split, in_ref, out_ref, cross_in, up_in, down_in, up_out, down_out, bup_in, bdn_in, bup_out, bdn_out, bx_out, bx_in, send_sem, recv_sem):
+    me = lax.axis_index("shard")
+    z, y = me // 2, lax.rem(me, 2)
+    cross = me + 1 - 2 * y
+    rows = in_ref.shape[1]
+    A = pl.ds(0, split); B = pl.ds(split, rows - split)
+    has_b = rows > split
+    greet(me, line, cross)
+    UP, DOWN, CROSS, BUP0, BUP1, BDN0, BDN1, BX = range(8)
+    def desc(way, slot, src, dst, peer):
+        return pltpu.make_async_remote_copy(src_ref=src, dst_ref=dst, send_sem=send_sem.at[way, slot], recv_sem=recv_sem.at[way, slot], device_id={"shard": peer}, device_id_type=MESH)
+    def cross_copy(dest):
+        return desc(CROSS, dest, in_ref.at[2 * dest + 1 - y, A], cross_in.at[dest], cross)
+    def up_copy(dest, src=None):
+        return desc(UP, dest, up_out.at[dest] if src is None else src, up_in.at[dest], me + 2)
+    def down_copy(dest, src=None):
+        return desc(DOWN, dest, down_out.at[dest] if src is None else src, down_in.at[dest], me - 2)
+    def b_copy(up, dest, o, src=None):
+        buf_o, buf_i = (bup_out, bup_in) if up else (bdn_out, bdn_in)
+        return desc((BUP0 if up else BDN0) + o, dest, buf_o.at[dest, o] if src is None else src, buf_i.at[dest, o], me + 2 if up else me - 2)
+    def bx_copy():
+        return desc(BX, 0, bx_out, bx_in, cross)
+    def col(o):
+        return y if o == 0 else 1 - y
+    tables = []
+    for zz in range(line):
+        seq = []
+        for k in range(line - 1, -1, -1):
+            for d in ((zz + k, zz - k) if k else (zz,)):
+                if 0 <= d < line:
+                    seq.append(d)
+        tables.append(seq)
+    def nth(i):
+        d = jnp.int32(tables[0][i])
+        for zz in range(1, line):
+            d = jnp.where(z == zz, tables[zz][i], d)
+        return d
+    order = [nth(i) for i in range(line)]
+    for i in range(DEPTH):
+        cross_copy(order[i]).start()
+    def b_hop(up, dest):
+        first = (z == 0) if up else (z == line - 1)
+        for o in (1, 0):
+            mine = in_ref.at[2 * dest + col(o), B]
+            @pl.when(first)
+            def _():
+                b_copy(up, dest, o, mine).start()
+            @pl.when(jnp.logical_not(first))
+            def _():
+                b_copy(up, dest, o).wait_recv()
+                buf_o, buf_i = (bup_out, bup_in) if up else (bdn_out, bdn_in)
+                total_into(buf_o.at[dest, o], mine, buf_i.at[dest, o])
+                b_copy(up, dest, o).start()
+    def a_hop(up, dest):
+        first = (z == 0) if up else (z == line - 1)
+        buf_o, buf_i = (up_out, up_in) if up else (down_out, down_in)
+        c = (up_copy if up else down_copy)(dest)
+        mine = in_ref.at[2 * dest + y, A]
+        @pl.when(first)
+        def _():
+            total_into(buf_o.at[dest], mine, cross_in.at[dest])
+        @pl.when(jnp.logical_not(first))
+        def _():
+            c.wait_recv()
+            total_into(buf_o.at[dest], mine, cross_in.at[dest], buf_i.at[dest])
+        c.start()
+    for i in range(line - 1):
+        if has_b:
+            pl.when(order[i] > z)(lambda: b_hop(True, order[i]))
+            pl.when(order[i] < z)(lambda: b_hop(False, order[i]))
+    for i in range(line - 1):
+        cross_copy(order[i]).wait_recv()
+        if i + DEPTH < line:
+            cross_copy(order[i + DEPTH]).start()
+        pl.when(order[i] > z)(lambda: a_hop(True, order[i]))
+        pl.when(order[i] < z)(lambda: a_hop(False, order[i]))
+    low_end, high_end = z == 0, z == line - 1
+    def finish(dst, mine, ups, downs):
+        @pl.when(low_end)
+        def _(): total_into(dst, *mine, downs)
+        @pl.when(high_end)
+        def _(): total_into(dst, *mine, ups)
+        @pl.when(jnp.logical_not(low_end | high_end))
+        def _(): total_into(dst, *mine, ups, downs)
+    if has_b:
+        for o in (1, 0):
+            pl.when(jnp.logical_not(low_end))(lambda: b_copy(True, z, o).wait_recv())
+            pl.when(jnp.logical_not(high_end))(lambda: b_copy(False, z, o).wait_recv())
+            if o:
+                finish(bx_out, (in_ref.at[2 * z + col(o), B],), bup_in.at[z, o], bdn_in.at[z, o])
+                bx_copy().start()
+        bx_copy().wait_recv()
+        finish(out_ref.at[B], (in_ref.at[me, B], bx_in), bup_in.at[z, 0], bdn_in.at[z, 0])
+    cross_copy(z).wait_recv()
+    pl.when(jnp.logical_not(low_end))(lambda: up_copy(z).wait_recv())
+    pl.when(jnp.logical_not(high_end))(lambda: down_copy(z).wait_recv())
+    finish(out_ref.at[A], (in_ref.at[me, A], cross_in.at[z]), up_in.at[z], down_in.at[z])
+    if has_b:
+        bx_copy().wait_send()
+    for dest in range(line):
+        cross_copy(dest).wait_send()
+        @pl.when(dest > z)
+        def _():
+            up_copy(dest).wait_send()
+            if has_b:
+                b_copy(True, dest, 0).wait_send(); b_copy(True, dest, 1).wait_send()
+        @pl.when(dest < z)
+        def _():
+            down_copy(dest).wait_send()
+            if has_b:
+                b_copy(False, dest, 0).wait_send(); b_copy(False, dest, 1).wait_send()
+
+def reduce(parts, ident, split=112, out_dtype=jnp.float32):
+    count, rows, width = parts.shape
+    line = count // 2
+    V = pltpu.VMEM; d = parts.dtype
+    b = max(rows - split, 16)
+    return pl.pallas_call(
+        functools.partial(reduce_kernel, line, split),
+        out_shape=jax.ShapeDtypeStruct((rows, width), out_dtype),
+        in_specs=[pl.BlockSpec(memory_space=V)],
+        out_specs=pl.BlockSpec(memory_space=V),
+        scratch_shapes=[V((line, split, width), d)] * 5 + [V((line, 2, b, width), d)] * 4 + [V((b, width), d)] * 2 + [pltpu.SemaphoreType.DMA((8, line)), pltpu.SemaphoreType.DMA((8, line))],
+        compiler_params=pltpu.CompilerParams(collective_id=ident, has_side_effects=True),
+        name=f"reduce{ident}")(parts)
+
+
+def everyone(axis, count, me, barrier):
+    for step in range(1, count):
+        pl.semaphore_signal(
+            barrier, inc=1, device_id={axis: lax.rem(me + step, count)}, device_id_type=MESH
+        )
+    pl.semaphore_wait(barrier, count - 1)
+
+
+def small_gather_kernel(count, own_ref, out_ref, send_sem, recv_sem):
+    me = lax.axis_index("shard")
+    everyone("shard", count, me, pltpu.get_barrier_semaphore())
+
+    def copy(step, peer, origin):
+        return pltpu.make_async_remote_copy(
+            src_ref=own_ref,
+            dst_ref=out_ref.at[origin],
+            send_sem=send_sem.at[step],
+            recv_sem=recv_sem.at[step],
+            device_id={"shard": peer},
+            device_id_type=MESH,
+        )
+
+    for step in range(1, count):
+        copy(step, lax.rem(me + step, count), me).start()
+    out_ref[me] = own_ref[...]
+    for step in range(1, count):
+        c = copy(step, me, lax.rem(me + count - step, count))
+        c.wait_send()
+        c.wait_recv()
+
+
+def small_gather(own, count, ident):
+    return pl.pallas_call(
+        functools.partial(small_gather_kernel, count),
+        out_shape=jax.ShapeDtypeStruct((count,) + own.shape, own.dtype),
+        in_specs=[pl.BlockSpec(memory_space=pltpu.VMEM)],
+        out_specs=pl.BlockSpec(memory_space=pltpu.VMEM),
+        scratch_shapes=[pltpu.SemaphoreType.DMA((count,)), pltpu.SemaphoreType.DMA((count,))],
+        compiler_params=pltpu.CompilerParams(collective_id=ident, has_side_effects=True),
+        name="small_gather",
+    )(own)
+
+
+def gain_sum_kernel(count, groups, parts_ref, out_ref, first, held, second, send_sem, recv_sem, send2, recv2):
+    me = lax.axis_index("shard")
+    group = lax.axis_index("grp")
+    barrier = pltpu.get_barrier_semaphore()
+    for step in range(1, count):
+        pl.semaphore_signal(
+            barrier, inc=1, device_id={"shard": lax.rem(me + step, count)}, device_id_type=MESH
+        )
+    for step in range(1, groups):
+        pl.semaphore_signal(
+            barrier, inc=1, device_id={"grp": lax.rem(group + step, groups)}, device_id_type=MESH
+        )
+    pl.semaphore_wait(barrier, count + groups - 2)
+
+    def copy(step, peer, origin):
+        return pltpu.make_async_remote_copy(
+            src_ref=parts_ref.at[peer],
+            dst_ref=first.at[origin],
+            send_sem=send_sem.at[step],
+            recv_sem=recv_sem.at[step],
+            device_id={"shard": peer},
+            device_id_type=MESH,
+        )
+
+    def copy2(step, peer, origin):
+        return pltpu.make_async_remote_copy(
+            src_ref=held,
+            dst_ref=second.at[origin],
+            send_sem=send2.at[step],
+            recv_sem=recv2.at[step],
+            device_id={"grp": peer},
+            device_id_type=MESH,
+        )
+
+    for step in range(1, count):
+        copy(step, lax.rem(me + step, count), me).start()
+    first[me] = parts_ref[me]
+    for step in range(1, count):
+        copy(step, me, lax.rem(me + count - step, count)).wait_recv()
+    total = first[0]
+    for peer in range(1, count):
+        total = total + first[peer]
+    held[...] = total
+    second[group] = total
+    for step in range(1, groups):
+        copy2(step, lax.rem(group + step, groups), group).start()
+    for step in range(1, groups):
+        copy2(step, group, lax.rem(group + groups - step, groups)).wait_recv()
+    total = second[0]
+    for peer in range(1, groups):
+        total = total + second[peer]
+    out_ref[...] = total
+    for step in range(1, count):
+        copy(step, lax.rem(me + step, count), me).wait_send()
+    for step in range(1, groups):
+        copy2(step, lax.rem(group + step, groups), group).wait_send()
+
+
+def gain_sum(parts, groups, ident):
+    count = parts.shape[0]
+    shape = parts.shape[1:]
+    vmem = pltpu.VMEM
+    dma = pltpu.SemaphoreType.DMA
+    return pl.pallas_call(
+        functools.partial(gain_sum_kernel, count, groups),
+        out_shape=jax.ShapeDtypeStruct(shape, parts.dtype),
+        in_specs=[pl.BlockSpec(memory_space=vmem)],
+        out_specs=pl.BlockSpec(memory_space=vmem),
+        scratch_shapes=[
+            vmem((count,) + shape, parts.dtype),
+            vmem(shape, parts.dtype),
+            vmem((groups,) + shape, parts.dtype),
+            dma((count,)),
+            dma((count,)),
+            dma((groups,)),
+            dma((groups,)),
+        ],
+        compiler_params=pltpu.CompilerParams(collective_id=ident, has_side_effects=True),
+        name="gain_sum",
+    )(parts)
+
+
+def group_total(part):
+    rank = lax.axis_index("grp")
+    core = lax.rem(rank, 2)
+    rows = part.shape[0] // 2
+    cores = [(0, 1), (1, 0), (2, 3), (3, 2)]
+    chips = [(0, 2), (2, 0), (1, 3), (3, 1)]
+    f32 = jnp.float32
+    first, second = part[:rows], part[rows:]
+    mine = jnp.where(core == 0, first, second)
+    other = lax.ppermute(jnp.where(core == 0, second, first), "grp", cores)
+    pair = (mine.astype(f32) + other.astype(f32)).astype(part.dtype)
+    whole = (pair.astype(f32) + lax.ppermute(pair, "grp", chips).astype(f32)).astype(part.dtype)
+    swapped = lax.ppermute(whole, "grp", cores)
+    return jnp.concatenate(
+        [jnp.where(core == 0, whole, swapped), jnp.where(core == 0, swapped, whole)], 0
+    ).astype(f32)
 
 
 epsilon = 1e-06
@@ -345,27 +719,39 @@
     slot_count = seq_dev * shard_count
     own_rows = seqs * seq_dev
     score_scale = 1.0 / math.sqrt(HD)
-    pairs = [[2 * pair, 2 * pair + 1] for pair in range(shard_count // 2)]
     half = HD // 2
     upper = shard_rank % 2
 
-    def gather(rows):
+    def all_rows(rows, ident):
+        return gather(rows, shard_count, ident, pl.ANY).reshape(shard_count * own_rows, -1)
+
+    def scatter(partial, ident):
+        return reduce(partial.astype(low).reshape(shard_count, own_rows, -1), ident)
+
+    def by_seq(rows):
         width = rows.shape[-1]
-        return lax.all_gather(rows.reshape(seqs, seq_dev, width), "shard", axis=1, tiled=True)
-
-    def scatter(partial):
-        return lax.psum_scatter(
-            partial.astype(low), "shard", scatter_dimension=1, tiled=True
-        ).reshape(own_rows, partial.shape[-1])
+        return (
+            rows.reshape(shard_count, seqs, seq_dev, width)
+            .transpose(1, 0, 2, 3)
+            .reshape(seqs, slot_count, width)
+        )
+
+    def by_device(rows):
+        width = rows.shape[-1]
+        return (
+            rows.reshape(seqs, shard_count, seq_dev, width)
+            .transpose(1, 0, 2, 3)
+            .reshape(shard_count * own_rows, width)
+        )
 
     def times(rows, weight):
-        return jnp.einsum("sta,ba->stb", rows, weight, preferred_element_type=jnp.float32)
+        return jnp.einsum("ta,ba->tb", rows, weight, preferred_element_type=jnp.float32)
 
     def into(rows, weight):
-        return jnp.einsum("stb,ba->sta", rows, weight, preferred_element_type=jnp.float32)
+        return jnp.dot(rows, weight, preferred_element_type=jnp.float32)
 
     def outer(left, right):
-        return jnp.einsum("stb,sta->ba", left, right, preferred_element_type=jnp.float32)
+        return jnp.einsum("tb,ta->ba", left, right, preferred_element_type=jnp.float32)
 
     key_pos = jnp.arange(slot_count, dtype=jnp.int32)
     local_pos = shard_rank * seq_dev + jnp.arange(seq_dev, dtype=jnp.int32)
@@ -374,26 +760,35 @@
     cosine_table = jnp.concatenate([jnp.cos(angles), jnp.cos(angles)], -1)
     sine_table = jnp.concatenate([jnp.sin(angles), jnp.sin(angles)], -1)
 
-    prenorm_f = lax.all_gather(prenorm_gain, "shard", axis=0, tiled=True).astype(jnp.float32)
-    midnorm_f = lax.all_gather(midnorm_gain, "shard", axis=0, tiled=True).astype(jnp.float32)
+    gains = jnp.broadcast_to(
+        jnp.stack([prenorm_gain, midnorm_gain])[:, None, :], (2, 8, prenorm_gain.shape[0])
+    ).reshape(16, -1)
+    gains = small_gather(gains, shard_count, 1).astype(jnp.float32)
+    prenorm_f = gains[:, 0].reshape(-1)
+    midnorm_f = gains[:, 8].reshape(-1)
     valid_rows = (local_pos[None, :] < lengths[:, None]).reshape(own_rows, 1)
     cot_low = jnp.where(valid_rows, cotangent.reshape(own_rows, model_width), jnp.zeros((), low))
 
-    key_head = lax.all_gather(
-        key_weight, "shard", axis=0, tiled=True, axis_index_groups=pairs
-    )
-    value_head = lax.all_gather(
-        value_weight, "shard", axis=0, tiled=True, axis_index_groups=pairs
-    )
+    swaps = [(rank, rank ^ 1) for rank in range(shard_count)]
+    swapped = lax.ppermute(jnp.concatenate([key_weight, value_weight], 0), "shard", swaps)
+    key_swap, value_swap = swapped[:half], swapped[half:]
+
+    def whole_head(own, other):
+        return jnp.concatenate(
+            [jnp.where(upper == 0, own, other), jnp.where(upper == 0, other, own)], 0
+        )
+
+    key_head = whole_head(key_weight, key_swap)
+    value_head = whole_head(value_weight, value_swap)
 
     source = tokens.reshape(own_rows, model_width).astype(jnp.float32)
     scaled_first, inverse_first = norm_forward(source, prenorm_f)
-    normed_first = gather(scaled_first.astype(low))
-    cot_all = gather(cot_low)
-
-    queries = rotate(times(normed_first, query_weight), cosine_table, sine_table).astype(low)
-    keys = rotate(times(normed_first, key_head), cosine_table, sine_table).astype(low)
-    values = times(normed_first, value_head).astype(low)
+    normed_first = all_rows(scaled_first.astype(low), 2)
+    cot_all = all_rows(cot_low, 3)
+
+    queries = rotate(by_seq(times(normed_first, query_weight)), cosine_table, sine_table).astype(low)
+    keys = rotate(by_seq(times(normed_first, key_head)), cosine_table, sine_table).astype(low)
+    values = by_seq(times(normed_first, value_head).astype(low))
     scores = (
         jnp.einsum("sqd,skd->sqk", queries, keys, preferred_element_type=jnp.float32) * score_scale
     )
@@ -404,12 +799,14 @@
     exp_scores = jnp.exp(scores - jnp.max(scores, -1, keepdims=True))
     probs = exp_scores / jnp.sum(exp_scores, -1, keepdims=True)
     probs_low = probs.astype(low)
-    attended = jnp.einsum(
-        "sqk,skd->sqd", probs_low, values, preferred_element_type=jnp.float32
-    ).astype(low)
-    middle = source + scatter(into(attended, out_weight)).astype(jnp.float32)
+    attended = by_device(
+        jnp.einsum(
+            "sqk,skd->sqd", probs_low, values, preferred_element_type=jnp.float32
+        ).astype(low)
+    )
+    middle = source + scatter(into(attended, out_weight), 4)
     scaled_second, inverse_second = norm_forward(middle, midnorm_f)
-    normed_second = gather(scaled_second.astype(low))
+    normed_second = all_rows(scaled_second.astype(low), 5)
 
     gate_pre = times(normed_second, gate_weight)
     up_pre = times(normed_second, up_weight)
@@ -421,43 +818,42 @@
         hidden_grad * up_pre * sigmoid_gate * (1.0 + gate_pre * (1.0 - sigmoid_gate))
     ).astype(low)
     up_grad = (hidden_grad * silu_gate).astype(low)
-    second_grad = scatter(into(gate_grad, gate_weight) + into(up_grad, up_weight)).astype(
-        jnp.float32
-    )
-    ffn_part = scatter(into(hidden, down_weight)).astype(jnp.float32)
+    second_grad = scatter(into(gate_grad, gate_weight) + into(up_grad, up_weight), 6)
+    ffn_part = scatter(into(hidden, down_weight), 7)
     mixed = jnp.where(valid_rows, middle + ffn_part, 0.0).astype(low)
-    gate_total = lax.psum(outer(gate_grad, normed_second).astype(low), "grp")
-    up_total = lax.psum(outer(up_grad, normed_second).astype(low), "grp")
-    down_total = lax.psum(outer(hidden, cot_all).astype(low), "grp")
+    gate_total = group_total(outer(gate_grad, normed_second).astype(low))
+    up_total = group_total(outer(up_grad, normed_second).astype(low))
+    down_total = group_total(outer(hidden, cot_all).astype(low))
 
     middle_part, midnorm_part = norm_backward(middle, inverse_second, midnorm_f, second_grad)
     middle_grad = cot_low.astype(jnp.float32) + middle_part
-    branch_grad = gather(middle_grad.astype(low))
-    attended_grad = times(branch_grad, out_weight).astype(low)
+    branch_grad = all_rows(middle_grad.astype(low), 8)
+    attended_grad = by_seq(times(branch_grad, out_weight).astype(low))
     out_total = outer(attended, branch_grad)
     probs_grad = jnp.einsum(
         "sqd,skd->sqk", attended_grad, values, preferred_element_type=jnp.float32
     )
     inner_sum = jnp.sum(probs * probs_grad, -1, keepdims=True)
     scores_grad = (probs * (probs_grad - inner_sum)).astype(low)
-    query_grad = unrotate(
+    query_grad = by_device(unrotate(
         jnp.einsum("sqk,skd->sqd", scores_grad, keys, preferred_element_type=jnp.float32)
         * score_scale,
         cosine_table,
         sine_table,
-    ).astype(low)
-    key_grad = unrotate(
+    ).astype(low))
+    key_grad = by_device(unrotate(
         jnp.einsum("sqk,sqd->skd", scores_grad, queries, preferred_element_type=jnp.float32)
         * score_scale,
         cosine_table,
         sine_table,
-    ).astype(low)
-    value_grad = jnp.einsum(
+    ).astype(low))
+    value_grad = by_device(jnp.einsum(
         "sqk,sqd->skd", probs_low, attended_grad, preferred_element_type=jnp.float32
-    ).astype(low)
+    ).astype(low))
     first_grad = scatter(
-        into(query_grad, query_weight) + into(key_grad, key_head) + into(value_grad, value_head)
-    ).astype(jnp.float32)
+        into(query_grad, query_weight) + into(key_grad, key_head) + into(value_grad, value_head),
+        9,
+    )
 
     def halves(grad):
         first, second = grad[..., :half], grad[..., half:]
@@ -468,45 +864,44 @@
 
     key_own, key_other = halves(key_grad)
     value_own, value_other = halves(value_grad)
-    swaps = [(rank, rank ^ 1) for rank in range(shard_count)]
     swapped = lax.ppermute(jnp.concatenate([key_other, value_other], -1), "shard", swaps)
     key_own = (key_own.astype(jnp.float32) + swapped[..., :half].astype(jnp.float32)).astype(low)
     value_own = (value_own.astype(jnp.float32) + swapped[..., half:].astype(jnp.float32)).astype(
         low
     )
-    attn_total = lax.psum(
+    out_total = group_total(out_total.astype(low))
+    attn_total = group_total(
         jnp.concatenate(
             [
                 outer(query_grad, normed_first),
                 outer(key_own, normed_first),
                 outer(value_own, normed_first),
-                out_total,
             ],
             0,
-        ).astype(low),
-        "grp",
+        ).astype(low)
     )
     source_part, prenorm_part = norm_backward(source, inverse_first, prenorm_f, first_grad)
     input_gradient = (middle_grad + source_part).astype(low)
 
-    gain_sums = lax.psum(jnp.stack([prenorm_part, midnorm_part]), ("grp", "shard"))
-    gain_share = model_width // shard_count
-    gain_own = lax.dynamic_slice_in_dim(gain_sums, shard_rank * gain_share, gain_share, 1)
-    f32 = jnp.float32
+    gain_parts = jnp.stack([prenorm_part, midnorm_part]).reshape(2, shard_count, 1, -1)
+    gain_parts = jnp.broadcast_to(
+        gain_parts.transpose(1, 0, 2, 3), (shard_count, 2, 8, gain_parts.shape[-1])
+    )
+    gain_own = gain_sum(gain_parts, lax.axis_size("grp"), 10)[:, 0]
     share = query_weight.shape[0]
     kv_share = key_weight.shape[0]
     return (
         mixed.reshape(tokens.shape),
         input_gradient.reshape(tokens.shape),
         gain_own[0],
-        attn_total[:share].astype(f32),
-        attn_total[share : share + kv_share].astype(f32),
-        attn_total[share + kv_share : share + 2 * kv_share].astype(f32),
-        attn_total[share + 2 * kv_share :].astype(f32),
+        attn_total[:share],
+        attn_total[share : share + kv_share],
+        attn_total[share + kv_share :],
+        out_total,
         gain_own[1],
-        gate_total.astype(f32),
-        up_total.astype(f32),
-        down_total.astype(f32),
+        gate_total,
+        up_total,
+        down_total,
     )
 
 

time: 1140 us -> 729 us (0.64)
  waiting for transfers between devices: 860 us -> 164 us
  Pallas kernels: 3.48 us -> 377 us
  blocking collectives: 82.6 us -> 0 us
  matrix products: 120 us -> 100 us
  between operations: 14.8 us -> 1.81 us
    pallas_call x0 -> x10, Pallas kernels: none -> 377 us  [the longest x4 175 us: reduce(): pl.pallas_call(functools.partial(reduce_kernel, line, split), out_shape=j...]
    reduce_scatter x4 -> x0, waiting for transfers between devices: 327 us -> none  [scatter(): lax.psum_scatter(partial.astype(low), 'shard', scatter_dimension=1, tiled...]
    all_gather x6 -> x0, waiting for transfers between devices: 268 us -> none  [the longest x4 256 us: gather(): lax.all_gather(rows.reshape(seqs, seq_dev, width), 'shard', axis=1, tiled...]
    psum x1 -> x0, waiting for transfers between devices: 255 us -> none  [local_heads(): lax.psum(jnp.concatenate([outer(query_grad, normed_first), outer(key_own,...]
    ppermute x0 -> x16, waiting for transfers between devices: none -> 158 us  [the longest x5 158 us: group_total(): lax.ppermute(pair, 'grp', chips).astype(f32)]
    all_gather x2 -> x0, blocking collectives: 42.2 us -> none  [the longest x1 22.3 us: local_heads(): lax.all_gather(prenorm_gain, 'shard', axis=0, tiled=True)]
    psum x1 -> x0, blocking collectives: 40.4 us -> none  [local_heads(): lax.psum(jnp.stack([prenorm_part, midnorm_part]), ('grp', 'shard'))]
    dot_general x22, matrix products: 111 us -> 94.7 us  [the longest x7 37.1 us: times(): jnp.einsum('ta,ba->tb', rows, weight, preferred_element_type=jnp.float32)]
  transfers between devices with their start and end apart: 12 -> 17, of which waited for: 11 -> 6; matrix products, arithmetic and copies ran while one was open for 8% -> 6% of each run, Pallas kernels for 0% -> 16%
where the time goes in v2:
time: 729 us; the launch traced here: 720 us
  Pallas kernels  377 us (52%)
  waiting for transfers between devices  164 us (22%)
  matrix products  100 us (14%)
  other arithmetic  54.2 us (7%)
  local copies, waits for them, and re-layouts  14 us (2%)
  starting transfers between devices  9.04 us (1%)
    pallas_call x4, Pallas kernels, reduce(): pl.pallas_call(functools.partial(reduce_kernel, line, split), out_shape=j...  175 us
    pallas_call x4, Pallas kernels, gather(): pl.pallas_call(functools.partial(gather_kernel, count // 2, split), out_s...  167 us
    ppermute x5, waiting for transfers between devices, group_total(): lax.ppermute(pair, 'grp', chips).astype(f32)  158 us
    dot_general x7, matrix products, times(): jnp.einsum('ta,ba->tb', rows, weight, preferred_element_type=jnp.float32)  37.1 us
    dot_general x7, matrix products, into(): return jnp.dot(rows, weight, preferred_element_type=jnp.float32)  31.5 us
    dot_general x7, matrix products, outer(): jnp.einsum('tb,ta->ba', left, right, preferred_element_type=jnp.float32)  24 us
    pallas_call x1, Pallas kernels, small_gather(): pl.pallas_call(functools.partial(small_gather_kernel, count), out_shape=j...  22.8 us
    convert_element_type x5, other arithmetic, group_total(): return jnp.concatenate([jnp.where(core == 0, whole, swapped), jnp.where(c...  14.9 us
  transfers between devices with their start and end apart: 17, of which 6 were waited for; matrix products, arithmetic and copies ran while one was open for 6% of the time, Pallas kernels for 16%

profile of v2, /device:TPU:0, one launch (start us, length us, event | category | flops | bytes accessed | tf_op | source)
XLA Modules:
  0.0 719.7 jit_solution(17076737899934684500)
XLA Ops:
  8.1 22.8 %small_gather.1 = bf16[8,16,256]{2,1,0:T(8,128)(2,1)} custom-call(bf16[16,256]{1,0:T(8,128)(2,1)} %broadcast_bitcast_fusion.own_ref), custom_call_target="tpu_custom_call" | custom-call | tf_op jit(solution)/shard_map/small_gather/pallas_call | solution.py:276
  35.1 49.6 %gather2.1 = bf16[8,128,2048]{2,1,0:T(8,128)(2,1)} custom-call(bf16[128,2048]{1,0:T(8,128)(2,1)} %fusion.15.own_ref), custom_call_target="tpu_custom_call" | custom-call | tf_op jit(solution)/shard_map/gather2/pallas_call | solution.py:97
  89.5 43.7 %gather3.1 = bf16[8,128,2048]{2,1,0:T(8,128)(2,1)} custom-call(bf16[128,2048]{1,0:T(8,128)(2,1)} %bitcast_select_fusion.own_ref), custom_call_target="tpu_custom_call" | custom-call | tf_op jit(solution)/shard_map/gather3/pallas_call | solution.py:97
  151.9 50.2 %reduce4.1 = f32[128,2048]{1,0:T(8,128)} custom-call(bf16[8,128,2048]{2,1,0:T(8,128)(2,1)} %bitcast.150), custom_call_target="tpu_custom_call" | custom-call | tf_op jit(solution)/shard_map/reduce4/pallas_call | solution.py:234
  204.6 39.7 %gather5.1 = bf16[8,128,2048]{2,1,0:T(8,128)(2,1)} custom-call(bf16[128,2048]{1,0:T(8,128)(2,1)} %multiply_convert_fusion.4.own_ref), custom_call_target="tpu_custom_call" | custom-call | tf_op jit(solution)/shard_map/gather5/pallas_call | solution.py:97
  244.3 10.1 %fusion.55 = f32[1024,1024]{1,0:T(8,128)} fusion(bf16[1024,2048]{1,0:T(8,128)(2,1)} %bitcast.166, bf16[1024,2048]{1,0:T(8,128)(2,1)} %param.20), kind=kOutput, calls=%fused_computation.163 | convolution fusion | flops 4294967296 | bytes 12582912 | tf_op jit(solution)/shard_map/ta,ba->tb/dot_general | solution.py:748
  254.5 6.1 fusion.56
  260.5 11.1 %multiply_convert_fusion = (bf16[1024,1024]{1,0:T(8,128)(2,1)S(1)}, bf16[1024,1024]{1,0:T(8,128)(2,1)}, bf16[1024,1024]{1,0:T(8,128)(2,1)}) fusion(f32[1024,1024]{1,0:T(8,128)} %fusion.55, f32[1024,1024]{1,0:T(8,128)} %fusion.56, bf16[1024,2048]{1,0:T(8,128)(2,1)S(1)} %bitcast.164, bf16[1024,2048]{1,0:T(8,128)(2,1)} %param.22), kind=kOutput, calls=%fused_computation.12 | convolution fusion | flops 4310695936 | bytes 23068672 | tf_op jit(solution)/shard_map/ta,ba->tb/dot_general | solution.py:748
  271.7 6.9 fusion.57
  278.5 6.1 add_convert_fusion.1
  284.6 41.4 %reduce6.1 = f32[128,2048]{1,0:T(8,128)} custom-call(bf16[8,128,2048]{2,1,0:T(8,128)(2,1)} %bitcast.162), custom_call_target="tpu_custom_call" | custom-call | tf_op jit(solution)/shard_map/reduce6/pallas_call | solution.py:234
  327.6 9.3 %convolution_convert_fusion.4 = bf16[1024,2048]{1,0:T(8,128)(2,1)} fusion(bf16[1024,1024]{1,0:T(8,128)(2,1)} %get-tuple-element.21, bf16[1024,2048]{1,0:T(8,128)(2,1)} %param.22), kind=kOutput, calls=%fused_computation.21 | convolution fusion | flops 4297064448 | bytes 10485760 | tf_op jit(solution)/shard_map/dot_general | solution.py:751
  336.9 47.8 %reduce7.1 = f32[128,2048]{1,0:T(8,128)} custom-call(bf16[8,128,2048]{2,1,0:T(8,128)(2,1)} %bitcast.163), custom_call_target="tpu_custom_call" | custom-call | tf_op jit(solution)/shard_map/reduce7/pallas_call | solution.py:234
  388.3 33.5 %gather8.1 = bf16[8,128,2048]{2,1,0:T(8,128)(2,1)} custom-call(bf16[128,2048]{1,0:T(8,128)(2,1)} %get-tuple-element.15.own_ref), custom_call_target="tpu_custom_call" | custom-call | tf_op jit(solution)/shard_map/gather8/pallas_call | solution.py:97
  433.6 6.4 convolution_convert_fusion.3
  440.0 6.2 convolution_convert_fusion.2
  446.3 6.3 convolution_convert_fusion.1
  461.1 35.6 %reduce9.1 = f32[128,2048]{1,0:T(8,128)} custom-call(bf16[8,128,2048]{2,1,0:T(8,128)(2,1)} %bitcast.151), custom_call_target="tpu_custom_call" | custom-call | tf_op jit(solution)/shard_map/reduce9/pallas_call | solution.py:234
  498.9 12.2 %gain_sum.1 = f32[2,8,256]{2,1,0:T(8,128)} custom-call(f32[8,2,8,256]{3,2,1,0:T(8,128)} %broadcast_in_dim.38.parts_ref), custom_call_target="tpu_custom_call" | custom-call | tf_op jit(solution)/shard_map/gain_sum/pallas_call | solution.py:350
  530.6 13.0 %collective-permute-done.6 = bf16[128,2048]{1,0:T(8,128)(2,1)S(1)} collective-permute-done((bf16[128,2048]{1,0:T(8,128)(2,1)S(1)}, bf16[128,2048]{1,0:T(8,128)(2,1)S(1)}, u32[]{:S(2)}, u32[]{:S(2)}) %collective-permute-start.6) | collective-permute-done | bytes 524320 | tf_op jit(solution)/shard_map/ppermute | solution.py:380
  551.4 19.0 %collective-permute-done.3 = bf16[256,2048]{1,0:T(8,128)(2,1)S(1)} collective-permute-done((bf16[256,2048]{1,0:T(8,128)(2,1)S(1)}, bf16[256,2048]{1,0:T(8,128)(2,1)S(1)}, u32[]{:S(2)}, u32[]{:S(2)}) %collective-permute-start.3) | collective-permute-done | bytes 1048608 | tf_op jit(solution)/shard_map/ppermute | solution.py:380
  572.7 42.7 %collective-permute-done.9 = bf16[512,2048]{1,0:T(8,128)(2,1)S(1)} collective-permute-done((bf16[512,2048]{1,0:T(8,128)(2,1)S(1)}, bf16[512,2048]{1,0:T(8,128)(2,1)S(1)}, u32[]{:S(2)}, u32[]{:S(2)}) %collective-permute-start.9) | collective-permute-done | bytes 2097184 | tf_op jit(solution)/shard_map/ppermute | solution.py:380
  616.5 43.8 %collective-permute-done.12 = bf16[512,2048]{1,0:T(8,128)(2,1)S(1)} collective-permute-done((bf16[512,2048]{1,0:T(8,128)(2,1)S(1)}, bf16[512,2048]{1,0:T(8,128)(2,1)S(1)}, u32[]{:S(2)}, u32[]{:S(2)}) %collective-permute-start.12) | collective-permute-done | bytes 2097184 | tf_op jit(solution)/shard_map/ppermute | solution.py:380
  665.1 39.8 %collective-permute-done.15 = bf16[512,2048]{1,0:T(8,128)(2,1)S(1)} collective-permute-done((bf16[512,2048]{1,0:T(8,128)(2,1)S(1)}, bf16[512,2048]{1,0:T(8,128)(2,1)S(1)}, u32[]{:S(2)}, u32[]{:S(2)}) %collective-permute-start.15) | collective-permute-done | bytes 2097184 | tf_op jit(solution)/shard_map/ppermute | solution.py:380
  (208 shorter events, 114.4 us)
Async XLA Ops:
  0.6 148.0 %copy-start = (bf16[256,2048]{1,0:T(8,128)(2,1)S(1)}, bf16[256,2048]{1,0:T(8,128)(2,1)}, u32[]{:S(2)}) copy-start(bf16[256,2048]{1,0:T(8,128)(2,1)} %param.18) | copy-start | bytes 3145732
  0.7 84.1 %copy-start.32 = (bf16[256,2048]{1,0:T(8,128)(2,1)S(1)}, bf16[256,2048]{1,0:T(8,128)(2,1)}, u32[]{:S(2)}) copy-start(bf16[256,2048]{1,0:T(8,128)(2,1)} %param.15) | copy-start | bytes 3145732
  3.1 132.1 %collective-permute-start = (bf16[256,2048]{1,0:T(8,128)(2,1)}, bf16[256,2048]{1,0:T(8,128)(2,1)}, u32[]{:S(2)}, u32[]{:S(2)}) collective-permute-start(bf16[256,2048]{1,0:T(8,128)(2,1)} %pad_maximum_fusion), channel_id=1, source_target_pairs={{0,1},{1,0},{2,3},{3,2},{4,5},{5,4},{6,7},{7,6},{8,9},{9,8},{10,11... | collective-permute-start | bytes 3145736 | tf_op jit(solution)/shard_map/ppermute | solution.py:773
  151.9 50.2 %copy-start.7 = (bf16[2,64,2048]{2,1,0:T(8,128)(2,1)S(1)}, bf16[2,64,2048]{2,1,0:T(8,128)(2,1)}, u32[]{:S(2)}) copy-start(bf16[2,64,2048]{2,1,0:T(8,128)(2,1)} %param.12) | copy-start | bytes 1572868
  244.3 10.2 %copy-start.12 = (bf16[8,128,2048]{2,1,0:T(8,128)(2,1)S(1)}, bf16[8,128,2048]{2,1,0:T(8,128)(2,1)}, u32[]{:S(2)}) copy-start(bf16[8,128,2048]{2,1,0:T(8,128)(2,1)} %gather5.1) | copy-start | bytes 12582916
  260.5 11.1 %copy-start.37 = (bf16[1024,2048]{1,0:T(8,128)(2,1)S(1)}, bf16[1024,2048]{1,0:T(8,128)(2,1)}, u32[]{:S(2)}) copy-start(bf16[1024,2048]{1,0:T(8,128)(2,1)} %param.20) | copy-start | bytes 12582916
  461.1 52.5 %copy-start.15 = (bf16[256,2048]{1,0:T(8,128)(2,1)S(1)}, bf16[256,2048]{1,0:T(8,128)(2,1)}, u32[]{:S(2)}) copy-start(bf16[256,2048]{1,0:T(8,128)(2,1)} %convolution_convert_fusion.5) | copy-start | bytes 3145732
  512.1 14.0 %collective-permute-start.1 = (bf16[1024,256]{1,0:T(8,128)(2,1)S(1)}, bf16[1024,256]{1,0:T(8,128)(2,1)S(1)}, u32[]{:S(2)}, u32[]{:S(2)}) collective-permute-start(bf16[1024,256]{1,0:T(8,128)(2,1)S(1)} %pad_maximum_fusion.10), channel_id=1, source_target_pairs={{0,1},{1,0},{2,3},{3,2},{4,5},{5,4},{6,7},{7,6},{8,9},{9,8},{10,11... | collective-permute-start | bytes 1572872 | tf_op jit(solution)/shard_map/ppermute | solution.py:867
  513.6 15.4 %collective-permute-start.5 = (bf16[128,2048]{1,0:T(8,128)(2,1)S(1)}, bf16[128,2048]{1,0:T(8,128)(2,1)S(1)}, u32[]{:S(2)}, u32[]{:S(2)}) collective-permute-start(bf16[128,2048]{1,0:T(8,128)(2,1)S(1)} %broadcast_select_fusion.14), channel_id=1, source_target_pairs={{0,8},{8,0},{16,24},{24,16},{1,9},{9,1},{17,25},{25,17},{2,10},{10... | collective-permute-start | bytes 1572872 | tf_op jit(solution)/shard_map/ppermute | solution.py:378
  516.1 28.6 %collective-permute-start.8 = (bf16[512,2048]{1,0:T(8,128)(2,1)S(1)}, bf16[512,2048]{1,0:T(8,128)(2,1)S(1)}, u32[]{:S(2)}, u32[]{:S(2)}) collective-permute-start(bf16[512,2048]{1,0:T(8,128)(2,1)S(1)} %broadcast_select_fusion.8), channel_id=1, source_target_pairs={{0,8},{8,0},{16,24},{24,16},{1,9},{9,1},{17,25},{25,17},{2,10},{10... | collective-permute-start | bytes 6291464 | tf_op jit(solution)/shard_map/ppermute | solution.py:378
  516.9 32.7 %collective-permute-start.11 = (bf16[512,2048]{1,0:T(8,128)(2,1)S(1)}, bf16[512,2048]{1,0:T(8,128)(2,1)S(1)}, u32[]{:S(2)}, u32[]{:S(2)}) collective-permute-start(bf16[512,2048]{1,0:T(8,128)(2,1)S(1)} %broadcast_select_fusion.5), channel_id=1, source_target_pairs={{0,8},{8,0},{16,24},{24,16},{1,9},{9,1},{17,25},{25,17},{2,10},{10... | collective-permute-start | bytes 6291464 | tf_op jit(solution)/shard_map/ppermute | solution.py:378
  518.5 52.4 %collective-permute-start.14 = (bf16[512,2048]{1,0:T(8,128)(2,1)S(1)}, bf16[512,2048]{1,0:T(8,128)(2,1)S(1)}, u32[]{:S(2)}, u32[]{:S(2)}) collective-permute-start(bf16[512,2048]{1,0:T(8,128)(2,1)S(1)} %broadcast_select_fusion.2), channel_id=1, source_target_pairs={{0,8},{8,0},{16,24},{24,16},{1,9},{9,1},{17,25},{25,17},{2,10},{10... | collective-permute-start | bytes 6291464 | tf_op jit(solution)/shard_map/ppermute | solution.py:378
  528.9 14.9 %collective-permute-start.2 = (bf16[256,2048]{1,0:T(8,128)(2,1)S(1)}, bf16[256,2048]{1,0:T(8,128)(2,1)S(1)}, u32[]{:S(2)}, u32[]{:S(2)}) collective-permute-start(bf16[256,2048]{1,0:T(8,128)(2,1)S(1)} %get-tuple-element.69), channel_id=1, source_target_pairs={{0,8},{8,0},{16,24},{24,16},{1,9},{9,1},{17,25},{25,17},{2,10},{10... | collective-permute-start | bytes 3145736 | tf_op jit(solution)/shard_map/ppermute | solution.py:378
  529.3 14.4 %collective-permute-start.6 = (bf16[128,2048]{1,0:T(8,128)(2,1)S(1)}, bf16[128,2048]{1,0:T(8,128)(2,1)S(1)}, u32[]{:S(2)}, u32[]{:S(2)}) collective-permute-start(bf16[128,2048]{1,0:T(8,128)(2,1)S(1)} %add_convert_fusion.11), channel_id=1, source_target_pairs={{0,16},{16,0},{8,24},{24,8},{1,17},{17,1},{9,25},{25,9},{2,18},{18... | collective-permute-start | bytes 1572872 | tf_op jit(solution)/shard_map/ppermute | solution.py:380
  529.4 15.4 %copy-start.6 = (bf16[1024,2048]{1,0:T(8,128)(2,1)S(1)}, bf16[1024,2048]{1,0:T(8,128)(2,1)}, u32[]{:S(2)}) copy-start(bf16[1024,2048]{1,0:T(8,128)(2,1)} %convolution_convert_fusion.3) | copy-start | bytes 12582916
  543.8 4.2 collective-permute-start.7
  544.4 26.0 %collective-permute-start.3 = (bf16[256,2048]{1,0:T(8,128)(2,1)S(1)}, bf16[256,2048]{1,0:T(8,128)(2,1)S(1)}, u32[]{:S(2)}, u32[]{:S(2)}) collective-permute-start(bf16[256,2048]{1,0:T(8,128)(2,1)S(1)} %add_convert_fusion.9), channel_id=1, source_target_pairs={{0,16},{16,0},{8,24},{24,8},{1,17},{17,1},{9,25},{25,9},{2,18},{18... | collective-permute-start | bytes 3145736 | tf_op jit(solution)/shard_map/ppermute | solution.py:380
  546.2 69.2 %collective-permute-start.9 = (bf16[512,2048]{1,0:T(8,128)(2,1)S(1)}, bf16[512,2048]{1,0:T(8,128)(2,1)S(1)}, u32[]{:S(2)}, u32[]{:S(2)}) collective-permute-start(bf16[512,2048]{1,0:T(8,128)(2,1)S(1)} %add_convert_fusion.7), channel_id=1, source_target_pairs={{0,16},{16,0},{8,24},{24,8},{1,17},{17,1},{9,25},{25,9},{2,18},{18... | collective-permute-start | bytes 6291464 | tf_op jit(solution)/shard_map/ppermute | solution.py:380
  551.0 109.3 %collective-permute-start.12 = (bf16[512,2048]{1,0:T(8,128)(2,1)S(1)}, bf16[512,2048]{1,0:T(8,128)(2,1)S(1)}, u32[]{:S(2)}, u32[]{:S(2)}) collective-permute-start(bf16[512,2048]{1,0:T(8,128)(2,1)S(1)} %add_convert_fusion.5), channel_id=1, source_target_pairs={{0,16},{16,0},{8,24},{24,8},{1,17},{17,1},{9,25},{25,9},{2,18},{18... | collective-permute-start | bytes 6291464 | tf_op jit(solution)/shard_map/ppermute | solution.py:380
  570.8 45.5 %collective-permute-start.4 = (bf16[256,2048]{1,0:T(8,128)(2,1)S(1)}, bf16[256,2048]{1,0:T(8,128)(2,1)S(1)}, u32[]{:S(2)}, u32[]{:S(2)}) collective-permute-start(bf16[256,2048]{1,0:T(8,128)(2,1)S(1)} %add_convert_fusion.8), channel_id=1, source_target_pairs={{0,8},{8,0},{16,24},{24,16},{1,9},{9,1},{17,25},{25,17},{2,10},{10... | collective-permute-start | bytes 3145736 | tf_op jit(solution)/shard_map/ppermute | solution.py:381
  572.3 132.5 %collective-permute-start.15 = (bf16[512,2048]{1,0:T(8,128)(2,1)S(1)}, bf16[512,2048]{1,0:T(8,128)(2,1)S(1)}, u32[]{:S(2)}, u32[]{:S(2)}) collective-permute-start(bf16[512,2048]{1,0:T(8,128)(2,1)S(1)} %add_convert_fusion.3), channel_id=1, source_target_pairs={{0,16},{16,0},{8,24},{24,8},{1,17},{17,1},{9,25},{25,9},{2,18},{18... | collective-permute-start | bytes 6291464 | tf_op jit(solution)/shard_map/ppermute | solution.py:380
  616.3 89.6 %collective-permute-start.10 = (bf16[512,2048]{1,0:T(8,128)(2,1)S(1)}, bf16[512,2048]{1,0:T(8,128)(2,1)S(1)}, u32[]{:S(2)}, u32[]{:S(2)}) collective-permute-start(bf16[512,2048]{1,0:T(8,128)(2,1)S(1)} %add_convert_fusion.6), channel_id=1, source_target_pairs={{0,8},{8,0},{16,24},{24,16},{1,9},{9,1},{17,25},{25,17},{2,10},{10... | collective-permute-start | bytes 6291464 | tf_op jit(solution)/shard_map/ppermute | solution.py:381
  661.4 49.0 %collective-permute-start.13 = (bf16[512,2048]{1,0:T(8,128)(2,1)S(1)}, bf16[512,2048]{1,0:T(8,128)(2,1)S(1)}, u32[]{:S(2)}, u32[]{:S(2)}) collective-permute-start(bf16[512,2048]{1,0:T(8,128)(2,1)S(1)} %add_convert_fusion.4), channel_id=1, source_target_pairs={{0,8},{8,0},{16,24},{24,16},{1,9},{9,1},{17,25},{25,17},{2,10},{10... | collective-permute-start | bytes 6291464 | tf_op jit(solution)/shard_map/ppermute | solution.py:381
  705.8 9.2 %collective-permute-start.16 = (bf16[512,2048]{1,0:T(8,128)(2,1)S(1)}, bf16[512,2048]{1,0:T(8,128)(2,1)S(1)}, u32[]{:S(2)}, u32[]{:S(2)}) collective-permute-start(bf16[512,2048]{1,0:T(8,128)(2,1)S(1)} %add_convert_fusion.2), channel_id=1, source_target_pairs={{0,8},{8,0},{16,24},{24,16},{1,9},{9,1},{17,25},{25,17},{2,10},{10... | collective-permute-start | bytes 6291464 | tf_op jit(solution)/shard_map/ppermute | solution.py:381
  (36 other events, 124.4 us)

commit v3 on v0

--- a/solution.py
+++ b/solution.py
@@ -1,13 +1,945 @@
+import functools
 import math
 
 import jax
 import jax.numpy as jnp
 from jax import lax
+from jax.experimental import pallas as pl
+from jax.experimental.pallas import tpu as pltpu
 from jax.sharding import PartitionSpec as P
+
+MESH = pl.DeviceIdType.MESH
+DEPTH = 2
 
 NH = 8
 KVH = 4
 HD = 256
+
+
+F32 = jnp.float32
+VMEM_LIMIT = 66_000_000
+
+
+def either(condition, action):
+    pl.when(condition)(action)
+
+
+def total_into(dst, *srcs):
+    step = 16
+
+    @pl.loop(0, dst.shape[0] // step)
+    def _(i):
+        at = pl.ds(pl.multiple_of(i * step, step), step)
+        value = srcs[0][at].astype(F32)
+        for src in srcs[1:]:
+            value = value + src[at].astype(F32)
+        dst[at] = value.astype(dst.dtype)
+
+
+class Place:
+    def __init__(self, line):
+        self.line = line
+        self.me = lax.axis_index("shard")
+        self.z = self.me // 2
+        self.y = lax.rem(self.me, 2)
+        self.cross = self.me + 1 - 2 * self.y
+        self.low_end = self.z == 0
+        self.high_end = self.z == line - 1
+        near = []
+        for z in range(line):
+            order = [z]
+            for k in range(1, line):
+                order += [d for d in (z - k, z + k) if 0 <= d < line]
+            near.append(order)
+        self.tables = near
+
+    def near(self, i):
+        out = jnp.int32(0)
+        for z in range(self.line):
+            row = jnp.int32(self.tables[z][0])
+            for k in range(1, self.line):
+                row = jnp.where(i == k, self.tables[z][k], row)
+            out = jnp.where(self.z == z, row, out)
+        return out
+
+    def far(self, i):
+        return self.near(self.line - 1 - i)
+
+    def greet(self, groups=()):
+        barrier = pltpu.get_barrier_semaphore()
+
+        def signal(**peer):
+            pl.semaphore_signal(barrier, inc=1, device_id=peer, device_id_type=MESH)
+
+        signal(shard=self.cross)
+        either(self.z > 0, lambda: signal(shard=self.me - 2))
+        either(self.z < self.line - 1, lambda: signal(shard=self.me + 2))
+        for group in groups:
+            signal(grp=group)
+        ends = jnp.where(self.z > 0, 1, 0) + jnp.where(self.z < self.line - 1, 1, 0)
+        pl.semaphore_wait(barrier, 1 + ends + len(groups))
+
+
+class Gather:
+    UP, DOWN, CROSS = 0, 1, 2
+
+    def __init__(self, place, split, own, out, local_sem, send_sem, recv_sem):
+        self.p, self.own, self.out = place, own, out
+        self.local_sem, self.send_sem, self.recv_sem = local_sem, send_sem, recv_sem
+        self.parts = (pl.ds(0, split), pl.ds(split, own.shape[0] - split))
+
+    def copy(self, way, origin, part, own=False):
+        p = self.p
+        peer = (p.me + 2, p.me - 2, p.cross)[way]
+        at = self.parts[part]
+        return pltpu.make_async_remote_copy(
+            src_ref=self.own.at[at] if own else self.out.at[origin, at],
+            dst_ref=self.out.at[origin, at],
+            send_sem=self.send_sem.at[way, origin, part],
+            recv_sem=self.recv_sem.at[origin, part],
+            device_id={"shard": peer},
+            device_id_type=MESH,
+        )
+
+    def arrived(self, origin, part):
+        self.copy(self.CROSS, origin, part).wait_recv()
+
+    def start(self):
+        p = self.p
+        self.keep = pltpu.make_async_copy(self.own, self.out.at[p.me], self.local_sem)
+        self.keep.start()
+        self.copy(self.CROSS, p.me, 1, True).start()
+        self.copy(self.CROSS, p.me, 0, True).start()
+        for part in (0, 1):
+            either(p.z < p.line - 1, self.copy(self.UP, p.me, part, True).start)
+            either(p.z > 0, self.copy(self.DOWN, p.me, part, True).start)
+        self.arrived(p.cross, 1)
+        either(p.z < p.line - 1, self.copy(self.UP, p.cross, 1).start)
+        either(p.z > 0, self.copy(self.DOWN, p.cross, 1).start)
+        self.keep.wait()
+
+    def hop(self, k):
+        p = self.p
+
+        def take(origin, other, way, more):
+            self.arrived(origin, 0)
+            self.copy(self.CROSS, origin, 0).start()
+            either(more, self.copy(way, origin, 0).start)
+            for block in (origin, other):
+                self.arrived(block, 1)
+                either(more, self.copy(way, block, 1).start)
+
+        below, above = p.me - 2 * k, p.me + 2 * k
+        either(p.z - k >= 0, lambda: take(below, p.cross - 2 * k, self.UP, p.z < p.line - 1))
+        either(p.z + k < p.line, lambda: take(above, p.cross + 2 * k, self.DOWN, p.z > 0))
+
+    def whole(self, position):
+        self.arrived(2 * position + 1 - self.p.y, 0)
+
+    def drain(self):
+        p = self.p
+
+        @pl.loop(0, p.line)
+        def _(d):
+            mine, other = 2 * d + p.y, 2 * d + 1 - p.y
+            self.copy(self.CROSS, mine, 0).wait_send()
+
+            @pl.when(d == p.z)
+            def _():
+                self.copy(self.CROSS, mine, 1).wait_send()
+
+            @pl.when((d <= p.z) & (p.z < p.line - 1))
+            def _():
+                for block, part in ((mine, 0), (mine, 1), (other, 1)):
+                    self.copy(self.UP, block, part).wait_send()
+
+            @pl.when((d >= p.z) & (p.z > 0))
+            def _():
+                for block, part in ((mine, 0), (mine, 1), (other, 1)):
+                    self.copy(self.DOWN, block, part).wait_send()
+
+
+class Reduce:
+    UP, DOWN, CROSS, BUP, BDN, BX = 0, 1, 2, 3, 5, 7
+
+    @staticmethod
+    def scratch(line, rows, split, width, dtype):
+        v = pltpu.VMEM
+        rest = rows - split
+        dma = pltpu.SemaphoreType.DMA
+        return (
+            [v((line, split, width), dtype)] * 5
+            + [v((line, 2, rest, width), dtype)] * 4
+            + [v((rest, width), dtype)] * 2
+            + [dma((8, line)), dma((8, line))]
+        )
+
+    def __init__(self, place, split, parts, out, scratch):
+        self.p, self.parts, self.out = place, parts, out
+        (self.cross_in, self.up_in, self.down_in, self.up_out, self.down_out) = scratch[:5]
+        (self.bup_in, self.bdn_in, self.bup_out, self.bdn_out) = scratch[5:9]
+        self.bx_out, self.bx_in, self.send_sem, self.recv_sem = scratch[9:]
+        self.a = pl.ds(0, split)
+        self.b = pl.ds(split, parts.shape[1] - split)
+
+    def desc(self, way, slot, src, dst, peer):
+        return pltpu.make_async_remote_copy(
+            src_ref=src,
+            dst_ref=dst,
+            send_sem=self.send_sem.at[way, slot],
+            recv_sem=self.recv_sem.at[way, slot],
+            device_id={"shard": peer},
+            device_id_type=MESH,
+        )
+
+    def cross_copy(self, d):
+        p = self.p
+        return self.desc(
+            self.CROSS, d, self.parts.at[2 * d + 1 - p.y, self.a], self.cross_in.at[d], p.cross
+        )
+
+    def line_copy(self, up, d):
+        p = self.p
+        if up:
+            return self.desc(self.UP, d, self.up_out.at[d], self.up_in.at[d], p.me + 2)
+        return self.desc(self.DOWN, d, self.down_out.at[d], self.down_in.at[d], p.me - 2)
+
+    def b_copy(self, up, d, o, src=None):
+        p = self.p
+        out, into = (self.bup_out, self.bup_in) if up else (self.bdn_out, self.bdn_in)
+        return self.desc(
+            (self.BUP if up else self.BDN) + o,
+            d,
+            out.at[d, o] if src is None else src,
+            into.at[d, o],
+            p.me + 2 if up else p.me - 2,
+        )
+
+    def bx_copy(self):
+        return self.desc(self.BX, 0, self.bx_out, self.bx_in, self.p.cross)
+
+    def column(self, o):
+        return self.p.y if o == 0 else 1 - self.p.y
+
+    def send_across(self, i):
+        self.cross_copy(self.p.far(i)).start()
+
+    def b_hop(self, i):
+        p = self.p
+        d = p.far(i)
+
+        def go(up):
+            first = p.low_end if up else p.high_end
+            out, into = (self.bup_out, self.bup_in) if up else (self.bdn_out, self.bdn_in)
+            for o in (1, 0):
+                mine = self.parts.at[2 * d + self.column(o), self.b]
+                either(first, self.b_copy(up, d, o, mine).start)
+
+                @pl.when(jnp.logical_not(first))
+                def _():
+                    self.b_copy(up, d, o).wait_recv()
+                    total_into(out.at[d, o], mine, into.at[d, o])
+                    self.b_copy(up, d, o).start()
+
+        either(d > p.z, lambda: go(True))
+        either(d < p.z, lambda: go(False))
+
+    def hop(self, i):
+        p = self.p
+        d = p.far(i)
+        self.cross_copy(d).wait_recv()
+        mine = self.parts.at[2 * d + p.y, self.a]
+
+        def go(up):
+            first = p.low_end if up else p.high_end
+            out, into = (self.up_out, self.up_in) if up else (self.down_out, self.down_in)
+            either(first, lambda: total_into(out.at[d], mine, self.cross_in.at[d]))
+
+            @pl.when(jnp.logical_not(first))
+            def _():
+                self.line_copy(up, d).wait_recv()
+                total_into(out.at[d], mine, self.cross_in.at[d], into.at[d])
+
+            self.line_copy(up, d).start()
+
+        either(d > p.z, lambda: go(True))
+        either(d < p.z, lambda: go(False))
+
+    def close(self, dst, mine, ups, downs):
+        p = self.p
+        either(p.low_end, lambda: total_into(dst, *mine, downs))
+        either(p.high_end, lambda: total_into(dst, *mine, ups))
+        either(
+            jnp.logical_not(p.low_end | p.high_end), lambda: total_into(dst, *mine, ups, downs)
+        )
+
+    def finish(self):
+        p = self.p
+        for o in (1, 0):
+            either(jnp.logical_not(p.low_end), self.b_copy(True, p.z, o).wait_recv)
+            either(jnp.logical_not(p.high_end), self.b_copy(False, p.z, o).wait_recv)
+            if o:
+                mine = self.parts.at[2 * p.z + self.column(o), self.b]
+                self.close(self.bx_out, (mine,), self.bup_in.at[p.z, o], self.bdn_in.at[p.z, o])
+                self.bx_copy().start()
+        self.bx_copy().wait_recv()
+        self.close(
+            self.out.at[self.b],
+            (self.parts.at[p.me, self.b], self.bx_in),
+            self.bup_in.at[p.z, 0],
+            self.bdn_in.at[p.z, 0],
+        )
+        self.cross_copy(p.z).wait_recv()
+        either(jnp.logical_not(p.low_end), self.line_copy(True, p.z).wait_recv)
+        either(jnp.logical_not(p.high_end), self.line_copy(False, p.z).wait_recv)
+        self.close(
+            self.out.at[self.a],
+            (self.parts.at[p.me, self.a], self.cross_in.at[p.z]),
+            self.up_in.at[p.z],
+            self.down_in.at[p.z],
+        )
+
+    def drain(self):
+        p = self.p
+        self.bx_copy().wait_send()
+
+        @pl.loop(0, p.line)
+        def _(d):
+            self.cross_copy(d).wait_send()
+
+            @pl.when(d > p.z)
+            def _():
+                self.line_copy(True, d).wait_send()
+                self.b_copy(True, d, 0).wait_send()
+                self.b_copy(True, d, 1).wait_send()
+
+            @pl.when(d < p.z)
+            def _():
+                self.line_copy(False, d).wait_send()
+                self.b_copy(False, d, 0).wait_send()
+                self.b_copy(False, d, 1).wait_send()
+
+
+def dot_t(a, b):
+    return lax.dot_general(a, b, (((1,), (1,)), ((), ())), preferred_element_type=F32)
+
+
+def t_dot(a, b):
+    return lax.dot_general(a, b, (((0,), (0,)), ((), ())), preferred_element_type=F32)
+
+
+def ffn_kernel(
+    line, split,
+    own, cot_hbm, gate_hbm, up_hbm, down_hbm,
+    second, ffn_hbm, mine_hbm, theirs_hbm,
+    normed, cot, gate_w, up_w, down_w, hidden, gate_g, up_g, parts, stage,
+    g_local, g_send, g_recv, load_sem, ffn_sem, stage_send, stage_recv, stage_local, *r_scratch,
+):
+    p = Place(line)
+    rank = lax.axis_index("grp")
+    core = lax.rem(rank, 2)
+    partner = rank + 1 - 2 * core
+    loads = [
+        pltpu.make_async_copy(src, dst, load_sem.at[i])
+        for i, (src, dst) in enumerate(
+            ((gate_hbm, gate_w), (up_hbm, up_w), (cot_hbm, cot), (down_hbm, down_w))
+        )
+    ]
+    for load in loads:
+        load.start()
+    p.greet((partner,))
+    gather = Gather(p, split, own, normed, g_local, g_send, g_recv)
+    gather.start()
+    for load in loads:
+        load.wait()
+    rows = own.shape[0]
+    pair = 2 * rows
+    low = own.dtype
+
+    @pl.loop(0, line)
+    def _(i):
+        gather.hop(i + 1)
+        d = p.near(i)
+        gather.whole(d)
+        x = normed[pl.ds(2 * d, 2)].reshape(pair, -1)
+        g = dot_t(x, gate_w[...])
+        u = dot_t(x, up_w[...])
+        dh = dot_t(cot[pl.ds(2 * d, 2)].reshape(pair, -1), down_w[...])
+        s = 1.0 / (1.0 + jnp.exp(-g))
+        silu = g * s
+        at = pl.ds(pl.multiple_of(d * pair, pair), pair)
+        hidden[at] = (silu * u).astype(low)
+        up_g[at] = (dh * silu).astype(low)
+        gate_g[at] = (dh * u * s * (1.0 + g * (1.0 - s))).astype(low)
+        part = jnp.dot(gate_g[at], gate_w[...], preferred_element_type=F32)
+        part = part + jnp.dot(up_g[at], up_w[...], preferred_element_type=F32)
+        parts[pl.ds(2 * d, 2)] = part.astype(low).reshape(2, rows, -1)
+
+    reduce = Reduce(p, split, parts, second, r_scratch)
+    for i in range(DEPTH):
+        reduce.send_across(i)
+    for i in range(line - 1):
+        reduce.b_hop(i)
+
+    units = hidden.shape[1]
+    quarter = units // 4
+    half = units // 2
+
+    def put(n, slot):
+        which, q = n // 4, lax.rem(n, 4)
+        keep = (q // 2) == core
+        at = pl.ds(pl.multiple_of(lax.rem(q, 2) * quarter, quarter), quarter)
+        local = pltpu.make_async_copy(stage.at[slot], mine_hbm.at[which, at], stage_local.at[slot])
+        remote = pltpu.make_async_remote_copy(
+            src_ref=stage.at[slot],
+            dst_ref=theirs_hbm.at[which, at],
+            send_sem=stage_send.at[slot],
+            recv_sem=stage_recv.at[which, lax.rem(q, 2)],
+            device_id={"grp": partner},
+            device_id_type=MESH,
+        )
+        return keep, local, remote
+
+    def release(n, slot):
+        keep, local, remote = put(n, slot)
+        either(keep, local.wait)
+        either(jnp.logical_not(keep), remote.wait_send)
+
+    def gradient(which, left, right):
+        @pl.loop(0, 4)
+        def _(q):
+            n = which * 4 + q
+            slot = lax.rem(n, 2)
+            either(n >= 2, lambda: release(n - 2, slot))
+            cols = pl.ds(pl.multiple_of(q * quarter, quarter), quarter)
+            stage[slot] = t_dot(left[:, cols], right[...].reshape(left.shape[0], -1)).astype(low)
+            keep, local, remote = put(n, slot)
+            either(keep, local.start)
+            either(jnp.logical_not(keep), remote.start)
+
+    sources = ((hidden, cot), (gate_g, normed), (up_g, normed))
+    for i in range(line - 1):
+        gradient(i, *sources[i])
+        reduce.hop(i)
+        if i + DEPTH < line:
+            reduce.send_across(i + DEPTH)
+    release(10, 0)
+    release(11, 1)
+    reduce.finish()
+    reduce.drain()
+    gather.drain()
+
+    @pl.loop(0, line)
+    def _(d):
+        at = pl.ds(pl.multiple_of(d * pair, pair), pair)
+        part = jnp.dot(hidden[at], down_w[...], preferred_element_type=F32)
+        parts[pl.ds(2 * d, 2)] = part.astype(low).reshape(2, rows, -1)
+
+    ffn = pltpu.make_async_copy(parts, ffn_hbm, ffn_sem)
+    ffn.start()
+    for which in range(3):
+        for q in range(2):
+            pltpu.make_async_remote_copy(
+                src_ref=stage.at[0],
+                dst_ref=theirs_hbm.at[which, pl.ds(q * quarter, quarter)],
+                send_sem=stage_send.at[0],
+                recv_sem=stage_recv.at[which, q],
+                device_id={"grp": partner},
+                device_id_type=MESH,
+            ).wait_recv()
+    ffn.wait()
+
+
+def ffn(own, cot, gate_w, up_w, down_w, ident, split=112):
+    rows, width = own.shape
+    count = cot.shape[0]
+    units = gate_w.shape[0]
+    low = own.dtype
+    hbm = pl.BlockSpec(memory_space=pl.ANY)
+    vm = pl.BlockSpec(memory_space=pltpu.VMEM)
+    v = pltpu.VMEM
+    dma = pltpu.SemaphoreType.DMA
+    tokens = count * rows
+    shape = jax.ShapeDtypeStruct
+    return pl.pallas_call(
+        functools.partial(ffn_kernel, count // 2, split),
+        out_shape=(
+            shape((rows, width), F32),
+            shape((count, rows, width), low),
+            shape((3, units // 2, width), low),
+            shape((3, units // 2, width), low),
+        ),
+        in_specs=[vm] + [hbm] * 4,
+        out_specs=(vm, hbm, hbm, hbm),
+        scratch_shapes=[
+            v((count, rows, width), low),
+            v((count, rows, width), low),
+            v((units, width), low),
+            v((units, width), low),
+            v((units, width), low),
+            v((tokens, units), low),
+            v((tokens, units), low),
+            v((tokens, units), low),
+            v((count, rows, width), low),
+            v((2, units // 4, width), low),
+            dma, dma((3, count, 2)), dma((count, 2)), dma((4,)), dma, dma((2,)), dma((3, 2)), dma((2,)),
+        ] + Reduce.scratch(count // 2, rows, split, width, low),
+        compiler_params=pltpu.CompilerParams(collective_id=ident, has_side_effects=True, vmem_limit_bytes=VMEM_LIMIT),
+        name="ffn",
+    )(own, cot, gate_w, up_w, down_w)
+
+
+def gather_kernel(line, split, own, out, local_sem, send_sem, recv_sem):
+    p = Place(line)
+    p.greet()
+    g = Gather(p, split, own, out, local_sem, send_sem, recv_sem)
+    g.start()
+    for k in range(1, line):
+        g.hop(k)
+    for d in range(line):
+        g.whole(d)
+    g.drain()
+
+
+def gather(own, count, ident, split=112):
+    rows, width = own.shape
+    hbm = pl.BlockSpec(memory_space=pl.ANY)
+    dma = pltpu.SemaphoreType.DMA
+    return pl.pallas_call(
+        functools.partial(gather_kernel, count // 2, split),
+        out_shape=jax.ShapeDtypeStruct((count, rows, width), own.dtype),
+        in_specs=[hbm],
+        out_specs=hbm,
+        scratch_shapes=[dma, dma((3, count, 2)), dma((count, 2))],
+        compiler_params=pltpu.CompilerParams(collective_id=ident, has_side_effects=True),
+        name="gather",
+    )(own)
+
+
+def reduce_kernel(line, split, parts, out, *scratch):
+    p = Place(line)
+    p.greet()
+    r = Reduce(p, split, parts, out, scratch)
+    for i in range(DEPTH):
+        r.send_across(i)
+    for i in range(line - 1):
+        r.b_hop(i)
+    for i in range(line - 1):
+        r.hop(i)
+        if i + DEPTH < line:
+            r.send_across(i + DEPTH)
+    r.finish()
+    r.drain()
+
+
+def reduce(parts, ident, split=112):
+    count, rows, width = parts.shape
+    vm = pl.BlockSpec(memory_space=pltpu.VMEM)
+    return pl.pallas_call(
+        functools.partial(reduce_kernel, count // 2, split),
+        out_shape=jax.ShapeDtypeStruct((rows, width), F32),
+        in_specs=[vm],
+        out_specs=vm,
+        scratch_shapes=Reduce.scratch(count // 2, rows, split, width, parts.dtype),
+        compiler_params=pltpu.CompilerParams(collective_id=ident, has_side_effects=True),
+        name="reduce",
+    )(parts)
+
+
+def everyone(axis, count, me, barrier):
+    for step in range(1, count):
+        pl.semaphore_signal(
+            barrier, inc=1, device_id={axis: lax.rem(me + step, count)}, device_id_type=MESH
+        )
+    pl.semaphore_wait(barrier, count - 1)
+
+
+def first_gather_kernel(
+    line, split, own, small, out, small_out, local_sem, send_sem, recv_sem, ssem, rsem
+):
+    count = 2 * line
+    p = Place(line)
+    me = p.me
+
+    def copy(step, peer, origin):
+        return pltpu.make_async_remote_copy(
+            src_ref=small,
+            dst_ref=small_out.at[origin],
+            send_sem=ssem.at[step],
+            recv_sem=rsem.at[step],
+            device_id={"shard": peer},
+            device_id_type=MESH,
+        )
+
+    everyone("shard", count, me, pltpu.get_barrier_semaphore())
+    for step in range(1, count):
+        copy(step, lax.rem(me + step, count), me).start()
+    g = Gather(p, split, own, out, local_sem, send_sem, recv_sem)
+    g.start()
+    small_out[me] = small[...]
+    for k in range(1, line):
+        g.hop(k)
+    for d in range(line):
+        g.whole(d)
+    g.drain()
+    for step in range(1, count):
+        c = copy(step, me, lax.rem(me + count - step, count))
+        c.wait_send()
+        c.wait_recv()
+
+
+def first_gather(own, small, count, ident, split=112):
+    rows, width = own.shape
+    any_spec = pl.BlockSpec(memory_space=pl.ANY)
+    vmem_spec = pl.BlockSpec(memory_space=pltpu.VMEM)
+    dma = pltpu.SemaphoreType.DMA
+    return pl.pallas_call(
+        functools.partial(first_gather_kernel, count // 2, split),
+        out_shape=(
+            jax.ShapeDtypeStruct((count, rows, width), own.dtype),
+            jax.ShapeDtypeStruct((count,) + small.shape, small.dtype),
+        ),
+        in_specs=[any_spec, vmem_spec],
+        out_specs=(any_spec, vmem_spec),
+        scratch_shapes=[dma, dma((3, count, 2)), dma((count, 2)), dma((count,)), dma((count,))],
+        compiler_params=pltpu.CompilerParams(collective_id=ident, has_side_effects=True),
+        name="first_gather",
+    )(own, small)
+
+
+def gain_sum_kernel(count, groups, parts_ref, out_ref, first, held, second, send_sem, recv_sem, send2, recv2):
+    me = lax.axis_index("shard")
+    group = lax.axis_index("grp")
+    barrier = pltpu.get_barrier_semaphore()
+    for step in range(1, count):
+        pl.semaphore_signal(
+            barrier, inc=1, device_id={"shard": lax.rem(me + step, count)}, device_id_type=MESH
+        )
+    for step in range(1, groups):
+        pl.semaphore_signal(
+            barrier, inc=1, device_id={"grp": lax.rem(group + step, groups)}, device_id_type=MESH
+        )
+    pl.semaphore_wait(barrier, count + groups - 2)
+
+    def copy(step, peer, origin):
+        return pltpu.make_async_remote_copy(
+            src_ref=parts_ref.at[peer],
+            dst_ref=first.at[origin],
+            send_sem=send_sem.at[step],
+            recv_sem=recv_sem.at[step],
+            device_id={"shard": peer},
+            device_id_type=MESH,
+        )
+
+    def copy2(step, peer, origin):
+        return pltpu.make_async_remote_copy(
+            src_ref=held,
+            dst_ref=second.at[origin],
+            send_sem=send2.at[step],
+            recv_sem=recv2.at[step],
+            device_id={"grp": peer},
+            device_id_type=MESH,
+        )
+
+    for step in range(1, count):
+        copy(step, lax.rem(me + step, count), me).start()
+    first[me] = parts_ref[me]
+    for step in range(1, count):
+        copy(step, me, lax.rem(me + count - step, count)).wait_recv()
+    total = first[0]
+    for peer in range(1, count):
+        total = total + first[peer]
+    held[...] = total
+    second[group] = total
+    for step in range(1, groups):
+        copy2(step, lax.rem(group + step, groups), group).start()
+    for step in range(1, groups):
+        copy2(step, group, lax.rem(group + groups - step, groups)).wait_recv()
+    total = second[0]
+    for peer in range(1, groups):
+        total = total + second[peer]
+    out_ref[...] = total
+    for step in range(1, count):
+        copy(step, lax.rem(me + step, count), me).wait_send()
+    for step in range(1, groups):
+        copy2(step, lax.rem(group + step, groups), group).wait_send()
+
+
+def gain_sum(parts, groups, ident):
+    count = parts.shape[0]
+    shape = parts.shape[1:]
+    vmem = pltpu.VMEM
+    dma = pltpu.SemaphoreType.DMA
+    return pl.pallas_call(
+        functools.partial(gain_sum_kernel, count, groups),
+        out_shape=jax.ShapeDtypeStruct(shape, parts.dtype),
+        in_specs=[pl.BlockSpec(memory_space=vmem)],
+        out_specs=pl.BlockSpec(memory_space=vmem),
+        scratch_shapes=[
+            vmem((count,) + shape, parts.dtype),
+            vmem(shape, parts.dtype),
+            vmem((groups,) + shape, parts.dtype),
+            dma((count,)),
+            dma((count,)),
+            dma((groups,)),
+            dma((groups,)),
+        ],
+        compiler_params=pltpu.CompilerParams(collective_id=ident, has_side_effects=True),
+        name="gain_sum",
+    )(parts)
+
+
+MASKED = -1e30
+
+
+def probabilities(query, keys, rows_from, bias):
+    scores = dot_t(query, keys) * (1.0 / math.sqrt(HD))
+    row = lax.broadcasted_iota(jnp.int32, scores.shape, 0) + rows_from
+    col = lax.broadcasted_iota(jnp.int32, scores.shape, 1)
+    scores = jnp.where((col <= row) & (bias >= 0.0), scores, MASKED)
+    weight = jnp.exp(scores - jnp.max(scores, -1, keepdims=True))
+    return weight / jnp.sum(weight, -1, keepdims=True)
+
+
+def attention_grad_kernel(
+    line, split, seqs,
+    own, bias, cosine, sine, ffn_hbm, normed_hbm, attended_hbm, q_hbm, k_hbm, v_hbm, wq_hbm, wk_hbm, wv_hbm, wo_hbm, sums_hbm,
+    first, ffn_own, sums_in_hbm, mine_hbm, theirs_hbm,
+    dbranch, normed, attended, q, k, v, wq, wk, wv, wo, da, dk_acc, dv_acc, dq_rows, dk_rows, dv_rows, halves, half_in, ffn_parts, parts, stage,
+    g_local, g_send, g_recv, load_sem, sum_send, sum_recv, half_send, half_recv, stage_send, stage_recv, stage_local, *r_scratch,
+):
+    p = Place(line)
+    rank = lax.axis_index("grp")
+    core = lax.rem(rank, 2)
+    partner = rank + 1 - 2 * core
+    opposite = lax.rem(rank + 2, 4)
+    pairs_in = ((wo_hbm, wo), (q_hbm, q), (k_hbm, k), (v_hbm, v), (ffn_hbm, ffn_parts), (wq_hbm, wq), (wk_hbm, wk), (wv_hbm, wv), (attended_hbm, attended), (normed_hbm, normed))
+    loads = [pltpu.make_async_copy(src, dst, load_sem.at[i]) for i, (src, dst) in enumerate(pairs_in)]
+    for load in loads:
+        load.start()
+    p.greet((partner, opposite))
+    gather = Gather(p, split, own, dbranch, g_local, g_send, g_recv)
+    n_sums = sums_hbm.shape[0]
+
+    def sum_copy(i):
+        return pltpu.make_async_remote_copy(
+            src_ref=sums_hbm.at[i],
+            dst_ref=sums_in_hbm.at[i],
+            send_sem=sum_send.at[i],
+            recv_sem=sum_recv.at[i],
+            device_id={"grp": opposite},
+            device_id_type=MESH,
+        )
+
+    for i in range(n_sums):
+        sum_copy(i).start()
+    gather.start()
+    for load in loads:
+        load.wait()
+    rows = own.shape[0]
+    pair = 2 * rows
+    slots = rows // seqs
+    low = own.dtype
+    scale = 1.0 / math.sqrt(HD)
+
+    @pl.loop(0, line)
+    def _(i):
+        gather.hop(i + 1)
+        d = p.near(i)
+        gather.whole(d)
+        grad = dot_t(dbranch[pl.ds(2 * d, 2)].reshape(pair, -1), wo[...]).astype(low)
+        for block in range(2):
+            for n in range(seqs):
+                at = pl.ds(pl.multiple_of(d * 2 * slots + block * slots, slots), slots)
+                da[n, at] = grad[block * rows + n * slots : block * rows + (n + 1) * slots]
+
+    ffn_sum = Reduce(p, split, ffn_parts, ffn_own, r_scratch[: len(r_scratch) // 2])
+    for i in range(DEPTH):
+        ffn_sum.send_across(i)
+    for i in range(line - 1):
+        ffn_sum.b_hop(i)
+
+    total_slots = q.shape[1]
+    tile = min(256, total_slots)
+
+    def backward(n):
+        dk_acc[...] = jnp.zeros_like(dk_acc)
+        dv_acc[...] = jnp.zeros_like(dv_acc)
+
+        def to_rows(target, value, start, count):
+            for c in range(count // slots):
+                b = (start + c * slots) // slots
+                target[pl.ds(b * rows + n * slots, slots)] = value[c * slots : (c + 1) * slots]
+
+        for t in range(total_slots // tile):
+            span = (t + 1) * tile
+            at = pl.ds(t * tile, tile)
+            query, keys, values, grad = q[n, at], k[n, pl.ds(0, span)], v[n, pl.ds(0, span)], da[n, at]
+            probs = probabilities(query, keys, t * tile, bias[n][:, :span])
+            dprobs = dot_t(grad, values)
+            dscores = (probs * (dprobs - jnp.sum(probs * dprobs, -1, keepdims=True))).astype(low)
+            dq = jnp.dot(dscores, keys, preferred_element_type=F32) * scale
+            dq = dq * cosine[at] - turned(dq) * sine[at]
+            to_rows(dq_rows, dq.astype(low), t * tile, tile)
+            dk_acc[pl.ds(0, span)] += t_dot(dscores, query)
+            dv_acc[pl.ds(0, span)] += t_dot(probs.astype(low), grad)
+        dk = dk_acc[...] * scale
+        dk = (dk * cosine[...] - turned(dk) * sine[...]).astype(low)
+        dv = dv_acc[...].astype(low)
+        to_rows(dk_rows, dk, 0, total_slots)
+        to_rows(dv_rows, dv, 0, total_slots)
+
+    half = HD // 2
+
+    def swap():
+        return pltpu.make_async_remote_copy(
+            src_ref=halves.at[1 - p.y],
+            dst_ref=half_in,
+            send_sem=half_send,
+            recv_sem=half_recv,
+            device_id={"shard": p.cross},
+            device_id_type=MESH,
+        )
+
+    @pl.loop(0, seqs)
+    def _(n):
+        backward(n)
+        ffn_sum.hop(n)
+        ffn_sum.send_across(n + DEPTH)
+
+    for h in range(2):
+        at = pl.ds(h * half, half)
+        halves[h, 0] = dk_rows[:, at]
+        halves[h, 1] = dv_rows[:, at]
+    swap().start()
+    reduce = Reduce(p, split, parts, first, r_scratch[len(r_scratch) // 2 :])
+
+    @pl.loop(0, line)
+    def _(i):
+        d = p.far(i)
+        at = pl.ds(pl.multiple_of(d * pair, pair), pair)
+        part = jnp.dot(dq_rows[at], wq[...], preferred_element_type=F32)
+        part = part + jnp.dot(dk_rows[at], wk[...], preferred_element_type=F32)
+        part = part + jnp.dot(dv_rows[at], wv[...], preferred_element_type=F32)
+        parts[pl.ds(2 * d, 2)] = part.astype(low).reshape(2, rows, -1)
+        reduce.send_across(i)
+
+    for i in range(line - 1):
+        reduce.b_hop(i)
+    for i in range(seqs, line - 1):
+        ffn_sum.hop(i)
+    ffn_sum.finish()
+
+    chunk = half
+
+    def put(n, slot):
+        keep = (n // 3) == core
+        at = pl.ds(pl.multiple_of(lax.rem(n, 3) * chunk, chunk), chunk)
+        local = pltpu.make_async_copy(stage.at[slot], mine_hbm.at[at], stage_local.at[slot])
+        remote = pltpu.make_async_remote_copy(
+            src_ref=stage.at[slot],
+            dst_ref=theirs_hbm.at[at],
+            send_sem=stage_send.at[slot],
+            recv_sem=stage_recv.at[lax.rem(n, 3)],
+            device_id={"grp": partner},
+            device_id_type=MESH,
+        )
+        return keep, local, remote
+
+    def release(n):
+        keep, local, remote = put(n, n % 2)
+        either(keep, local.wait)
+        either(jnp.logical_not(keep), remote.wait_send)
+
+    def gradient(n, left, right):
+        slot = n % 2
+        if n >= 2:
+            release(n - 2)
+        stage[slot] = t_dot(left, right[...].reshape(left.shape[0], -1)).astype(low)
+        keep, local, remote = put(n, slot)
+        either(keep, local.start)
+        either(jnp.logical_not(keep), remote.start)
+
+    def summed(which):
+        return (halves[p.y, which].astype(F32) + half_in[which].astype(F32)).astype(low)
+
+    reduce.hop(0)
+    gradient(0, attended[:, :chunk], dbranch)
+    gradient(1, attended[:, chunk:], dbranch)
+    gradient(2, dq_rows[:, :chunk], normed)
+    reduce.hop(1)
+    gradient(3, dq_rows[:, chunk:], normed)
+    swap().wait_recv()
+    gradient(4, summed(0), normed)
+    gradient(5, summed(1), normed)
+    reduce.hop(2)
+    release(4)
+    release(5)
+    reduce.finish()
+    reduce.drain()
+    ffn_sum.drain()
+    gather.drain()
+    swap().wait_send()
+    for n in range(3):
+        put(n, 0)[2].wait_recv()
+    for i in range(n_sums):
+        sum_copy(i).wait_send()
+        sum_copy(i).wait_recv()
+
+
+def attention_grad(own, bias, cosine, sine, ffn_parts, normed, attended, q, k, v, wq, wk, wv, wo, sums, ident, split=112):
+    rows, width = own.shape
+    count = normed.shape[0]
+    line = count // 2
+    seqs, total_slots, hd = q.shape
+    low = own.dtype
+    hbm = pl.BlockSpec(memory_space=pl.ANY)
+    vm = pl.BlockSpec(memory_space=pltpu.VMEM)
+    vmem = pltpu.VMEM
+    dma = pltpu.SemaphoreType.DMA
+    tokens = count * rows
+    half = hd // 2
+    shape = jax.ShapeDtypeStruct
+    big = vmem((count, rows, width), low)
+    head = vmem((seqs, total_slots, hd), low)
+    weight = vmem((hd, width), low)
+    flat = vmem((tokens, hd), low)
+    return pl.pallas_call(
+        functools.partial(attention_grad_kernel, line, split, seqs),
+        out_shape=(
+            shape((rows, width), F32),
+            shape((rows, width), F32),
+            shape(sums.shape, low),
+            shape((3 * half, width), low),
+            shape((3 * half, width), low),
+        ),
+        in_specs=[vm] * 4 + [hbm] * 11,
+        out_specs=(vm, vm, hbm, hbm, hbm),
+        scratch_shapes=[
+            big, big, flat, head, head, head, weight, weight, weight, weight, head,
+            vmem((total_slots, hd), F32), vmem((total_slots, hd), F32),
+            flat, flat, flat,
+            vmem((2, 2, tokens, half), low), vmem((2, tokens, half), low),
+            big, big, vmem((2, half, width), low),
+            dma, dma((3, count, 2)), dma((count, 2)), dma((10,)), dma((sums.shape[0],)), dma((sums.shape[0],)),
+            dma, dma, dma((2,)), dma((3,)), dma((2,)),
+        ] + Reduce.scratch(line, rows, split, width, low) * 2,
+        compiler_params=pltpu.CompilerParams(collective_id=ident, has_side_effects=True, vmem_limit_bytes=VMEM_LIMIT),
+        name="attention_grad",
+    )(own, bias, cosine, sine, ffn_parts, normed, attended, q, k, v, wq, wk, wv, wo, sums)
+
+
+def between_chips(pair):
+    return lax.ppermute(pair, "grp", [(0, 2), (2, 0), (1, 3), (3, 1)])
+
+
+def both_halves(pair, other):
+    whole = (pair.astype(F32) + other.astype(F32)).astype(pair.dtype)
+    swapped = lax.ppermute(whole, "grp", [(0, 1), (1, 0), (2, 3), (3, 2)])
+    core = lax.rem(lax.axis_index("grp"), 2)
+    return jnp.concatenate(
+        [jnp.where(core == 0, whole, swapped), jnp.where(core == 0, swapped, whole)], -2
+    ).astype(F32)
 
 
 epsilon = 1e-06
@@ -79,7 +1011,7 @@
     return (weight_term, shard_rows)
 
 
-def local(
+def local_rows(
     tokens,
     lengths,
     prenorm_gain,
@@ -324,7 +1256,186 @@
     )
 
 
+def local_heads(
+    tokens,
+    lengths,
+    prenorm_gain,
+    query_weight,
+    key_weight,
+    value_weight,
+    out_weight,
+    midnorm_gain,
+    gate_weight,
+    up_weight,
+    down_weight,
+    cotangent,
+):
+    low = jnp.bfloat16
+    shard_count = lax.axis_size("shard")
+    shard_rank = lax.axis_index("shard")
+    seqs, seq_dev, model_width = tokens.shape
+    slot_count = seq_dev * shard_count
+    own_rows = seqs * seq_dev
+    score_scale = 1.0 / math.sqrt(HD)
+    half = HD // 2
+    upper = shard_rank % 2
+
+    def all_rows(rows, ident):
+        return gather(rows, shard_count, ident).reshape(shard_count * own_rows, -1)
+
+    def scatter(partial, ident):
+        return reduce(partial.astype(low).reshape(shard_count, own_rows, -1), ident)
+
+    def by_seq(rows):
+        width = rows.shape[-1]
+        return (
+            rows.reshape(shard_count, seqs, seq_dev, width)
+            .transpose(1, 0, 2, 3)
+            .reshape(seqs, slot_count, width)
+        )
+
+    def by_device(rows):
+        width = rows.shape[-1]
+        return (
+            rows.reshape(seqs, shard_count, seq_dev, width)
+            .transpose(1, 0, 2, 3)
+            .reshape(shard_count * own_rows, width)
+        )
+
+    def times(rows, weight):
+        return jnp.einsum("ta,ba->tb", rows, weight, preferred_element_type=jnp.float32)
+
+    def into(rows, weight):
+        return jnp.dot(rows, weight, preferred_element_type=jnp.float32)
+
+    def outer(left, right):
+        return jnp.einsum("tb,ta->ba", left, right, preferred_element_type=jnp.float32)
+
+    key_pos = jnp.arange(slot_count, dtype=jnp.int32)
+    local_pos = shard_rank * seq_dev + jnp.arange(seq_dev, dtype=jnp.int32)
+    inverse_freq = theta_base ** (-(jnp.arange(0, HD, 2).astype(jnp.float32) / HD))
+    angles = key_pos.astype(jnp.float32)[:, None] * inverse_freq[None, :]
+    cosine_table = jnp.concatenate([jnp.cos(angles), jnp.cos(angles)], -1)
+    sine_table = jnp.concatenate([jnp.sin(angles), jnp.sin(angles)], -1)
+
+    gains = jnp.broadcast_to(
+        jnp.stack([prenorm_gain, midnorm_gain])[:, None, :], (2, 8, prenorm_gain.shape[0])
+    ).reshape(16, -1)
+    tokens_all, gains = first_gather(
+        tokens.reshape(own_rows, model_width), gains, shard_count, 1
+    )
+    gains = gains.astype(jnp.float32)
+    prenorm_f = gains[:, 0].reshape(-1)
+    midnorm_f = gains[:, 8].reshape(-1)
+    valid_rows = (local_pos[None, :] < lengths[:, None]).reshape(own_rows, 1)
+    cot_low = jnp.where(valid_rows, cotangent.reshape(own_rows, model_width), jnp.zeros((), low))
+
+    swaps = [(rank, rank ^ 1) for rank in range(shard_count)]
+    swapped = lax.ppermute(jnp.concatenate([key_weight, value_weight], 0), "shard", swaps)
+    key_swap, value_swap = swapped[:half], swapped[half:]
+
+    def whole_head(own, other):
+        return jnp.concatenate(
+            [jnp.where(upper == 0, own, other), jnp.where(upper == 0, other, own)], 0
+        )
+
+    key_head = whole_head(key_weight, key_swap)
+    value_head = whole_head(value_weight, value_swap)
+
+    source = tokens.reshape(own_rows, model_width).astype(jnp.float32)
+    inverse_first = lax.rsqrt(jnp.mean(source * source, -1, keepdims=True) + epsilon)
+    normed_first = (
+        norm_forward(
+            tokens_all.reshape(shard_count * own_rows, model_width).astype(jnp.float32), prenorm_f
+        )[0]
+    ).astype(low)
+    cot_all = all_rows(cot_low, 3)
+
+    queries = rotate(by_seq(times(normed_first, query_weight)), cosine_table, sine_table).astype(low)
+    keys = rotate(by_seq(times(normed_first, key_head)), cosine_table, sine_table).astype(low)
+    values = by_seq(times(normed_first, value_head).astype(low))
+    scores = (
+        jnp.einsum("sqd,skd->sqk", queries, keys, preferred_element_type=jnp.float32) * score_scale
+    )
+    allowed = (key_pos[None, None, :] <= key_pos[None, :, None]) & (
+        key_pos[None, None, :] < lengths[:, None, None]
+    )
+    scores = jnp.where(allowed, scores, masked_value)
+    exp_scores = jnp.exp(scores - jnp.max(scores, -1, keepdims=True))
+    probs = exp_scores / jnp.sum(exp_scores, -1, keepdims=True)
+    probs_low = probs.astype(low)
+    attended = by_device(
+        jnp.einsum(
+            "sqk,skd->sqd", probs_low, values, preferred_element_type=jnp.float32
+        ).astype(low)
+    )
+    middle = source + scatter(into(attended, out_weight), 4)
+    scaled_second, inverse_second = norm_forward(middle, midnorm_f)
+    second_grad, ffn_parts, mine, theirs = ffn(
+        scaled_second.astype(low),
+        cot_all.reshape(shard_count, own_rows, model_width),
+        gate_weight,
+        up_weight,
+        down_weight,
+        5,
+    )
+    ffn_pair = (mine.astype(F32) + theirs.astype(F32)).astype(low)
+
+    middle_part, midnorm_part = norm_backward(middle, inverse_second, midnorm_f, second_grad)
+    middle_grad = cot_low.astype(jnp.float32) + middle_part
+    bias = jnp.where(key_pos[None, None, :] < lengths[:, None, None], 0.0, -1.0)
+    first_grad, ffn_part, ffn_other, mine, theirs = attention_grad(
+        middle_grad.astype(low),
+        bias,
+        cosine_table,
+        sine_table,
+        ffn_parts,
+        normed_first.reshape(shard_count, own_rows, model_width),
+        attended,
+        queries,
+        keys,
+        values,
+        query_weight,
+        key_head,
+        value_head,
+        out_weight,
+        ffn_pair,
+        6,
+    )
+    mixed = jnp.where(valid_rows, middle + ffn_part, 0.0).astype(low)
+    attn_pair = (mine.astype(F32) + theirs.astype(F32)).astype(low)
+    attn_total = both_halves(attn_pair, between_chips(attn_pair))
+    down_total, gate_total, up_total = (
+        both_halves(ffn_pair[i], ffn_other[i]) for i in range(3)
+    )
+
+    source_part, prenorm_part = norm_backward(source, inverse_first, prenorm_f, first_grad)
+    input_gradient = (middle_grad + source_part).astype(low)
+
+    gain_parts = jnp.stack([prenorm_part, midnorm_part]).reshape(2, shard_count, 1, -1)
+    gain_parts = jnp.broadcast_to(
+        gain_parts.transpose(1, 0, 2, 3), (shard_count, 2, 8, gain_parts.shape[-1])
+    )
+    gain_own = gain_sum(gain_parts, lax.axis_size("grp"), 10)[:, 0]
+    share = query_weight.shape[0]
+    kv_share = key_weight.shape[0]
+    return (
+        mixed.reshape(tokens.shape),
+        input_gradient.reshape(tokens.shape),
+        gain_own[0],
+        attn_total[share : 2 * share],
+        attn_total[2 * share : 2 * share + kv_share],
+        attn_total[2 * share + kv_share :],
+        attn_total[:share],
+        gain_own[1],
+        gate_total,
+        up_total,
+        down_total,
+    )
+
+
 def solution(mesh):
+    local = local_heads if mesh.shape["shard"] == NH else local_rows
     in_specs = (
         P("grp", "shard", None),
         P("grp"),

time: 2350 us -> 598 us (0.25)
  waiting for transfers between devices: 1890 us -> 0.02 us
  Pallas kernels: 0 us -> 481 us
  matrix products: 213 us -> 11.7 us
  blocking collectives: 81.7 us -> 0 us
  local copies, waits for them, and re-layouts: 45.9 us -> 10.2 us
    reduce_scatter x8 -> x0, waiting for transfers between devices: 1110 us -> none  [the longest x2 742 us: local(): lax.psum_scatter(weight_term(jnp.int32(0), lax.axis_size('shard') * shard...]
    all_gather x10 -> x0, waiting for transfers between devices: 575 us -> none  [the longest x1 121 us: local(): lax.all_gather(query_weight, 'shard', axis=0, tiled=True)]
    pallas_call x0 -> x6, Pallas kernels: none -> 481 us  [the longest x1 183 us: attention_grad(): pl.pallas_call(functools.partial(attention_grad_kernel, line, split, seqs...]
    dot_general x54 -> x5, matrix products: 213 us -> 9.43 us  [the longest x3 3.94 us: times(): jnp.einsum('ta,ba->tb', rows, weight, preferred_element_type=jnp.float32)]
    psum x1 -> x0, waiting for transfers between devices: 201 us -> none  [local(): lax.psum(attn_total.astype(jnp.bfloat16), 'grp').astype(jnp.float32)]
    psum x1 -> x0, blocking collectives: 41.1 us -> none  [local(): gain_sums = lax.psum((prenorm_total, midnorm_total), ('grp', 'shard'))]
    all_gather x2 -> x0, blocking collectives: 40.7 us -> none  [the longest x1 22.4 us: local(): lax.all_gather(prenorm_gain, 'shard', axis=0, tiled=True)]
    concatenate x7 -> x3, other arithmetic: 42.7 us -> 3.83 us  [the longest x1 1.45 us: whole_head(): jnp.concatenate([jnp.where(upper == 0, own, other), jnp.where(upper == 0,...]
  transfers between devices with their start and end apart: 19 -> 6, of which waited for: 19 -> 0; matrix products, arithmetic and copies ran while one was open for 12% -> 9% of each run, Pallas kernels for 0% -> 24%
where the time goes in v3:
time: 598 us; the launch traced here: 589 us
  Pallas kernels  481 us (80%)
  other arithmetic  80 us (13%)
  matrix products  11.7 us (2%)
  local copies, waits for them, and re-layouts  10.2 us (2%)
    pallas_call x1, Pallas kernels, attention_grad(): pl.pallas_call(functools.partial(attention_grad_kernel, line, split, seqs...  183 us
    pallas_call x1, Pallas kernels, ffn(): pl.pallas_call(functools.partial(ffn_kernel, count // 2, split), out_shap...  110 us
    pallas_call x1, Pallas kernels, first_gather(): pl.pallas_call(functools.partial(first_gather_kernel, count // 2, split),...  61.3 us
    pallas_call x1, Pallas kernels, gather(): pl.pallas_call(functools.partial(gather_kernel, count // 2, split), out_s...  53.9 us
    pallas_call x1, Pallas kernels, reduce(): pl.pallas_call(functools.partial(reduce_kernel, count // 2, split), out_s...  48.6 us
    pallas_call x1, Pallas kernels, gain_sum(): pl.pallas_call(functools.partial(gain_sum_kernel, count, groups), out_sha...  23.7 us
    convert_element_type x4, other arithmetic, both_halves(): return jnp.concatenate([jnp.where(core == 0, whole, swapped), jnp.where(c...  13.7 us
  transfers between devices with their start and end apart: 6, of which 0 were waited for; matrix products, arithmetic and copies ran while one was open for 9% of the time, Pallas kernels for 24%

profile of v3, /device:TPU:0, one launch (start us, length us, event | category | flops | bytes accessed | tf_op | source)
XLA Modules:
  0.0 589.5 jit_solution(14531288996523585602)
XLA Ops:
  1.9 3.0 collective-permute-start
  9.7 61.3 %first_gather.1 = (bf16[8,128,2048]{2,1,0:T(8,128)(2,1)}, bf16[8,16,256]{2,1,0:T(8,128)(2,1)}) custom-call(bf16[128,2048]{1,0:T(8,128)(2,1)} %bitcast.76, bf16[16,256]{1,0:T(8,128)(2,1)} %broadcast_bitcast_fusion.small), custom_call_target="tpu_custom_call" | custom-call | tf_op jit(solution)/shard_map/first_gather/pallas_call | solution.py:596
  71.8 3.1 multiply_reduce_fusion
  75.0 5.4 multiply_convert_fusion.normed_hbm
  85.2 53.9 %gather.1.cot_hbm = bf16[8,128,2048]{2,1,0:T(8,128)(2,1)} custom-call(bf16[128,2048]{1,0:T(8,128)(2,1)} %bitcast_select_fusion.own), custom_call_target="tpu_custom_call" | custom-call | tf_op jit(solution)/shard_map/gather/pallas_call | solution.py:508
  141.1 3.3 fusion.2
  144.7 1.9 copy-done.1
  152.0 2.3 fusion.35
  154.3 2.2 convolution_convert_fusion.1
  156.6 3.3 convolution_convert_fusion
  159.9 48.6 %reduce.3 = f32[128,2048]{1,0:T(8,128)} custom-call(bf16[8,128,2048]{2,1,0:T(8,128)(2,1)} %bitcast.75), custom_call_target="tpu_custom_call" | custom-call | tf_op jit(solution)/shard_map/reduce/pallas_call | solution.py:538
  211.9 110.3 %ffn.1 = (f32[128,2048]{1,0:T(8,128)}, bf16[8,128,2048]{2,1,0:T(8,128)(2,1)}, bf16[3,512,2048]{2,1,0:T(8,128)(2,1)}, bf16[3,512,2048]{2,1,0:T(8,128)(2,1)}) custom-call(bf16[128,2048]{1,0:T(8,128)(2,1)} %multiply_convert_fusion.4.own, bf16[8,128,2048]{2,1,0:T(8,128)(2,1)} %gather.1.cot_hbm, bf16[1024,2048]{1,0:T(8,128)(2,1)} %gate_hbm.1, ...), custom_call_target="tpu_custom_call" | custom-call | tf_op jit(solution)/shard_map/ffn/pallas_call | solution.py:464
  324.0 3.3 fusion.32
  327.3 11.0 %add_convert_fusion.sums_hbm = bf16[3,512,2048]{2,1,0:T(8,128)(2,1)} fusion(bf16[3,512,2048]{2,1,0:T(8,128)(2,1)} %get-tuple-element.27, bf16[3,512,2048]{2,1,0:T(8,128)(2,1)} %get-tuple-element.26), kind=kLoop, calls=%fused_computation.1 | loop fusion | flops 12582912 | bytes 18874368 | tf_op jit(solution)/shard_map/convert_element_type | solution.py:1382
  338.3 183.2 %attention_grad.1 = (f32[128,2048]{1,0:T(8,128)}, f32[128,2048]{1,0:T(8,128)}, bf16[3,512,2048]{2,1,0:T(8,128)(2,1)}, bf16[384,2048]{1,0:T(8,128)(2,1)}, bf16[384,2048]{1,0:T(8,128)(2,1)}) custom-call(bf16[128,2048]{1,0:T(8,128)(2,1)} %get-tuple-element.37.own, f32[2,1,512]{2,1,0:T(1,128)} %compare_select_fusion.bias, f32[512,256]{1,0:T(8,128)} %copy-done.6, ...), custom_call_target="tpu_custom_call" | custom-call | tf_op jit(solution)/shard_map/attention_grad/pallas_call | solution.py:907
  521.5 7.6 %fusion.5 = (bf16[512,2048]{1,0:T(8,128)(2,1)S(1)}, bf16[512,2048]{1,0:T(8,128)(2,1)}, bf16[512,2048]{1,0:T(8,128)(2,1)}) fusion(bf16[3,512,2048]{2,1,0:T(8,128)(2,1)} %add_convert_fusion.sums_hbm, bf16[3,512,2048]{2,1,0:T(8,128)(2,1)} %get-tuple-element.32), kind=kLoop, calls=%fused_computation.20 | loop fusion | flops 12582912 | bytes 18874368 | tf_op jit(solution)/shard_map/convert_element_type | solution.py:937
  534.5 23.7 %gain_sum.1 = f32[2,8,256]{2,1,0:T(8,128)} custom-call(f32[8,2,8,256]{3,2,1,0:T(8,128)} %broadcast_in_dim.48.parts_ref), custom_call_target="tpu_custom_call" | custom-call | tf_op jit(solution)/shard_map/gain_sum/pallas_call | solution.py:673
  559.7 2.8 fusion.13
  562.4 2.5 add_convert_fusion.4
  565.4 2.5 broadcast_select_fusion.3
  567.9 2.5 broadcast_select_fusion.5
  570.4 4.3 maximum_convert_fusion
  574.7 4.3 maximum_convert_fusion.1
  579.3 4.3 maximum_convert_fusion.2
  (103 shorter events, 37.8 us)
Async XLA Ops:
  1.9 142.5 %collective-permute-start = (bf16[256,2048]{1,0:T(8,128)(2,1)S(1)}, bf16[256,2048]{1,0:T(8,128)(2,1)S(1)}, u32[]{:S(2)}, u32[]{:S(2)}) collective-permute-start(bf16[256,2048]{1,0:T(8,128)(2,1)S(1)} %pad_maximum_fusion), channel_id=1, source_target_pairs={{0,1},{1,0},{2,3},{3,2},{4,5},{5,4},{6,7},{7,6},{8,9},{9,8},{10,11... | collective-permute-start | bytes 3145736 | tf_op jit(solution)/shard_map/ppermute | solution.py:1334
  75.0 7.1 %copy-start.13 = (bf16[2,64,2048]{2,1,0:T(8,128)(2,1)S(1)}, bf16[2,64,2048]{2,1,0:T(8,128)(2,1)}, u32[]{:S(2)}) copy-start(bf16[2,64,2048]{2,1,0:T(8,128)(2,1)} %param.23) | copy-start | bytes 1572868
  75.0 8.0 %copy-start = (bf16[8,128,2048]{2,1,0:T(8,128)(2,1)S(1)}, bf16[8,128,2048]{2,1,0:T(8,128)(2,1)}, u32[]{:S(2)}) copy-start(bf16[8,128,2048]{2,1,0:T(8,128)(2,1)} %get-tuple-element.22) | copy-start | bytes 12582916
  75.0 8.0 %copy-start.18 = (bf16[256,2048]{1,0:T(8,128)(2,1)S(1)}, bf16[256,2048]{1,0:T(8,128)(2,1)}, u32[]{:S(2)}) copy-start(bf16[256,2048]{1,0:T(8,128)(2,1)} %wq_hbm.1) | copy-start | bytes 3145732
  85.2 55.1 %copy-start.21 = (s32[2]{0:T(128)S(1)}, s32[2]{0:T(128)}, u32[]{:S(2)}) copy-start(s32[2]{0:T(128)} %param.13) | copy-start | bytes 28
  140.3 10.7 %copy-start.6 = (f32[512,256]{1,0:T(8,128)}, f32[512,256]{1,0:T(8,128)S(1)}, u32[]{:S(2)}) copy-start(f32[512,256]{1,0:T(8,128)S(1)} %get-tuple-element.78.cosine) | copy-start | bytes 1572868
  140.3 10.7 %copy-start.7 = (f32[512,256]{1,0:T(8,128)}, f32[512,256]{1,0:T(8,128)S(1)}, u32[]{:S(2)}) copy-start(f32[512,256]{1,0:T(8,128)S(1)} %get-tuple-element.79.sine) | copy-start | bytes 1572868
  141.1 3.3 copy-start.14
  141.1 3.3 copy-start.15
  150.9 3.4 copy-start.12
  151.4 5.1 copy-start.10
  151.4 5.1 copy-start.11
  156.6 3.3 copy-start.5
  159.9 48.6 %copy-start.4 = (bf16[2,64,2048]{2,1,0:T(8,128)(2,1)S(1)}, bf16[2,64,2048]{2,1,0:T(8,128)(2,1)}, u32[]{:S(2)}) copy-start(bf16[2,64,2048]{2,1,0:T(8,128)(2,1)} %param.12) | copy-start | bytes 1572868
  521.5 7.6 %copy-start.16 = (bf16[384,2048]{1,0:T(8,128)(2,1)S(1)}, bf16[384,2048]{1,0:T(8,128)(2,1)}, u32[]{:S(2)}) copy-start(bf16[384,2048]{1,0:T(8,128)(2,1)} %get-tuple-element.30) | copy-start | bytes 4718596
  521.5 7.6 %copy-start.17 = (bf16[384,2048]{1,0:T(8,128)(2,1)S(1)}, bf16[384,2048]{1,0:T(8,128)(2,1)}, u32[]{:S(2)}) copy-start(bf16[384,2048]{1,0:T(8,128)(2,1)} %get-tuple-element.31) | copy-start | bytes 4718596
  529.1 3.5 copy-start.3
  529.1 3.5 copy-start.19
  529.1 4.4 copy-start.8
  531.0 31.5 %collective-permute-start.1 = (bf16[384,2048]{1,0:T(8,128)(2,1)}, bf16[384,2048]{1,0:T(8,128)(2,1)}, u32[]{:S(2)}, u32[]{:S(2)}) collective-permute-start(bf16[384,2048]{1,0:T(8,128)(2,1)} %add_convert_fusion.5), channel_id=1, source_target_pairs={{0,16},{16,0},{8,24},{24,8},{1,17},{17,1},{9,25},{25,9},{2,18},{18... | collective-permute-start | bytes 4718600 | tf_op jit(solution)/shard_map/ppermute | solution.py:933
  532.1 33.4 %collective-permute-start.4 = (bf16[512,2048]{1,0:T(8,128)(2,1)}, bf16[512,2048]{1,0:T(8,128)(2,1)}, u32[]{:S(2)}, u32[]{:S(2)}) collective-permute-start(bf16[512,2048]{1,0:T(8,128)(2,1)} %get-tuple-element.42), channel_id=1, source_target_pairs={{0,8},{8,0},{16,24},{24,16},{1,9},{9,1},{17,25},{25,17},{2,10},{10... | collective-permute-start | bytes 6291464 | tf_op jit(solution)/shard_map/ppermute | solution.py:938
  532.1 35.9 %collective-permute-start.3 = (bf16[512,2048]{1,0:T(8,128)(2,1)}, bf16[512,2048]{1,0:T(8,128)(2,1)}, u32[]{:S(2)}, u32[]{:S(2)}) collective-permute-start(bf16[512,2048]{1,0:T(8,128)(2,1)} %get-tuple-element.43), channel_id=1, source_target_pairs={{0,8},{8,0},{16,24},{24,16},{1,9},{9,1},{17,25},{25,17},{2,10},{10... | collective-permute-start | bytes 6291464 | tf_op jit(solution)/shard_map/ppermute | solution.py:938
  558.2 20.8 %collective-permute-start.5 = (bf16[512,2048]{1,0:T(8,128)(2,1)S(1)}, bf16[512,2048]{1,0:T(8,128)(2,1)S(1)}, u32[]{:S(2)}, u32[]{:S(2)}) collective-permute-start(bf16[512,2048]{1,0:T(8,128)(2,1)S(1)} %get-tuple-element.41), channel_id=1, source_target_pairs={{0,8},{8,0},{16,24},{24,16},{1,9},{9,1},{17,25},{25,17},{2,10},{10... | collective-permute-start | bytes 6291464 | tf_op jit(solution)/shard_map/ppermute | solution.py:938
  565.0 18.6 %collective-permute-start.2 = (bf16[384,2048]{1,0:T(8,128)(2,1)S(1)}, bf16[384,2048]{1,0:T(8,128)(2,1)S(1)}, u32[]{:S(2)}, u32[]{:S(2)}) collective-permute-start(bf16[384,2048]{1,0:T(8,128)(2,1)S(1)} %add_convert_fusion.4), channel_id=1, source_target_pairs={{0,8},{8,0},{16,24},{24,16},{1,9},{9,1},{17,25},{25,17},{2,10},{10... | collective-permute-start | bytes 4718600 | tf_op jit(solution)/shard_map/ppermute | solution.py:938
  (4 other events, 6.4 us)

commit v4 on v0

--- a/solution.py
+++ b/solution.py
@@ -1,13 +1,1114 @@
+import functools
 import math
 
 import jax
 import jax.numpy as jnp
 from jax import lax
+from jax.experimental import pallas as pl
+from jax.experimental.pallas import tpu as pltpu
 from jax.sharding import PartitionSpec as P
 
 NH = 8
 KVH = 4
 HD = 256
+MASKED = -1e30
+EPSILON = 1e-06
+DEPTH = 2
+MESH = pl.DeviceIdType.MESH
+F32 = jnp.float32
+VMEM_LIMIT = 66_000_000
+
+
+def either(condition, action):
+    pl.when(condition)(action)
+
+
+def total_into(dst, *srcs):
+    step = 16
+
+    @pl.loop(0, dst.shape[0] // step)
+    def _(i):
+        at = pl.ds(pl.multiple_of(i * step, step), step)
+        value = srcs[0][at].astype(F32)
+        for src in srcs[1:]:
+            value = value + src[at].astype(F32)
+        dst[at] = value.astype(dst.dtype)
+
+
+class Place:
+    def __init__(self, line):
+        self.line = line
+        self.me = lax.axis_index("shard")
+        self.z = self.me // 2
+        self.y = lax.rem(self.me, 2)
+        self.cross = self.me + 1 - 2 * self.y
+        self.low_end = self.z == 0
+        self.high_end = self.z == line - 1
+        near = []
+        for z in range(line):
+            order = [z]
+            for k in range(1, line):
+                order += [d for d in (z - k, z + k) if 0 <= d < line]
+            near.append(order)
+        self.tables = near
+
+    def near(self, i):
+        out = jnp.int32(0)
+        for z in range(self.line):
+            row = jnp.int32(self.tables[z][0])
+            for k in range(1, self.line):
+                row = jnp.where(i == k, self.tables[z][k], row)
+            out = jnp.where(self.z == z, row, out)
+        return out
+
+    def far(self, i):
+        return self.near(self.line - 1 - i)
+
+    def greet(self, groups):
+        barrier = pltpu.get_barrier_semaphore()
+        count = 2 * self.line
+        rank = lax.axis_index("grp")
+        for step in range(1, count):
+            pl.semaphore_signal(
+                barrier,
+                inc=1,
+                device_id={"shard": lax.rem(self.me + step, count)},
+                device_id_type=MESH,
+            )
+        for step in range(1, groups):
+            pl.semaphore_signal(
+                barrier,
+                inc=1,
+                device_id={"grp": lax.rem(rank + step, groups)},
+                device_id_type=MESH,
+            )
+        pl.semaphore_wait(barrier, count + groups - 2)
+
+
+class Gather:
+    UP, DOWN, CROSS = 0, 1, 2
+
+    def __init__(self, place, split, own, out, local_sem, send_sem, recv_sem):
+        self.p, self.own, self.out = place, own, out
+        self.local_sem, self.send_sem, self.recv_sem = local_sem, send_sem, recv_sem
+        self.parts = (pl.ds(0, split), pl.ds(split, own.shape[0] - split))
+
+    def copy(self, way, origin, part, own=False):
+        p = self.p
+        peer = (p.me + 2, p.me - 2, p.cross)[way]
+        at = self.parts[part]
+        return pltpu.make_async_remote_copy(
+            src_ref=self.own.at[at] if own else self.out.at[origin, at],
+            dst_ref=self.out.at[origin, at],
+            send_sem=self.send_sem.at[way, origin, part],
+            recv_sem=self.recv_sem.at[origin, part],
+            device_id={"shard": peer},
+            device_id_type=MESH,
+        )
+
+    def arrived(self, origin, part):
+        self.copy(self.CROSS, origin, part).wait_recv()
+
+    def start(self):
+        p = self.p
+        self.keep = pltpu.make_async_copy(self.own, self.out.at[p.me], self.local_sem)
+        self.keep.start()
+        self.copy(self.CROSS, p.me, 1, True).start()
+        self.copy(self.CROSS, p.me, 0, True).start()
+        for part in (0, 1):
+            either(p.z < p.line - 1, lambda: self.copy(self.UP, p.me, part, True).start())
+            either(p.z > 0, lambda: self.copy(self.DOWN, p.me, part, True).start())
+        self.arrived(p.cross, 1)
+        either(p.z < p.line - 1, lambda: self.copy(self.UP, p.cross, 1).start())
+        either(p.z > 0, lambda: self.copy(self.DOWN, p.cross, 1).start())
+        self.keep.wait()
+
+    def hop(self, k):
+        p = self.p
+
+        def take(origin, other, way, more):
+            self.arrived(origin, 0)
+            self.copy(self.CROSS, origin, 0).start()
+            either(more, lambda: self.copy(way, origin, 0).start())
+            for block in (origin, other):
+                self.arrived(block, 1)
+                either(more, lambda: self.copy(way, block, 1).start())
+
+        below, above = p.me - 2 * k, p.me + 2 * k
+        either(p.z - k >= 0, lambda: take(below, p.cross - 2 * k, self.UP, p.z < p.line - 1))
+        either(p.z + k < p.line, lambda: take(above, p.cross + 2 * k, self.DOWN, p.z > 0))
+
+    def whole(self, position):
+        self.arrived(2 * position + 1 - self.p.y, 0)
+
+    def drain(self):
+        p = self.p
+
+        @pl.loop(0, p.line)
+        def _(d):
+            mine, other = 2 * d + p.y, 2 * d + 1 - p.y
+            self.copy(self.CROSS, mine, 0).wait_send()
+
+            @pl.when(d == p.z)
+            def _():
+                self.copy(self.CROSS, mine, 1).wait_send()
+
+            @pl.when((d <= p.z) & (p.z < p.line - 1))
+            def _():
+                for block, part in ((mine, 0), (mine, 1), (other, 1)):
+                    self.copy(self.UP, block, part).wait_send()
+
+            @pl.when((d >= p.z) & (p.z > 0))
+            def _():
+                for block, part in ((mine, 0), (mine, 1), (other, 1)):
+                    self.copy(self.DOWN, block, part).wait_send()
+
+
+class Reduce:
+    UP, DOWN, CROSS, BUP, BDN, BX = 0, 1, 2, 3, 5, 7
+    N_SCRATCH = 9
+
+    @staticmethod
+    def scratch(line, rows, split, width, dtype):
+        v = pltpu.VMEM
+        rest = rows - split
+        dma = pltpu.SemaphoreType.DMA
+        return (
+            [v((line, split, width), dtype)] * 3
+            + [v((line, 2, rest, width), dtype)] * 2
+            + [v((rest, width), dtype)] * 2
+            + [dma((8, line)), dma((8, line))]
+        )
+
+    def __init__(self, place, split, parts, out, scratch):
+        self.p, self.parts, self.out = place, parts, out
+        self.cross_in, self.up_in, self.down_in, self.bup_in, self.bdn_in = scratch[:5]
+        self.bx_out, self.bx_in, self.send_sem, self.recv_sem = scratch[5:]
+        self.a = pl.ds(0, split)
+        self.b = pl.ds(split, parts.shape[1] - split)
+
+    def desc(self, way, slot, src, dst, peer):
+        return pltpu.make_async_remote_copy(
+            src_ref=src,
+            dst_ref=dst,
+            send_sem=self.send_sem.at[way, slot],
+            recv_sem=self.recv_sem.at[way, slot],
+            device_id={"shard": peer},
+            device_id_type=MESH,
+        )
+
+    def cross_copy(self, d):
+        p = self.p
+        return self.desc(
+            self.CROSS, d, self.parts.at[2 * d + 1 - p.y, self.a], self.cross_in.at[d], p.cross
+        )
+
+    def line_copy(self, up, d):
+        p = self.p
+        if up:
+            return self.desc(self.UP, d, self.cross_in.at[d], self.up_in.at[d], p.me + 2)
+        return self.desc(self.DOWN, d, self.cross_in.at[d], self.down_in.at[d], p.me - 2)
+
+    def b_copy(self, up, d, o, src=None):
+        p = self.p
+        held = self.bup_in if up else self.bdn_in
+        return self.desc(
+            (self.BUP if up else self.BDN) + o,
+            d,
+            held.at[d, o] if src is None else src,
+            held.at[d, o],
+            p.me + 2 if up else p.me - 2,
+        )
+
+    def bx_copy(self):
+        return self.desc(self.BX, 0, self.bx_out, self.bx_in, self.p.cross)
+
+    def column(self, o):
+        return self.p.y if o == 0 else 1 - self.p.y
+
+    def send_across(self, i):
+        self.cross_copy(self.p.far(i)).start()
+
+    def b_hop(self, i):
+        p = self.p
+        d = p.far(i)
+
+        def go(up):
+            first = p.low_end if up else p.high_end
+            held = self.bup_in if up else self.bdn_in
+            for o in (1, 0):
+                mine = self.parts.at[2 * d + self.column(o), self.b]
+                either(first, lambda: self.b_copy(up, d, o, mine).start())
+
+                @pl.when(jnp.logical_not(first))
+                def _():
+                    self.b_copy(up, d, o).wait_recv()
+                    total_into(held.at[d, o], mine, held.at[d, o])
+                    self.b_copy(up, d, o).start()
+
+        either(d > p.z, lambda: go(True))
+        either(d < p.z, lambda: go(False))
+
+    def hop(self, i):
+        p = self.p
+        d = p.far(i)
+        self.cross_copy(d).wait_recv()
+        mine = self.parts.at[2 * d + p.y, self.a]
+        held = self.cross_in.at[d]
+
+        def go(up):
+            first = p.low_end if up else p.high_end
+            came = self.up_in if up else self.down_in
+            either(first, lambda: total_into(held, mine, held))
+
+            @pl.when(jnp.logical_not(first))
+            def _():
+                self.line_copy(up, d).wait_recv()
+                total_into(held, mine, held, came.at[d])
+
+            self.line_copy(up, d).start()
+
+        either(d > p.z, lambda: go(True))
+        either(d < p.z, lambda: go(False))
+
+    def close(self, dst, mine, ups, downs):
+        p = self.p
+        either(p.low_end, lambda: total_into(dst, *mine, downs))
+        either(p.high_end, lambda: total_into(dst, *mine, ups))
+        either(
+            jnp.logical_not(p.low_end | p.high_end), lambda: total_into(dst, *mine, ups, downs)
+        )
+
+    def finish(self):
+        p = self.p
+        for o in (1, 0):
+            either(jnp.logical_not(p.low_end), lambda: self.b_copy(True, p.z, o).wait_recv())
+            either(jnp.logical_not(p.high_end), lambda: self.b_copy(False, p.z, o).wait_recv())
+            if o:
+                mine = self.parts.at[2 * p.z + self.column(o), self.b]
+                self.close(self.bx_out, (mine,), self.bup_in.at[p.z, o], self.bdn_in.at[p.z, o])
+                self.bx_copy().start()
+        self.bx_copy().wait_recv()
+        self.close(
+            self.out.at[self.b],
+            (self.parts.at[p.me, self.b], self.bx_in),
+            self.bup_in.at[p.z, 0],
+            self.bdn_in.at[p.z, 0],
+        )
+        self.cross_copy(p.z).wait_recv()
+        either(jnp.logical_not(p.low_end), lambda: self.line_copy(True, p.z).wait_recv())
+        either(jnp.logical_not(p.high_end), lambda: self.line_copy(False, p.z).wait_recv())
+        self.close(
+            self.out.at[self.a],
+            (self.parts.at[p.me, self.a], self.cross_in.at[p.z]),
+            self.up_in.at[p.z],
+            self.down_in.at[p.z],
+        )
+
+    def drain(self):
+        p = self.p
+        self.bx_copy().wait_send()
+
+        @pl.loop(0, p.line)
+        def _(d):
+            self.cross_copy(d).wait_send()
+
+            @pl.when(d > p.z)
+            def _():
+                self.line_copy(True, d).wait_send()
+                self.b_copy(True, d, 0).wait_send()
+                self.b_copy(True, d, 1).wait_send()
+
+            @pl.when(d < p.z)
+            def _():
+                self.line_copy(False, d).wait_send()
+                self.b_copy(False, d, 0).wait_send()
+                self.b_copy(False, d, 1).wait_send()
+
+
+def dot(a, b):
+    return jnp.dot(a, b, preferred_element_type=F32)
+
+
+def dot_t(a, b):
+    return lax.dot_general(a, b, (((1,), (1,)), ((), ())), preferred_element_type=F32)
+
+
+def t_dot(a, b):
+    return lax.dot_general(a, b, (((0,), (0,)), ((), ())), preferred_element_type=F32)
+
+
+def to_peer(axis, peer, src, dst, send_sem, recv_sem):
+    return pltpu.make_async_remote_copy(
+        src_ref=src,
+        dst_ref=dst,
+        send_sem=send_sem,
+        recv_sem=recv_sem,
+        device_id={axis: peer},
+        device_id_type=MESH,
+    )
+
+
+def turn_by(v, cosine, sine):
+    half = v.shape[-1] // 2
+    a, b = v[:, :half], v[:, half:]
+    return jnp.concatenate([a * cosine - b * sine, b * cosine + a * sine], -1)
+
+
+def turn_back(v, cosine, sine):
+    return turn_by(v, cosine, -sine)
+
+
+def probabilities(query, keys, rows_from, bias):
+    scores = dot_t(query, keys) * (1.0 / math.sqrt(HD))
+    row = lax.broadcasted_iota(jnp.int32, scores.shape, 0) + rows_from
+    col = lax.broadcasted_iota(jnp.int32, scores.shape, 1)
+    scores = jnp.where((col <= row) & (bias >= 0.0), scores, MASKED)
+    weight = jnp.exp(scores - jnp.max(scores, -1, keepdims=True))
+    return weight / jnp.sum(weight, -1, keepdims=True)
+
+
+def start_all(copies):
+    for c in copies:
+        c.start()
+
+
+def wait_all(copies):
+    for c in copies:
+        c.wait()
+
+
+def hbm():
+    return pl.BlockSpec(memory_space=pl.ANY)
+
+
+def vm():
+    return pl.BlockSpec(memory_space=pltpu.VMEM)
+
+
+def params(ident):
+    return pltpu.CompilerParams(
+        collective_id=ident, has_side_effects=True, vmem_limit_bytes=VMEM_LIMIT
+    )
+
+
+DMA = pltpu.SemaphoreType.DMA
+
+
+def gather_sems(count):
+    return [DMA, DMA((3, count, 2)), DMA((count, 2))]
+
+
+def attention_kernel(
+    line, split, groups, seqs,
+    own, cot_own, small, bias, freq, wq_hbm, wk_hbm, wv_hbm, wo_hbm,
+    branch, small_out, normed_hbm, cot_hbm, q_hbm, k_hbm, v_hbm, attended_hbm, wkv_hbm, cos_hbm, sin_hbm,
+    rows_all, normed, cot_all, q, k, v, attended, wq, wkv, wo, cosine, sine, parts,
+    *scratch,
+):
+    p = Place(line)
+    count = 2 * line
+    rank = lax.axis_index("grp")
+    g1, g2 = scratch[:3], scratch[3:6]
+    (load_sem, small_send, small_recv, wy_send, wg_send, w_recv, save_sem) = scratch[6:13]
+    r_scratch = scratch[13:]
+    half = wk_hbm.shape[0]
+    piece = half // 2
+    at_own = pl.ds(pl.multiple_of(p.y * half, half), half)
+    loads = [
+        pltpu.make_async_copy(src, dst, load_sem.at[i])
+        for i, (src, dst) in enumerate(
+            (
+                (wk_hbm, wkv.at[0, at_own]),
+                (wv_hbm, wkv.at[1, at_own]),
+                (wq_hbm, wq),
+                (wo_hbm, wo),
+            )
+        )
+    ]
+    start_all(loads)
+    p.greet(groups)
+
+    def small_copy(step, peer, origin):
+        return to_peer(
+            "shard", peer, small, small_out.at[origin], small_send.at[step], small_recv.at[step]
+        )
+
+    for step in range(1, count):
+        small_copy(step, lax.rem(p.me + step, count), p.me).start()
+    gather = Gather(p, split, own, rows_all, *g1)
+    gather.start()
+    small_out[p.me] = small[...]
+
+    def rows_of(quarter, column):
+        return wkv.at[
+            quarter // 2,
+            pl.ds(pl.multiple_of(column * half + lax.rem(quarter, 2) * piece, piece), piece),
+        ]
+
+    def across():
+        ref = rows_of(rank, p.y)
+        return to_peer("shard", p.cross, ref, ref, wy_send, w_recv.at[rank])
+
+    def share(step):
+        ref = rows_of(rank, 1 - p.y)
+        return to_peer(
+            "grp", lax.rem(rank + step, groups), ref, ref, wg_send.at[step], w_recv.at[rank]
+        )
+
+    wait_all(loads)
+    across().start()
+    pos = lax.broadcasted_iota(jnp.int32, cosine.shape, 0).astype(F32)
+    angle = pos * freq[...]
+    cosine[...] = jnp.cos(angle)
+    sine[...] = jnp.sin(angle)
+    for step in range(1, count):
+        small_copy(step, p.me, lax.rem(p.me + count - step, count)).wait_recv()
+    gain = jnp.concatenate([small_out[s, 0:1] for s in range(count)], 1).astype(F32)
+    across().wait_recv()
+    for step in range(1, groups):
+        share(step).start()
+    rows = own.shape[0]
+    pair = 2 * rows
+    slots = rows // seqs
+    low = own.dtype
+    for step in range(1, groups):
+        quarter = lax.rem(rank + step, groups)
+        ref = rows_of(quarter, 1 - p.y)
+        to_peer("grp", rank, ref, ref, wg_send.at[step], w_recv.at[quarter]).wait_recv()
+
+    @pl.loop(0, line)
+    def _(i):
+        gather.hop(i + 1)
+        d = p.near(i)
+        gather.whole(d)
+        x = rows_all[pl.ds(2 * d, 2)].reshape(pair, -1).astype(F32)
+        n = (
+            x * lax.rsqrt(jnp.mean(x * x, -1, keepdims=True) + EPSILON) * gain
+        ).astype(low)
+        normed[pl.ds(2 * d, 2)] = n.reshape(2, rows, -1)
+        at = pl.ds(pl.multiple_of(d * 2 * slots, 2 * slots), 2 * slots)
+        c, s = cosine[at], sine[at]
+
+        def by_rows(t):
+            return jnp.concatenate([t[:slots]] * seqs + [t[slots:]] * seqs, 0)
+
+        c, s = by_rows(c), by_rows(s)
+
+        def put(target, value):
+            for block in range(2):
+                for m in range(seqs):
+                    to = pl.ds(
+                        pl.multiple_of(d * 2 * slots + block * slots, slots), slots
+                    )
+                    target[m, to] = value[block * rows + m * slots : block * rows + (m + 1) * slots]
+
+        put(q, turn_by(dot_t(n, wq[...]), c, s).astype(low))
+        put(k, turn_by(dot_t(n, wkv[0]), c, s).astype(low))
+        put(v, dot_t(n, wkv[1]).astype(low))
+
+    saves = [
+        pltpu.make_async_copy(src, dst, save_sem.at[i])
+        for i, (src, dst) in enumerate(
+            (
+                (normed, normed_hbm),
+                (q, q_hbm),
+                (k, k_hbm),
+                (v, v_hbm),
+                (wkv, wkv_hbm),
+                (cosine, cos_hbm),
+                (sine, sin_hbm),
+            )
+        )
+    ]
+    start_all(saves)
+    cots = Gather(p, split, cot_own, cot_all, *g2)
+    cots.start()
+    total_slots = q.shape[1]
+    tile = min(256, total_slots)
+
+    @pl.loop(0, seqs)
+    def _(n):
+        for t in range(total_slots // tile):
+            span = (t + 1) * tile
+            at = pl.ds(t * tile, tile)
+            probs = probabilities(q[n, at], k[n, pl.ds(0, span)], t * tile, bias[n][:, :span])
+            out = dot(probs.astype(low), v[n, pl.ds(0, span)]).astype(low)
+            for c in range(tile // slots):
+                b = (t * tile) // slots + c
+                attended[pl.ds(pl.multiple_of(b * rows + n * slots, slots), slots)] = out[
+                    c * slots : (c + 1) * slots
+                ]
+        cots.hop(n + 1)
+
+    for h in range(seqs + 1, line):
+        cots.hop(h)
+
+    @pl.loop(0, line)
+    def _(d):
+        at = pl.ds(pl.multiple_of(d * pair, pair), pair)
+        parts[pl.ds(2 * d, 2)] = dot(attended[at], wo[...]).astype(low).reshape(2, rows, -1)
+
+    reduce = Reduce(p, split, parts, branch, r_scratch)
+    for i in range(DEPTH):
+        reduce.send_across(i)
+    saves2 = [pltpu.make_async_copy(attended, attended_hbm, save_sem.at[7])]
+    start_all(saves2)
+    for d in range(line):
+        cots.whole(d)
+    saves3 = [pltpu.make_async_copy(cot_all, cot_hbm, save_sem.at[8])]
+    start_all(saves3)
+    for i in range(line - 1):
+        reduce.b_hop(i)
+    for i in range(line - 1):
+        reduce.hop(i)
+        if i + DEPTH < line:
+            reduce.send_across(i + DEPTH)
+    reduce.finish()
+    reduce.drain()
+    gather.drain()
+    cots.drain()
+    wait_all(saves + saves2 + saves3)
+    across().wait_send()
+    for step in range(1, groups):
+        share(step).wait_send()
+    for step in range(1, count):
+        small_copy(step, lax.rem(p.me + step, count), p.me).wait_send()
+
+
+def attention(own, cot, small, bias, freq, wq, wk, wv, wo, count, groups, ident, split=112):
+    rows, width = own.shape
+    seqs, _, total_slots = bias.shape
+    line = count // 2
+    low = own.dtype
+    v = pltpu.VMEM
+    shape = jax.ShapeDtypeStruct
+    hd = wq.shape[0]
+    big = (count, rows, width)
+    head = (seqs, total_slots, hd)
+    table = (total_slots, hd // 2)
+    flat = (count * rows, hd)
+    return pl.pallas_call(
+        functools.partial(attention_kernel, line, split, groups, seqs),
+        out_shape=(
+            shape((rows, width), F32),
+            shape((count,) + small.shape, small.dtype),
+            shape(big, low),
+            shape(big, low),
+            shape(head, low),
+            shape(head, low),
+            shape(head, low),
+            shape(flat, low),
+            shape((2, hd, width), low),
+            shape(table, F32),
+            shape(table, F32),
+        ),
+        in_specs=[vm()] * 5 + [hbm()] * 4,
+        out_specs=(vm(), vm()) + (hbm(),) * 9,
+        scratch_shapes=[
+            v(big, low), v(big, low), v(big, low), v(head, low), v(head, low), v(head, low), v(flat, low),
+            v((hd, width), low), v((2, hd, width), low), v((hd, width), low), v(table, F32), v(table, F32), v(big, low),
+        ]
+        + gather_sems(count) * 2
+        + [DMA((4,)), DMA((count,)), DMA((count,)), DMA, DMA((groups,)), DMA((groups,)), DMA((9,))]
+        + Reduce.scratch(line, rows, split, width, low),
+        compiler_params=params(ident),
+        name="attention",
+    )(own, cot, small, bias, freq, wq, wk, wv, wo)
+
+
+def ffn_kernel(
+    line, split, groups,
+    own, cot_hbm, gate_hbm, up_hbm, down_hbm,
+    second, ffn_hbm, pair_hbm, total_hbm,
+    normed, cot, gate_w, up_w, down_w, hidden, gate_g, up_g, parts, stage, theirs, chip_in,
+    *scratch,
+):
+    p = Place(line)
+    rank = lax.axis_index("grp")
+    core = lax.rem(rank, 2)
+    partner = rank + 1 - 2 * core
+    opposite = lax.rem(rank + 2, groups)
+    (load_sem, out_sem, stage_send, stage_recv, chip_send, chip_recv, back_send, back_recv) = scratch[3:11]
+    loads = [
+        pltpu.make_async_copy(src, dst, load_sem.at[i])
+        for i, (src, dst) in enumerate(
+            ((gate_hbm, gate_w), (up_hbm, up_w), (cot_hbm, cot), (down_hbm, down_w))
+        )
+    ]
+    start_all(loads)
+    p.greet(groups)
+    gather = Gather(p, split, own, normed, *scratch[:3])
+    gather.start()
+    wait_all(loads)
+    rows = own.shape[0]
+    pair = 2 * rows
+    low = own.dtype
+
+    @pl.loop(0, line)
+    def _(i):
+        gather.hop(i + 1)
+        d = p.near(i)
+        gather.whole(d)
+        x = normed[pl.ds(2 * d, 2)].reshape(pair, -1)
+        g = dot_t(x, gate_w[...])
+        u = dot_t(x, up_w[...])
+        dh = dot_t(cot[pl.ds(2 * d, 2)].reshape(pair, -1), down_w[...])
+        s = 1.0 / (1.0 + jnp.exp(-g))
+        silu = g * s
+        at = pl.ds(pl.multiple_of(d * pair, pair), pair)
+        hidden[at] = (silu * u).astype(low)
+        up_g[at] = (dh * silu).astype(low)
+        gate_g[at] = (dh * u * s * (1.0 + g * (1.0 - s))).astype(low)
+        part = dot(gate_g[at], gate_w[...]) + dot(up_g[at], up_w[...])
+        parts[pl.ds(2 * d, 2)] = part.astype(low).reshape(2, rows, -1)
+
+    reduce = Reduce(p, split, parts, second, scratch[11:])
+    for i in range(DEPTH):
+        reduce.send_across(i)
+    for i in range(line - 1):
+        reduce.b_hop(i)
+
+    units = hidden.shape[1]
+    quarter = units // 4
+    half = units // 2
+    mine = (up_w.at[pl.ds(0, half)], gate_w.at[pl.ds(0, half)], gate_w.at[pl.ds(half, half)])
+
+    def to_partner(which, j):
+        return to_peer(
+            "grp",
+            partner,
+            stage.at[j],
+            theirs.at[which, pl.ds(j * quarter, quarter)],
+            stage_send.at[j],
+            stage_recv.at[which, j],
+        )
+
+    def gradient(which, left, right):
+        def block(q):
+            cols = pl.ds(pl.multiple_of(q * quarter, quarter), quarter)
+            return t_dot(left[:, cols], right[...].reshape(left.shape[0], -1)).astype(low)
+
+        @pl.loop(0, 2)
+        def _(j):
+            if which:
+                to_partner(which - 1, j).wait_send()
+            stage[j] = block(2 * (1 - core) + j)
+            to_partner(which, j).start()
+
+        @pl.loop(0, 2)
+        def _(j):
+            at = pl.ds(pl.multiple_of(j * quarter, quarter), quarter)
+            mine[which][at] = block(2 * core + j)
+
+    def add_theirs(which):
+        for j in range(2):
+            to_partner(which, j).wait_recv()
+        total_into(mine[which], mine[which], theirs.at[which])
+
+    def chip_copy():
+        return to_peer("grp", opposite, mine[0], chip_in, chip_send, chip_recv)
+
+    def save_pair(which):
+        return pltpu.make_async_copy(mine[which], pair_hbm.at[which - 1], out_sem.at[which])
+
+    gradient(0, hidden, cot)
+    reduce.hop(0)
+    reduce.send_across(DEPTH)
+    add_theirs(0)
+    chip_copy().start()
+    gradient(1, gate_g, normed)
+    reduce.hop(1)
+    reduce.send_across(DEPTH + 1)
+    add_theirs(1)
+    save_pair(1).start()
+    gradient(2, up_g, normed)
+    reduce.hop(2)
+    gather.drain()
+
+    @pl.loop(0, line)
+    def _(d):
+        at = pl.ds(pl.multiple_of(d * pair, pair), pair)
+        normed[pl.ds(2 * d, 2)] = dot(hidden[at], down_w[...]).astype(low).reshape(2, rows, -1)
+
+    ffn_save = pltpu.make_async_copy(normed, ffn_hbm, out_sem.at[0])
+    ffn_save.start()
+    add_theirs(2)
+    save_pair(2).start()
+    reduce.finish()
+    for j in range(2):
+        to_partner(2, j).wait_send()
+
+    at = pl.ds(pl.multiple_of(core * half, half), half)
+    keep = pltpu.make_async_copy(chip_in, total_hbm.at[at], out_sem.at[3])
+    give = to_peer("grp", partner, chip_in, total_hbm.at[at], back_send, back_recv)
+    chip_copy().wait_recv()
+    total_into(chip_in, mine[0], chip_in)
+    keep.start()
+    give.start()
+    reduce.drain()
+    chip_copy().wait_send()
+    ffn_save.wait()
+    for which in (1, 2):
+        save_pair(which).wait()
+    keep.wait()
+    give.wait()
+
+
+def ffn(own, cot, gate_w, up_w, down_w, groups, ident, split=112):
+    rows, width = own.shape
+    count = cot.shape[0]
+    line = count // 2
+    units = gate_w.shape[0]
+    low = own.dtype
+    v = pltpu.VMEM
+    tokens = count * rows
+    shape = jax.ShapeDtypeStruct
+    big = (count, rows, width)
+    half = (units // 2, width)
+    return pl.pallas_call(
+        functools.partial(ffn_kernel, line, split, groups),
+        out_shape=(
+            shape((rows, width), F32),
+            shape(big, low),
+            shape((2,) + half, low),
+            shape((units, width), low),
+        ),
+        in_specs=[vm()] + [hbm()] * 4,
+        out_specs=(vm(), hbm(), hbm(), hbm()),
+        scratch_shapes=[v(big, low)] * 2
+        + [v((units, width), low)] * 3
+        + [v((tokens, units), low)] * 3
+        + [v(big, low), v((2, units // 4, width), low), v((3,) + half, low), v(half, low)]
+        + gather_sems(count)
+        + [DMA((4,)), DMA((4,)), DMA((2,)), DMA((3, 2)), DMA, DMA, DMA, DMA]
+        + Reduce.scratch(line, rows, split, width, low),
+        compiler_params=params(ident),
+        name="ffn",
+    )(own, cot, gate_w, up_w, down_w)
+
+
+def attention_grad_kernel(
+    line, split, groups, seqs,
+    own, bias, cosine, sine, gain, gain_parts,
+    ffn_hbm, normed_hbm, attended_hbm, q_hbm, k_hbm, v_hbm, wq_hbm, wkv_hbm, wo_hbm, sums_hbm,
+    first, ffn_own, gain_out, total_hbm, attn_hbm,
+    dbranch, normed, attended, q, k, v, wq, wkv, wo, da, dk_acc, dv_acc, dq_rows, dk_rows, dv_rows,
+    halves, half_in, ffn_parts, parts, sums, sums_in, stage, mine, theirs, mine_in, gain_held, gain_in, gain_sum, gain_all,
+    *scratch,
+):
+    p = Place(line)
+    count = 2 * line
+    rank = lax.axis_index("grp")
+    core = lax.rem(rank, 2)
+    partner = rank + 1 - 2 * core
+    opposite = lax.rem(rank + 2, groups)
+    (
+        load_sem, chip_send, chip_recv, half_send, half_recv, stage_send, stage_recv,
+        back_send, back_recv, keep_sem, ga_send, ga_recv, gb_send, gb_recv,
+    ) = scratch[3:17]
+    n = Reduce.N_SCRATCH
+    loads = [
+        pltpu.make_async_copy(src, dst, load_sem.at[i])
+        for i, (src, dst) in enumerate(
+            (
+                (wo_hbm, wo),
+                (ffn_hbm, ffn_parts),
+                (attended_hbm, attended),
+                (q_hbm, q),
+                (k_hbm, k),
+                (v_hbm, v),
+                (wq_hbm, wq),
+                (wkv_hbm, wkv),
+                (normed_hbm, normed),
+                (sums_hbm, sums),
+            )
+        )
+    ]
+    start_all(loads)
+    p.greet(groups)
+    gather = Gather(p, split, own, dbranch, *scratch[:3])
+    n_sums = sums_hbm.shape[0]
+    part_rows = sums.shape[1]
+
+    def chip_copy(i):
+        return to_peer(
+            "grp", opposite, sums_hbm.at[i], sums_in.at[i], chip_send.at[i], chip_recv.at[i]
+        )
+
+    for i in range(n_sums):
+        chip_copy(i).start()
+    gather.start()
+    wait_all(loads)
+    rows = own.shape[0]
+    pair = 2 * rows
+    slots = rows // seqs
+    low = own.dtype
+    scale = 1.0 / math.sqrt(HD)
+
+    @pl.loop(0, line)
+    def _(i):
+        gather.hop(i + 1)
+        d = p.near(i)
+        gather.whole(d)
+        grad = dot_t(dbranch[pl.ds(2 * d, 2)].reshape(pair, -1), wo[...]).astype(low)
+        for block in range(2):
+            for m in range(seqs):
+                at = pl.ds(pl.multiple_of(d * 2 * slots + block * slots, slots), slots)
+                da[m, at] = grad[block * rows + m * slots : block * rows + (m + 1) * slots]
+
+    ffn_sum = Reduce(p, split, ffn_parts, ffn_own, scratch[17 : 17 + n])
+    for i in range(DEPTH):
+        ffn_sum.send_across(i)
+    for i in range(line - 1):
+        ffn_sum.b_hop(i)
+
+    chunk = stage.shape[1]
+
+    def to_partner(b):
+        return to_peer(
+            "grp",
+            partner,
+            stage.at[b % 3],
+            theirs.at[pl.ds((b % 3) * chunk, chunk)],
+            stage_send.at[b % 3],
+            stage_recv.at[b % 3],
+        )
+
+    def gradient(b, left, right):
+        value = t_dot(left, right[...].reshape(left.shape[0], -1)).astype(low)
+        keep = core == b // 3
+
+        @pl.when(keep)
+        def _():
+            mine[pl.ds((b % 3) * chunk, chunk)] = value
+
+        @pl.when(jnp.logical_not(keep))
+        def _():
+            stage[b % 3] = value
+            to_partner(b).start()
+
+    total_slots = q.shape[1]
+    tile = min(256, total_slots)
+
+    def backward(m):
+        dk_acc[...] = jnp.zeros_like(dk_acc)
+        dv_acc[...] = jnp.zeros_like(dv_acc)
+
+        def to_rows(target, value, start, size):
+            for c in range(size // slots):
+                b = start // slots + c
+                target[pl.ds(pl.multiple_of(b * rows + m * slots, slots), slots)] = value[
+                    c * slots : (c + 1) * slots
+                ]
+
+        for t in range(total_slots // tile):
+            span = (t + 1) * tile
+            at = pl.ds(t * tile, tile)
+            query, grad = q[m, at], da[m, at]
+            keys, values = k[m, pl.ds(0, span)], v[m, pl.ds(0, span)]
+            probs = probabilities(query, keys, t * tile, bias[m][:, :span])
+            dprobs = dot_t(grad, values)
+            inner = jnp.sum(probs * dprobs, -1, keepdims=True)
+            dscores = (probs * (dprobs - inner)).astype(low)
+            dq = turn_back(dot(dscores, keys) * scale, cosine[at], sine[at])
+            to_rows(dq_rows, dq.astype(low), t * tile, tile)
+            dk_acc[pl.ds(0, span)] += t_dot(dscores, query)
+            dv_acc[pl.ds(0, span)] += t_dot(probs.astype(low), grad)
+        dk = turn_back(dk_acc[...] * scale, cosine[...], sine[...])
+        to_rows(dk_rows, dk.astype(low), 0, total_slots)
+        to_rows(dv_rows, dv_acc[...].astype(low), 0, total_slots)
+
+    half = HD // 2
+
+    def swap():
+        return to_peer("shard", p.cross, halves.at[1 - p.y], half_in, half_send, half_recv)
+
+    gradient(0, attended[:, :chunk], dbranch)
+    gradient(1, attended[:, chunk:], dbranch)
+
+    @pl.loop(0, seqs)
+    def _(m):
+        backward(m)
+        ffn_sum.hop(m)
+        ffn_sum.send_across(m + DEPTH)
+
+    for h in range(2):
+        halves[h, 0] = dk_rows[:, h * half : (h + 1) * half]
+        halves[h, 1] = dv_rows[:, h * half : (h + 1) * half]
+    swap().start()
+    gradient(2, dq_rows[:, :chunk], normed)
+    gradient(3, dq_rows[:, chunk:], normed)
+
+    @pl.loop(0, line)
+    def _(d):
+        at = pl.ds(pl.multiple_of(d * pair, pair), pair)
+        part = dot(dq_rows[at], wq[...]) + dot(dk_rows[at], wkv[0]) + dot(dv_rows[at], wkv[1])
+        parts[pl.ds(2 * d, 2)] = part.astype(low).reshape(2, rows, -1)
+
+    for i in range(seqs, line - 1):
+        ffn_sum.hop(i)
+    reduce = Reduce(p, split, parts, first, scratch[17 + n :])
+    for i in range(DEPTH):
+        reduce.send_across(i)
+    swap().wait_recv()
+
+    def summed(which):
+        return (halves[p.y, which].astype(F32) + half_in[which].astype(F32)).astype(low)
+
+    gradient(4, summed(0), normed)
+    gradient(5, summed(1), normed)
+
+    def attn_chip():
+        return to_peer(
+            "grp", opposite, mine, mine_in, chip_send.at[n_sums], chip_recv.at[n_sums]
+        )
+
+    for b in range(3):
+        to_partner(b).wait_recv()
+    total_into(mine, mine, theirs)
+    attn_chip().start()
+    ffn_sum.finish()
+    for i in range(line - 1):
+        reduce.b_hop(i)
+
+    def back(i):
+        if i < n_sums:
+            whole, size, out = sums.at[i], part_rows, total_hbm.at[i]
+        else:
+            whole, size, out = mine, 3 * chunk, attn_hbm
+        at = pl.ds(pl.multiple_of(core * size, size), size)
+        return (
+            pltpu.make_async_copy(whole, out.at[at], keep_sem.at[i]),
+            to_peer("grp", partner, whole, out.at[at], back_send.at[i], back_recv.at[i]),
+        )
+
+    def sum_up(i):
+        chip_copy(i).wait()
+        total_into(sums.at[i], sums.at[i], sums_in.at[i])
+        start_all(back(i))
+
+    def gain_copy(step, peer, origin):
+        return to_peer(
+            "shard", peer, gain_held.at[peer], gain_in.at[origin], ga_send.at[step], ga_recv.at[step]
+        )
+
+    def gain_group(step, peer, origin):
+        return to_peer(
+            "grp", peer, gain_sum, gain_all.at[origin], gb_send.at[step], gb_recv.at[step]
+        )
+
+    def gain_first():
+        def body(i, total):
+            at = pl.ds(pl.multiple_of(i * 16, 16), 16)
+            for b in range(count):
+                total = total + parts[b, at].astype(F32) * normed[b, at].astype(F32)
+            return total
+
+        total = lax.fori_loop(0, rows // 16, body, jnp.zeros((16, parts.shape[2]), F32))
+        total = jnp.sum(total, 0, keepdims=True) / gain[...]
+        share = gain_held.shape[2]
+        for b in range(count):
+            gain_held[b] = gain_parts[b]
+            gain_held[b, 0:1] = total[:, b * share : (b + 1) * share]
+        for step in range(1, count):
+            gain_copy(step, lax.rem(p.me + step, count), p.me).start()
+
+    def gain_second():
+        for step in range(1, count):
+            gain_copy(step, p.me, lax.rem(p.me + count - step, count)).wait_recv()
+        gain_in[p.me] = gain_held[p.me]
+        total = gain_in[0]
+        for b in range(1, count):
+            total = total + gain_in[b]
+        gain_sum[...] = total
+        gain_all[rank] = total
+        for step in range(1, groups):
+            gain_group(step, lax.rem(rank + step, groups), rank).start()
+
+    reduce.hop(0)
+    reduce.send_across(DEPTH)
+    gain_first()
+    sum_up(0)
+    reduce.hop(1)
+    reduce.send_across(DEPTH + 1)
+    gain_second()
+    reduce.hop(2)
+    for i in range(1, n_sums):
+        sum_up(i)
+    reduce.finish()
+    for step in range(1, groups):
+        gain_group(step, rank, lax.rem(rank + groups - step, groups)).wait_recv()
+    total = gain_all[0]
+    for b in range(1, groups):
+        total = total + gain_all[b]
+    gain_out[...] = total
+    attn_chip().wait()
+    total_into(mine, mine, mine_in)
+    start_all(back(n_sums))
+    reduce.drain()
+    ffn_sum.drain()
+    gather.drain()
+    swap().wait_send()
+    for b in range(3):
+        to_partner(b).wait_send()
+    for step in range(1, count):
+        gain_copy(step, lax.rem(p.me + step, count), p.me).wait_send()
+    for step in range(1, groups):
+        gain_group(step, lax.rem(rank + step, groups), rank).wait_send()
+    for i in range(n_sums + 1):
+        wait_all(back(i))
+
+
+def attention_grad(
+    own, bias, cosine, sine, gain, gain_parts, ffn_parts, normed, attended, q, k, v, wq, wkv, wo, sums,
+    groups, ident, split=112,
+):
+    rows, width = own.shape
+    count = normed.shape[0]
+    line = count // 2
+    seqs, total_slots, hd = q.shape
+    low = own.dtype
+    vmem = pltpu.VMEM
+    tokens = count * rows
+    half = hd // 2
+    n_sums, part_rows, _ = sums.shape
+    shape = jax.ShapeDtypeStruct
+    big = vmem((count, rows, width), low)
+    head = vmem((seqs, total_slots, hd), low)
+    weight = vmem((hd, width), low)
+    flat = vmem((tokens, hd), low)
+    acc = vmem((total_slots, hd), F32)
+    third = vmem((3 * half, width), low)
+    g = gain_parts.shape
+    return pl.pallas_call(
+        functools.partial(attention_grad_kernel, line, split, groups, seqs),
+        out_shape=(
+            shape((rows, width), F32),
+            shape((rows, width), F32),
+            shape(g[1:], F32),
+            shape((n_sums, 2 * part_rows, width), low),
+            shape((6 * half, width), low),
+        ),
+        in_specs=[vm()] * 6 + [hbm()] * 10,
+        out_specs=(vm(), vm(), vm(), hbm(), hbm()),
+        scratch_shapes=[
+            big, big, flat, head, head, head, weight, vmem((2, hd, width), low), weight, head, acc, acc,
+            flat, flat, flat,
+            vmem((2, 2, tokens, half), low), vmem((2, tokens, half), low), big, big,
+            vmem(sums.shape, low), vmem(sums.shape, low), vmem((3, half, width), low), third, third, third,
+            vmem(g, F32), vmem(g, F32), vmem(g[1:], F32), vmem((groups,) + g[1:], F32),
+        ]
+        + gather_sems(count)
+        + [
+            DMA((10,)), DMA((n_sums + 1,)), DMA((n_sums + 1,)), DMA, DMA, DMA((3,)), DMA((3,)),
+            DMA((n_sums + 1,)), DMA((n_sums + 1,)), DMA((n_sums + 1,)),
+            DMA((count,)), DMA((count,)), DMA((groups,)), DMA((groups,)),
+        ]
+        + Reduce.scratch(line, rows, split, width, low) * 2,
+        compiler_params=params(ident),
+        name="attention_grad",
+    )(own, bias, cosine, sine, gain, gain_parts, ffn_parts, normed, attended, q, k, v, wq, wkv, wo, sums)
 
 
 epsilon = 1e-06
@@ -79,7 +1180,7 @@
     return (weight_term, shard_rows)
 
 
-def local(
+def local_rows(
     tokens,
     lengths,
     prenorm_gain,
@@ -324,7 +1425,122 @@
     )
 
 
+def local_heads(
+    tokens,
+    lengths,
+    prenorm_gain,
+    query_weight,
+    key_weight,
+    value_weight,
+    out_weight,
+    midnorm_gain,
+    gate_weight,
+    up_weight,
+    down_weight,
+    cotangent,
+):
+    low = jnp.bfloat16
+    count = lax.axis_size("shard")
+    groups = lax.axis_size("grp")
+    shard_rank = lax.axis_index("shard")
+    seqs, seq_dev, model_width = tokens.shape
+    rows = seqs * seq_dev
+    key_pos = jnp.arange(seq_dev * count, dtype=jnp.int32)
+    local_pos = shard_rank * seq_dev + jnp.arange(seq_dev, dtype=jnp.int32)
+    valid_rows = (local_pos[None, :] < lengths[:, None]).reshape(rows, 1)
+    bias = jnp.where(key_pos[None, None, :] < lengths[:, None, None], 0.0, -1.0)
+    inverse_freq = theta_base ** (-(jnp.arange(0, HD, 2).astype(jnp.float32) / HD))
+    cot_low = jnp.where(valid_rows, cotangent.reshape(rows, model_width), jnp.zeros((), low))
+    share = prenorm_gain.shape[0]
+    own_gains = jnp.broadcast_to(
+        jnp.stack([prenorm_gain, midnorm_gain])[:, None, :], (2, 8, share)
+    ).reshape(16, share)
+    tokens_low = tokens.reshape(rows, model_width)
+    branch, gains, normed_first, cot_all, queries, keys, values, attended, kv_head, cosine, sine = (
+        attention(
+            tokens_low,
+            cot_low,
+            own_gains,
+            bias,
+            inverse_freq[None, :],
+            query_weight,
+            key_weight,
+            value_weight,
+            out_weight,
+            count,
+            groups,
+            1,
+        )
+    )
+    gains = gains.astype(jnp.float32)
+    prenorm_f = gains[:, 0].reshape(-1)
+    midnorm_f = gains[:, 8].reshape(-1)
+    source = tokens_low.astype(jnp.float32)
+    middle = source + branch
+    scaled_second, inverse_second = norm_forward(middle, midnorm_f)
+    second_grad, ffn_parts, pair_sums, down_total = ffn(
+        scaled_second.astype(low), cot_all, gate_weight, up_weight, down_weight, groups, 2
+    )
+    middle_part, midnorm_part = norm_backward(middle, inverse_second, midnorm_f, second_grad)
+    middle_grad = cot_low.astype(jnp.float32) + middle_part
+    gain_parts = jnp.concatenate(
+        [
+            jnp.zeros((count, 1, share), jnp.float32),
+            midnorm_part.reshape(count, 1, share),
+            jnp.zeros((count, 6, share), jnp.float32),
+        ],
+        1,
+    )
+    first_grad, ffn_part, gain_own, totals, attn_total = attention_grad(
+        middle_grad.astype(low),
+        bias,
+        cosine,
+        sine,
+        prenorm_f[None, :],
+        gain_parts,
+        ffn_parts,
+        normed_first,
+        attended,
+        queries,
+        keys,
+        values,
+        query_weight,
+        kv_head,
+        out_weight,
+        pair_sums,
+        groups,
+        3,
+    )
+    mixed = jnp.where(valid_rows, middle + ffn_part, 0.0).astype(low)
+    inverse_first = lax.rsqrt(jnp.mean(source * source, -1, keepdims=True) + epsilon)
+    weighted = first_grad * prenorm_f
+    inner_sum = jnp.sum(weighted * source, -1, keepdims=True)
+    input_gradient = (
+        middle_grad
+        + inverse_first * weighted
+        - source * inverse_first * inverse_first * inverse_first * inner_sum / model_width
+    ).astype(low)
+    head = query_weight.shape[0]
+    kv_share = key_weight.shape[0]
+    f32 = jnp.float32
+    return (
+        mixed.reshape(tokens.shape),
+        input_gradient.reshape(tokens.shape),
+        gain_own[0],
+        attn_total[head : 2 * head].astype(f32),
+        attn_total[2 * head : 2 * head + kv_share].astype(f32),
+        attn_total[2 * head + kv_share :].astype(f32),
+        attn_total[:head].astype(f32),
+        gain_own[1],
+        totals[0].astype(f32),
+        totals[1].astype(f32),
+        down_total.astype(f32),
+    )
+
+
 def solution(mesh):
+    planes = mesh.shape["shard"] == NH and mesh.shape["grp"] == 4
+    local = local_heads if planes else local_rows
     in_specs = (
         P("grp", "shard", None),
         P("grp"),

time: 2350 us -> 504 us (0.21)
  waiting for transfers between devices: 1890 us -> 0 us
  Pallas kernels: 0 us -> 459 us
  matrix products: 213 us -> 0 us
  blocking collectives: 81.7 us -> 0 us
  other arithmetic: 99.2 us -> 38.6 us
  local copies, waits for them, and re-layouts: 45.9 us -> 4.97 us
    reduce_scatter x8 -> x0, waiting for transfers between devices: 1110 us -> none  [the longest x2 742 us: local(): lax.psum_scatter(weight_term(jnp.int32(0), lax.axis_size('shard') * shard...]
    all_gather x10 -> x0, waiting for transfers between devices: 575 us -> none  [the longest x1 121 us: local(): lax.all_gather(query_weight, 'shard', axis=0, tiled=True)]
    pallas_call x0 -> x3, Pallas kernels: none -> 459 us  [the longest x1 184 us: attention_grad(): pl.pallas_call(functools.partial(attention_grad_kernel, line, split, grou...]
    dot_general x54 -> x0, matrix products: 213 us -> none  [the longest x2 15.8 us: local(): jnp.einsum('sf,sd->fd', gate_grad, normed_all, preferred_element_type=jnp...]
    psum x1 -> x0, waiting for transfers between devices: 201 us -> none  [local(): lax.psum(attn_total.astype(jnp.bfloat16), 'grp').astype(jnp.float32)]
    concatenate x7 -> x1, other arithmetic: 42.7 us -> 0.71 us  [local_heads(): jnp.concatenate([jnp.zeros((count, 1, share), jnp.float32), midnorm_part....]
    psum x1 -> x0, blocking collectives: 41.1 us -> none  [local(): gain_sums = lax.psum((prenorm_total, midnorm_total), ('grp', 'shard'))]
    all_gather x2 -> x0, blocking collectives: 40.7 us -> none  [the longest x1 22.4 us: local(): lax.all_gather(prenorm_gain, 'shard', axis=0, tiled=True)]
  transfers between devices with their start and end apart: 19 -> 0, of which waited for: 19 -> 0; matrix products, arithmetic and copies ran while one was open for 12% -> 0% of each run, Pallas kernels for 0% -> 0%
where the time goes in v4:
time: 504 us; the launch traced here: 503 us
  Pallas kernels  459 us (91%)
  other arithmetic  38.6 us (8%)
    pallas_call x1, Pallas kernels, attention_grad(): pl.pallas_call(functools.partial(attention_grad_kernel, line, split, grou...  184 us
    pallas_call x1, Pallas kernels, attention(): pl.pallas_call(functools.partial(attention_kernel, line, split, groups, s...  151 us
    pallas_call x1, Pallas kernels, ffn(): pl.pallas_call(functools.partial(ffn_kernel, line, split, groups), out_sh...  124 us
    convert_element_type x1, other arithmetic, local_heads(): totals[1].astype(f32)  11.9 us

profile of v4, /device:TPU:0, one launch (start us, length us, event | category | flops | bytes accessed | tf_op | source)
XLA Modules:
  0.0 503.2 jit_solution(9715050093527612458)
XLA Ops:
  0.7 0.8 broadcast_compare_fusion
  1.5 1.9 bitcast_select_fusion.cot_own
  3.5 0.7 stack.10
  4.1 0.7 stack.9
  4.8 0.6 broadcast_bitcast_fusion.small
  5.4 1.3 compare_select_fusion.bias
  6.7 0.5 negate_power_fusion.freq
  7.3 151.4 %attention.1 = (f32[128,2048]{1,0:T(8,128)}, bf16[8,16,256]{2,1,0:T(8,128)(2,1)}, bf16[8,128,2048]{2,1,0:T(8,128)(2,1)}, bf16[8,128,2048]{2,1,0:T(8,128)(2,1)}, ...) custom-call(bf16[128,2048]{1,0:T(8,128)(2,1)} %bitcast.26, ...), custom_call_target="tpu_custom_call" | custom-call | tf_op jit(solution)/shard_map/attention/pallas_call | solution.py:591
  158.7 1.4 multiply_reduce_fusion.3
  160.2 1.4 fusion.8
  161.6 1.0 multiply_convert_fusion.own
  162.6 123.7 %ffn.1 = (f32[128,2048]{1,0:T(8,128)}, bf16[8,128,2048]{2,1,0:T(8,128)(2,1)}, bf16[2,512,2048]{2,1,0:T(8,128)(2,1)}, bf16[1024,2048]{1,0:T(8,128)(2,1)}) custom-call(bf16[128,2048]{1,0:T(8,128)(2,1)} %multiply_convert_fusion.own, bf16[8,128,2048]{2,1,0:T(8,128)(2,1)} %get-tuple-element.33.cot_hbm, bf16[1024,2048]{1,0:T(8,128)(2,1)} %gate_hbm.1, ...), custom_call_target="tpu_custom_call" | custom-call | tf_op jit(solution)/shard_map/ffn/pallas_call | solution.py:769
  286.3 1.8 multiply_reduce_fusion.1
  288.1 3.3 fusion.7
  291.5 0.7 maximum_maximum_fusion.gain_parts
  292.2 183.8 %attention_grad.1 = (f32[128,2048]{1,0:T(8,128)}, f32[128,2048]{1,0:T(8,128)}, f32[8,256]{1,0:T(8,128)}, bf16[2,1024,2048]{2,1,0:T(8,128)(2,1)}, bf16[768,2048]{1,0:T(8,128)(2,1)}) custom-call(bf16[128,2048]{1,0:T(8,128)(2,1)} %get-tuple-element.53.own, f32[2,1,512]{2,1,0:T(1,128)} %compare_select_fusion.bias, f32[512,128]{1,0:T(8,128)} %get-tuple-element.35.cosine, ...), custom_call_target="tpu_custom_call" | custom-call | tf_op jit(solution)/shard_map/attention_grad/pallas_call | solution.py:1084
  476.0 1.5 fusion.6
  477.4 0.2 multiply_reduce_fusion
  477.7 3.7 fusion.5
  481.4 1.3 fusion.9
  482.8 2.5 slice_convert_fusion
  485.3 1.6 slice_convert_fusion.2
  486.9 11.9 %bitcast_convert_fusion = (f32[1024,2048]{1,0:T(8,128)}, f32[1024,2048]{1,0:T(8,128)}) fusion(bf16[2,1024,2048]{2,1,0:T(8,128)(2,1)} %get-tuple-element.49), kind=kLoop, calls=%fused_computation | loop fusion | flops 4194304 | bytes 25165824 | tf_op jit(solution)/shard_map/convert_element_type | solution.py:1536
  498.8 4.4 convert_element_type.78
  (19 shorter events, 0.3 us)
Async XLA Ops:
  0.6 158.1 %copy-start.1 = (bf16[2,64,2048]{2,1,0:T(8,128)(2,1)S(1)}, bf16[2,64,2048]{2,1,0:T(8,128)(2,1)}, u32[]{:S(2)}) copy-start(bf16[2,64,2048]{2,1,0:T(8,128)(2,1)} %param.12) | copy-start | bytes 1572868
  160.2 1.4 copy-start
  292.2 183.8 %copy-start.4 = (f32[8,1,256]{2,1,0:T(1,128)S(1)}, f32[8,1,256]{2,1,0:T(1,128)}, u32[]{:S(2)}) copy-start(f32[8,1,256]{2,1,0:T(1,128)} %get-tuple-element.63) | copy-start | bytes 24580
  477.7 5.1 %copy-start.3 = (bf16[768,2048]{1,0:T(8,128)(2,1)S(1)}, bf16[768,2048]{1,0:T(8,128)(2,1)}, u32[]{:S(2)}) copy-start(bf16[768,2048]{1,0:T(8,128)(2,1)} %get-tuple-element.48) | copy-start | bytes 9437188
  486.9 11.9 %copy-start.2 = (bf16[1024,2048]{1,0:T(8,128)(2,1)S(1)}, bf16[1024,2048]{1,0:T(8,128)(2,1)}, u32[]{:S(2)}) copy-start(bf16[1024,2048]{1,0:T(8,128)(2,1)} %get-tuple-element.50) | copy-start | bytes 12582916

commit v5 on v4

--- a/solution.py
+++ b/solution.py
@@ -16,6 +16,17 @@
 DEPTH = 2
 MESH = pl.DeviceIdType.MESH
 F32 = jnp.float32
+DMA = pltpu.SemaphoreType.DMA
+REST = 16
+CHUNKS = 2
+
+
+def pieces(rows):
+    size = -(-(rows - REST) // (16 * CHUNKS)) * 16
+    cuts = [min(i * size, rows - REST) for i in range(CHUNKS + 1)] + [rows]
+    return [pl.ds(a, b - a) for a, b in zip(cuts, cuts[1:])]
+
+
 VMEM_LIMIT = 66_000_000
 
 
@@ -88,15 +99,16 @@
 class Gather:
     UP, DOWN, CROSS = 0, 1, 2
 
-    def __init__(self, place, split, own, out, local_sem, send_sem, recv_sem):
+    def __init__(self, place, own, out, local_sem, send_sem, recv_sem):
         self.p, self.own, self.out = place, own, out
         self.local_sem, self.send_sem, self.recv_sem = local_sem, send_sem, recv_sem
-        self.parts = (pl.ds(0, split), pl.ds(split, own.shape[0] - split))
+        self.pieces = pieces(own.shape[0])
+        self.last = len(self.pieces) - 1
 
     def copy(self, way, origin, part, own=False):
         p = self.p
         peer = (p.me + 2, p.me - 2, p.cross)[way]
-        at = self.parts[part]
+        at = self.pieces[part]
         return pltpu.make_async_remote_copy(
             src_ref=self.own.at[at] if own else self.out.at[origin, at],
             dst_ref=self.out.at[origin, at],
@@ -113,33 +125,40 @@
         p = self.p
         self.keep = pltpu.make_async_copy(self.own, self.out.at[p.me], self.local_sem)
         self.keep.start()
-        self.copy(self.CROSS, p.me, 1, True).start()
-        self.copy(self.CROSS, p.me, 0, True).start()
-        for part in (0, 1):
+        for part in (self.last,) + tuple(range(self.last)):
+            self.copy(self.CROSS, p.me, part, True).start()
+        for part in range(self.last + 1):
             either(p.z < p.line - 1, lambda: self.copy(self.UP, p.me, part, True).start())
             either(p.z > 0, lambda: self.copy(self.DOWN, p.me, part, True).start())
-        self.arrived(p.cross, 1)
-        either(p.z < p.line - 1, lambda: self.copy(self.UP, p.cross, 1).start())
-        either(p.z > 0, lambda: self.copy(self.DOWN, p.cross, 1).start())
+        self.arrived(p.cross, self.last)
+        either(p.z < p.line - 1, lambda: self.copy(self.UP, p.cross, self.last).start())
+        either(p.z > 0, lambda: self.copy(self.DOWN, p.cross, self.last).start())
         self.keep.wait()
 
     def hop(self, k):
         p = self.p
-
-        def take(origin, other, way, more):
-            self.arrived(origin, 0)
-            self.copy(self.CROSS, origin, 0).start()
-            either(more, lambda: self.copy(way, origin, 0).start())
+        below, above = p.me - 2 * k, p.me + 2 * k
+        has_below, has_above = p.z - k >= 0, p.z + k < p.line
+
+        def first(origin, part, way, more):
+            self.arrived(origin, part)
+            self.copy(self.CROSS, origin, part).start()
+            either(more, lambda: self.copy(way, origin, part).start())
+
+        def last(origin, other, way, more):
             for block in (origin, other):
-                self.arrived(block, 1)
-                either(more, lambda: self.copy(way, block, 1).start())
-
-        below, above = p.me - 2 * k, p.me + 2 * k
-        either(p.z - k >= 0, lambda: take(below, p.cross - 2 * k, self.UP, p.z < p.line - 1))
-        either(p.z + k < p.line, lambda: take(above, p.cross + 2 * k, self.DOWN, p.z > 0))
+                self.arrived(block, self.last)
+                either(more, lambda: self.copy(way, block, self.last).start())
+
+        for part in range(self.last):
+            either(has_below, lambda: first(below, part, self.UP, p.z < p.line - 1))
+            either(has_above, lambda: first(above, part, self.DOWN, p.z > 0))
+        either(has_below, lambda: last(below, p.cross - 2 * k, self.UP, p.z < p.line - 1))
+        either(has_above, lambda: last(above, p.cross + 2 * k, self.DOWN, p.z > 0))
 
     def whole(self, position):
-        self.arrived(2 * position + 1 - self.p.y, 0)
+        for part in range(self.last):
+            self.arrived(2 * position + 1 - self.p.y, part)
 
     def drain(self):
         p = self.p
@@ -147,45 +166,44 @@
         @pl.loop(0, p.line)
         def _(d):
             mine, other = 2 * d + p.y, 2 * d + 1 - p.y
-            self.copy(self.CROSS, mine, 0).wait_send()
+            for part in range(self.last):
+                self.copy(self.CROSS, mine, part).wait_send()
 
             @pl.when(d == p.z)
             def _():
-                self.copy(self.CROSS, mine, 1).wait_send()
-
-            @pl.when((d <= p.z) & (p.z < p.line - 1))
-            def _():
-                for block, part in ((mine, 0), (mine, 1), (other, 1)):
-                    self.copy(self.UP, block, part).wait_send()
-
-            @pl.when((d >= p.z) & (p.z > 0))
-            def _():
-                for block, part in ((mine, 0), (mine, 1), (other, 1)):
-                    self.copy(self.DOWN, block, part).wait_send()
+                self.copy(self.CROSS, mine, self.last).wait_send()
+
+            def line_sent(way):
+                for part in range(self.last + 1):
+                    self.copy(way, mine, part).wait_send()
+                self.copy(way, other, self.last).wait_send()
+
+            either((d <= p.z) & (p.z < p.line - 1), lambda: line_sent(self.UP))
+            either((d >= p.z) & (p.z > 0), lambda: line_sent(self.DOWN))
 
 
 class Reduce:
-    UP, DOWN, CROSS, BUP, BDN, BX = 0, 1, 2, 3, 5, 7
+    BUP, BDN, BX = 0, 2, 4
+    UP, DOWN, CROSS = 5, 5 + CHUNKS, 5 + 2 * CHUNKS
+    WAYS = 5 + 3 * CHUNKS
     N_SCRATCH = 9
 
     @staticmethod
-    def scratch(line, rows, split, width, dtype):
+    def scratch(line, rows, width, dtype):
         v = pltpu.VMEM
-        rest = rows - split
-        dma = pltpu.SemaphoreType.DMA
         return (
-            [v((line, split, width), dtype)] * 3
-            + [v((line, 2, rest, width), dtype)] * 2
-            + [v((rest, width), dtype)] * 2
-            + [dma((8, line)), dma((8, line))]
-        )
-
-    def __init__(self, place, split, parts, out, scratch):
+            [v((line, rows - REST, width), dtype)] * 3
+            + [v((line, 2, REST, width), dtype)] * 2
+            + [v((REST, width), dtype)] * 2
+            + [DMA((Reduce.WAYS, line)), DMA((Reduce.WAYS, line))]
+        )
+
+    def __init__(self, place, parts, out, scratch):
         self.p, self.parts, self.out = place, parts, out
         self.cross_in, self.up_in, self.down_in, self.bup_in, self.bdn_in = scratch[:5]
         self.bx_out, self.bx_in, self.send_sem, self.recv_sem = scratch[5:]
-        self.a = pl.ds(0, split)
-        self.b = pl.ds(split, parts.shape[1] - split)
+        self.pieces = pieces(parts.shape[1])
+        self.b = self.pieces[-1]
 
     def desc(self, way, slot, src, dst, peer):
         return pltpu.make_async_remote_copy(
@@ -197,17 +215,26 @@
             device_id_type=MESH,
         )
 
-    def cross_copy(self, d):
-        p = self.p
+    def cross_copy(self, d, c):
+        p, at = self.p, self.pieces[c]
         return self.desc(
-            self.CROSS, d, self.parts.at[2 * d + 1 - p.y, self.a], self.cross_in.at[d], p.cross
-        )
-
-    def line_copy(self, up, d):
-        p = self.p
-        if up:
-            return self.desc(self.UP, d, self.cross_in.at[d], self.up_in.at[d], p.me + 2)
-        return self.desc(self.DOWN, d, self.cross_in.at[d], self.down_in.at[d], p.me - 2)
+            self.CROSS + c,
+            d,
+            self.parts.at[2 * d + 1 - p.y, at],
+            self.cross_in.at[d, at],
+            p.cross,
+        )
+
+    def line_copy(self, up, d, c):
+        p, at = self.p, self.pieces[c]
+        came = self.up_in if up else self.down_in
+        return self.desc(
+            (self.UP if up else self.DOWN) + c,
+            d,
+            self.cross_in.at[d, at],
+            came.at[d, at],
+            p.me + 2 if up else p.me - 2,
+        )
 
     def b_copy(self, up, d, o, src=None):
         p = self.p
@@ -227,7 +254,8 @@
         return self.p.y if o == 0 else 1 - self.p.y
 
     def send_across(self, i):
-        self.cross_copy(self.p.far(i)).start()
+        for c in range(CHUNKS):
+            self.cross_copy(self.p.far(i), c).start()
 
     def b_hop(self, i):
         p = self.p
@@ -252,24 +280,26 @@
     def hop(self, i):
         p = self.p
         d = p.far(i)
-        self.cross_copy(d).wait_recv()
-        mine = self.parts.at[2 * d + p.y, self.a]
-        held = self.cross_in.at[d]
-
-        def go(up):
-            first = p.low_end if up else p.high_end
-            came = self.up_in if up else self.down_in
-            either(first, lambda: total_into(held, mine, held))
-
-            @pl.when(jnp.logical_not(first))
-            def _():
-                self.line_copy(up, d).wait_recv()
-                total_into(held, mine, held, came.at[d])
-
-            self.line_copy(up, d).start()
-
-        either(d > p.z, lambda: go(True))
-        either(d < p.z, lambda: go(False))
+        for c in range(CHUNKS):
+            self.cross_copy(d, c).wait_recv()
+            at = self.pieces[c]
+            mine = self.parts.at[2 * d + p.y, at]
+            held = self.cross_in.at[d, at]
+
+            def go(up):
+                first = p.low_end if up else p.high_end
+                came = self.up_in if up else self.down_in
+                either(first, lambda: total_into(held, mine, held))
+
+                @pl.when(jnp.logical_not(first))
+                def _():
+                    self.line_copy(up, d, c).wait_recv()
+                    total_into(held, mine, held, came.at[d, at])
+
+                self.line_copy(up, d, c).start()
+
+            either(d > p.z, lambda: go(True))
+            either(d < p.z, lambda: go(False))
 
     def close(self, dst, mine, ups, downs):
         p = self.p
@@ -295,15 +325,17 @@
             self.bup_in.at[p.z, 0],
             self.bdn_in.at[p.z, 0],
         )
-        self.cross_copy(p.z).wait_recv()
-        either(jnp.logical_not(p.low_end), lambda: self.line_copy(True, p.z).wait_recv())
-        either(jnp.logical_not(p.high_end), lambda: self.line_copy(False, p.z).wait_recv())
-        self.close(
-            self.out.at[self.a],
-            (self.parts.at[p.me, self.a], self.cross_in.at[p.z]),
-            self.up_in.at[p.z],
-            self.down_in.at[p.z],
-        )
+        for c in range(CHUNKS):
+            self.cross_copy(p.z, c).wait_recv()
+            either(jnp.logical_not(p.low_end), lambda: self.line_copy(True, p.z, c).wait_recv())
+            either(jnp.logical_not(p.high_end), lambda: self.line_copy(False, p.z, c).wait_recv())
+            at = self.pieces[c]
+            self.close(
+                self.out.at[at],
+                (self.parts.at[p.me, at], self.cross_in.at[p.z, at]),
+                self.up_in.at[p.z, at],
+                self.down_in.at[p.z, at],
+            )
 
     def drain(self):
         p = self.p
@@ -311,19 +343,16 @@
 
         @pl.loop(0, p.line)
         def _(d):
-            self.cross_copy(d).wait_send()
-
-            @pl.when(d > p.z)
-            def _():
-                self.line_copy(True, d).wait_send()
-                self.b_copy(True, d, 0).wait_send()
-                self.b_copy(True, d, 1).wait_send()
-
-            @pl.when(d < p.z)
-            def _():
-                self.line_copy(False, d).wait_send()
-                self.b_copy(False, d, 0).wait_send()
-                self.b_copy(False, d, 1).wait_send()
+            def line_sent(up):
+                for c in range(CHUNKS):
+                    self.line_copy(up, d, c).wait_send()
+                self.b_copy(up, d, 0).wait_send()
+                self.b_copy(up, d, 1).wait_send()
+
+            for c in range(CHUNKS):
+                self.cross_copy(d, c).wait_send()
+            either(d > p.z, lambda: line_sent(True))
+            either(d < p.z, lambda: line_sent(False))
 
 
 def dot(a, b):
@@ -359,13 +388,36 @@
     return turn_by(v, cosine, -sine)
 
 
-def probabilities(query, keys, rows_from, bias):
+def probabilities(query, keys, rows_from, limit):
     scores = dot_t(query, keys) * (1.0 / math.sqrt(HD))
     row = lax.broadcasted_iota(jnp.int32, scores.shape, 0) + rows_from
     col = lax.broadcasted_iota(jnp.int32, scores.shape, 1)
-    scores = jnp.where((col <= row) & (bias >= 0.0), scores, MASKED)
+    scores = jnp.where((col <= row) & (col < limit), scores, MASKED)
     weight = jnp.exp(scores - jnp.max(scores, -1, keepdims=True))
     return weight / jnp.sum(weight, -1, keepdims=True)
+
+
+def row_valid(place, lengths, rows):
+    slots = rows // lengths.shape[0]
+    row = lax.broadcasted_iota(jnp.int32, (rows, 1), 0)
+    limit = jnp.full((rows, 1), lengths[0], jnp.int32)
+    for n in range(1, lengths.shape[0]):
+        limit = jnp.where(row >= n * slots, lengths[n], limit)
+    return place.me * slots + lax.rem(row, slots) < limit
+
+
+def gain_row(shares, which):
+    return jnp.concatenate([shares[b, which : which + 1] for b in range(shares.shape[0])], 1)
+
+
+def inverse_rms(x):
+    return lax.rsqrt(jnp.mean(x * x, -1, keepdims=True) + EPSILON)
+
+
+def norm_grad(x, inverse, gain, grad):
+    weighted = grad * gain
+    inner = jnp.sum(weighted * x, -1, keepdims=True)
+    return inverse * weighted - x * inverse * inverse * inverse * inner / x.shape[-1]
 
 
 def start_all(copies):
@@ -376,6 +428,10 @@
 def wait_all(copies):
     for c in copies:
         c.wait()
+
+
+def scalars():
+    return pl.BlockSpec(memory_space=pltpu.SMEM)
 
 
 def hbm():
@@ -392,18 +448,15 @@
     )
 
 
-DMA = pltpu.SemaphoreType.DMA
-
-
 def gather_sems(count):
-    return [DMA, DMA((3, count, 2)), DMA((count, 2))]
+    return [DMA, DMA((3, count, CHUNKS + 1)), DMA((count, CHUNKS + 1))]
 
 
 def attention_kernel(
-    line, split, groups, seqs,
-    own, cot_own, small, bias, freq, wq_hbm, wk_hbm, wv_hbm, wo_hbm,
+    line, groups, seqs,
+    lengths, own, cot_raw, pre_gain, mid_gain, freq, wq_hbm, wk_hbm, wv_hbm, wo_hbm,
     branch, small_out, normed_hbm, cot_hbm, q_hbm, k_hbm, v_hbm, attended_hbm, wkv_hbm, cos_hbm, sin_hbm,
-    rows_all, normed, cot_all, q, k, v, attended, wq, wkv, wo, cosine, sine, parts,
+    small, cot_own, rows_all, normed, cot_all, q, k, v, attended, wq, wkv, wo, cosine, sine, parts,
     *scratch,
 ):
     p = Place(line)
@@ -429,6 +482,10 @@
     start_all(loads)
     p.greet(groups)
 
+    small[...] = jnp.zeros_like(small)
+    small[0:1] = pre_gain[...].astype(F32)
+    small[1:2] = mid_gain[...].astype(F32)
+
     def small_copy(step, peer, origin):
         return to_peer(
             "shard", peer, small, small_out.at[origin], small_send.at[step], small_recv.at[step]
@@ -436,7 +493,7 @@
 
     for step in range(1, count):
         small_copy(step, lax.rem(p.me + step, count), p.me).start()
-    gather = Gather(p, split, own, rows_all, *g1)
+    gather = Gather(p, own, rows_all, *g1)
     gather.start()
     small_out[p.me] = small[...]
 
@@ -462,9 +519,11 @@
     angle = pos * freq[...]
     cosine[...] = jnp.cos(angle)
     sine[...] = jnp.sin(angle)
+    cot = cot_raw[...]
+    cot_own[...] = jnp.where(row_valid(p, lengths, cot.shape[0]), cot, jnp.zeros_like(cot))
     for step in range(1, count):
         small_copy(step, p.me, lax.rem(p.me + count - step, count)).wait_recv()
-    gain = jnp.concatenate([small_out[s, 0:1] for s in range(count)], 1).astype(F32)
+    gain = gain_row(small_out, 0)
     across().wait_recv()
     for step in range(1, groups):
         share(step).start()
@@ -483,9 +542,7 @@
         d = p.near(i)
         gather.whole(d)
         x = rows_all[pl.ds(2 * d, 2)].reshape(pair, -1).astype(F32)
-        n = (
-            x * lax.rsqrt(jnp.mean(x * x, -1, keepdims=True) + EPSILON) * gain
-        ).astype(low)
+        n = (x * inverse_rms(x) * gain).astype(low)
         normed[pl.ds(2 * d, 2)] = n.reshape(2, rows, -1)
         at = pl.ds(pl.multiple_of(d * 2 * slots, 2 * slots), 2 * slots)
         c, s = cosine[at], sine[at]
@@ -522,7 +579,7 @@
         )
     ]
     start_all(saves)
-    cots = Gather(p, split, cot_own, cot_all, *g2)
+    cots = Gather(p, cot_own, cot_all, *g2)
     cots.start()
     total_slots = q.shape[1]
     tile = min(256, total_slots)
@@ -532,7 +589,7 @@
         for t in range(total_slots // tile):
             span = (t + 1) * tile
             at = pl.ds(t * tile, tile)
-            probs = probabilities(q[n, at], k[n, pl.ds(0, span)], t * tile, bias[n][:, :span])
+            probs = probabilities(q[n, at], k[n, pl.ds(0, span)], t * tile, lengths[n])
             out = dot(probs.astype(low), v[n, pl.ds(0, span)]).astype(low)
             for c in range(tile // slots):
                 b = (t * tile) // slots + c
@@ -549,13 +606,13 @@
         at = pl.ds(pl.multiple_of(d * pair, pair), pair)
         parts[pl.ds(2 * d, 2)] = dot(attended[at], wo[...]).astype(low).reshape(2, rows, -1)
 
-    reduce = Reduce(p, split, parts, branch, r_scratch)
-    for i in range(DEPTH):
-        reduce.send_across(i)
+    reduce = Reduce(p, parts, branch, r_scratch)
     saves2 = [pltpu.make_async_copy(attended, attended_hbm, save_sem.at[7])]
     start_all(saves2)
     for d in range(line):
         cots.whole(d)
+    for i in range(DEPTH):
+        reduce.send_across(i)
     saves3 = [pltpu.make_async_copy(cot_all, cot_hbm, save_sem.at[8])]
     start_all(saves3)
     for i in range(line - 1):
@@ -576,9 +633,11 @@
         small_copy(step, lax.rem(p.me + step, count), p.me).wait_send()
 
 
-def attention(own, cot, small, bias, freq, wq, wk, wv, wo, count, groups, ident, split=112):
+def attention(lengths, own, cot, pre_gain, mid_gain, freq, wq, wk, wv, wo, count, groups, ident):
     rows, width = own.shape
-    seqs, _, total_slots = bias.shape
+    seqs = lengths.shape[0]
+    total_slots = count * rows // seqs
+    small = (8, pre_gain.shape[1])
     line = count // 2
     low = own.dtype
     v = pltpu.VMEM
@@ -589,10 +648,10 @@
     table = (total_slots, hd // 2)
     flat = (count * rows, hd)
     return pl.pallas_call(
-        functools.partial(attention_kernel, line, split, groups, seqs),
+        functools.partial(attention_kernel, line, groups, seqs),
         out_shape=(
             shape((rows, width), F32),
-            shape((count,) + small.shape, small.dtype),
+            shape((count,) + small, F32),
             shape(big, low),
             shape(big, low),
             shape(head, low),
@@ -603,25 +662,25 @@
             shape(table, F32),
             shape(table, F32),
         ),
-        in_specs=[vm()] * 5 + [hbm()] * 4,
+        in_specs=[scalars()] + [vm()] * 5 + [hbm()] * 4,
         out_specs=(vm(), vm()) + (hbm(),) * 9,
         scratch_shapes=[
-            v(big, low), v(big, low), v(big, low), v(head, low), v(head, low), v(head, low), v(flat, low),
+            v(small, F32), v((rows, width), low), v(big, low), v(big, low), v(big, low), v(head, low), v(head, low), v(head, low), v(flat, low),
             v((hd, width), low), v((2, hd, width), low), v((hd, width), low), v(table, F32), v(table, F32), v(big, low),
         ]
         + gather_sems(count) * 2
         + [DMA((4,)), DMA((count,)), DMA((count,)), DMA, DMA((groups,)), DMA((groups,)), DMA((9,))]
-        + Reduce.scratch(line, rows, split, width, low),
+        + Reduce.scratch(line, rows, width, low),
         compiler_params=params(ident),
         name="attention",
-    )(own, cot, small, bias, freq, wq, wk, wv, wo)
+    )(lengths, own, cot, pre_gain, mid_gain, freq, wq, wk, wv, wo)
 
 
 def ffn_kernel(
-    line, split, groups,
-    own, cot_hbm, gate_hbm, up_hbm, down_hbm,
-    second, ffn_hbm, pair_hbm, total_hbm,
-    normed, cot, gate_w, up_w, down_w, hidden, gate_g, up_g, parts, stage, theirs, chip_in,
+    line, groups,
+    tokens, branch, gains, cot_hbm, gate_hbm, up_hbm, down_hbm,
+    second, ffn_hbm, pair_hbm, chip_in,
+    own, normed, cot, gate_w, up_w, down_w, hidden, gate_g, up_g, parts, stage, theirs,
     *scratch,
 ):
     p = Place(line)
@@ -629,7 +688,7 @@
     core = lax.rem(rank, 2)
     partner = rank + 1 - 2 * core
     opposite = lax.rem(rank + 2, groups)
-    (load_sem, out_sem, stage_send, stage_recv, chip_send, chip_recv, back_send, back_recv) = scratch[3:11]
+    (load_sem, out_sem, stage_send, stage_recv, chip_send, chip_recv) = scratch[3:9]
     loads = [
         pltpu.make_async_copy(src, dst, load_sem.at[i])
         for i, (src, dst) in enumerate(
@@ -637,8 +696,10 @@
         )
     ]
     start_all(loads)
+    middle = tokens[...].astype(F32) + branch[...]
+    own[...] = (middle * inverse_rms(middle) * gain_row(gains, 1)).astype(own.dtype)
     p.greet(groups)
-    gather = Gather(p, split, own, normed, *scratch[:3])
+    gather = Gather(p, own, normed, *scratch[:3])
     gather.start()
     wait_all(loads)
     rows = own.shape[0]
@@ -663,7 +724,7 @@
         part = dot(gate_g[at], gate_w[...]) + dot(up_g[at], up_w[...])
         parts[pl.ds(2 * d, 2)] = part.astype(low).reshape(2, rows, -1)
 
-    reduce = Reduce(p, split, parts, second, scratch[11:])
+    reduce = Reduce(p, parts, second, scratch[9:])
     for i in range(DEPTH):
         reduce.send_across(i)
     for i in range(line - 1):
@@ -707,16 +768,19 @@
         total_into(mine[which], mine[which], theirs.at[which])
 
     def chip_copy():
-        return to_peer("grp", opposite, mine[0], chip_in, chip_send, chip_recv)
+        return to_peer(
+            "grp", opposite, mine[0].at[pl.ds(0, quarter)], chip_in, chip_send, chip_recv
+        )
 
     def save_pair(which):
-        return pltpu.make_async_copy(mine[which], pair_hbm.at[which - 1], out_sem.at[which])
+        return pltpu.make_async_copy(mine[which], pair_hbm.at[which], out_sem.at[which])
 
     gradient(0, hidden, cot)
     reduce.hop(0)
     reduce.send_across(DEPTH)
     add_theirs(0)
     chip_copy().start()
+    save_pair(0).start()
     gradient(1, gate_g, normed)
     reduce.hop(1)
     reduce.send_across(DEPTH + 1)
@@ -731,7 +795,7 @@
         at = pl.ds(pl.multiple_of(d * pair, pair), pair)
         normed[pl.ds(2 * d, 2)] = dot(hidden[at], down_w[...]).astype(low).reshape(2, rows, -1)
 
-    ffn_save = pltpu.make_async_copy(normed, ffn_hbm, out_sem.at[0])
+    ffn_save = pltpu.make_async_copy(normed, ffn_hbm, out_sem.at[3])
     ffn_save.start()
     add_theirs(2)
     save_pair(2).start()
@@ -739,62 +803,54 @@
     for j in range(2):
         to_partner(2, j).wait_send()
 
-    at = pl.ds(pl.multiple_of(core * half, half), half)
-    keep = pltpu.make_async_copy(chip_in, total_hbm.at[at], out_sem.at[3])
-    give = to_peer("grp", partner, chip_in, total_hbm.at[at], back_send, back_recv)
-    chip_copy().wait_recv()
-    total_into(chip_in, mine[0], chip_in)
-    keep.start()
-    give.start()
     reduce.drain()
-    chip_copy().wait_send()
+    chip_copy().wait()
     ffn_save.wait()
-    for which in (1, 2):
+    for which in range(3):
         save_pair(which).wait()
-    keep.wait()
-    give.wait()
-
-
-def ffn(own, cot, gate_w, up_w, down_w, groups, ident, split=112):
-    rows, width = own.shape
+
+
+def ffn(tokens, branch, gains, cot, gate_w, up_w, down_w, groups, ident):
+    rows, width = tokens.shape
     count = cot.shape[0]
     line = count // 2
     units = gate_w.shape[0]
-    low = own.dtype
+    low = tokens.dtype
     v = pltpu.VMEM
-    tokens = count * rows
+    tall = count * rows
     shape = jax.ShapeDtypeStruct
     big = (count, rows, width)
     half = (units // 2, width)
     return pl.pallas_call(
-        functools.partial(ffn_kernel, line, split, groups),
+        functools.partial(ffn_kernel, line, groups),
         out_shape=(
             shape((rows, width), F32),
             shape(big, low),
-            shape((2,) + half, low),
-            shape((units, width), low),
+            shape((3,) + half, low),
+            shape((units // 4, width), low),
         ),
-        in_specs=[vm()] + [hbm()] * 4,
+        in_specs=[vm()] * 3 + [hbm()] * 4,
         out_specs=(vm(), hbm(), hbm(), hbm()),
-        scratch_shapes=[v(big, low)] * 2
+        scratch_shapes=[v((rows, width), low)]
+        + [v(big, low)] * 2
         + [v((units, width), low)] * 3
-        + [v((tokens, units), low)] * 3
-        + [v(big, low), v((2, units // 4, width), low), v((3,) + half, low), v(half, low)]
+        + [v((tall, units), low)] * 3
+        + [v(big, low), v((2, units // 4, width), low), v((3,) + half, low)]
         + gather_sems(count)
-        + [DMA((4,)), DMA((4,)), DMA((2,)), DMA((3, 2)), DMA, DMA, DMA, DMA]
-        + Reduce.scratch(line, rows, split, width, low),
+        + [DMA((4,)), DMA((4,)), DMA((2,)), DMA((3, 2)), DMA, DMA]
+        + Reduce.scratch(line, rows, width, low),
         compiler_params=params(ident),
         name="ffn",
-    )(own, cot, gate_w, up_w, down_w)
+    )(tokens, branch, gains, cot, gate_w, up_w, down_w)
 
 
 def attention_grad_kernel(
-    line, split, groups, seqs,
-    own, bias, cosine, sine, gain, gain_parts,
-    ffn_hbm, normed_hbm, attended_hbm, q_hbm, k_hbm, v_hbm, wq_hbm, wkv_hbm, wo_hbm, sums_hbm,
-    first, ffn_own, gain_out, total_hbm, attn_hbm,
-    dbranch, normed, attended, q, k, v, wq, wkv, wo, da, dk_acc, dv_acc, dq_rows, dk_rows, dv_rows,
-    halves, half_in, ffn_parts, parts, sums, sums_in, stage, mine, theirs, mine_in, gain_held, gain_in, gain_sum, gain_all,
+    line, groups, seqs,
+    lengths, tokens, branch, cot, second, gains, cosine, sine,
+    ffn_hbm, normed_hbm, attended_hbm, q_hbm, k_hbm, v_hbm, wq_hbm, wkv_hbm, wo_hbm, sums_hbm, early_hbm,
+    mixed, input_grad, gain_out, total_hbm, attn_hbm,
+    own, middle_grad, first, ffn_own, dbranch, normed, attended, q, k, v, wq, wkv, wo, da, dk_acc, dv_acc, dq_rows, dk_rows, dv_rows,
+    halves, half_in, ffn_parts, sums, sums_in, stage, mine, theirs, mine_in, gain_held, gain_in, gain_sum, gain_all,
     *scratch,
 ):
     p = Place(line)
@@ -821,13 +877,31 @@
                 (wq_hbm, wq),
                 (wkv_hbm, wkv),
                 (normed_hbm, normed),
-                (sums_hbm, sums),
+                (early_hbm, sums_in.at[0]),
             )
         )
     ]
     start_all(loads)
+
+    def load_sum(i):
+        return pltpu.make_async_copy(sums_hbm.at[i], sums.at[i % 2], load_sem.at[10 + i % 2])
+
+    load_sum(0).start()
+    load_sum(1).start()
+    middle = tokens[...].astype(F32) + branch[...]
+    inverse = inverse_rms(middle)
+    grad = cot[...].astype(F32)
+    grad = jnp.where(row_valid(p, lengths, grad.shape[0]), grad, jnp.zeros_like(grad))
+    grad = grad + norm_grad(middle, inverse, gain_row(gains, 1), second[...])
+    middle_grad[...] = grad
+    own[...] = grad.astype(own.dtype)
+    mid_total = jnp.sum(second[...] * middle * inverse, 0, keepdims=True)
+    share = gain_held.shape[2]
+    for b in range(count):
+        gain_held[b] = jnp.zeros(gain_held.shape[1:], F32)
+        gain_held[b, 1:2] = mid_total[:, b * share : (b + 1) * share]
     p.greet(groups)
-    gather = Gather(p, split, own, dbranch, *scratch[:3])
+    gather = Gather(p, own, dbranch, *scratch[:3])
     n_sums = sums_hbm.shape[0]
     part_rows = sums.shape[1]
 
@@ -836,7 +910,7 @@
             "grp", opposite, sums_hbm.at[i], sums_in.at[i], chip_send.at[i], chip_recv.at[i]
         )
 
-    for i in range(n_sums):
+    for i in range(1, n_sums):
         chip_copy(i).start()
     gather.start()
     wait_all(loads)
@@ -857,7 +931,7 @@
                 at = pl.ds(pl.multiple_of(d * 2 * slots + block * slots, slots), slots)
                 da[m, at] = grad[block * rows + m * slots : block * rows + (m + 1) * slots]
 
-    ffn_sum = Reduce(p, split, ffn_parts, ffn_own, scratch[17 : 17 + n])
+    ffn_sum = Reduce(p, ffn_parts, ffn_own, scratch[17 : 17 + n])
     for i in range(DEPTH):
         ffn_sum.send_across(i)
     for i in range(line - 1):
@@ -907,7 +981,7 @@
             at = pl.ds(t * tile, tile)
             query, grad = q[m, at], da[m, at]
             keys, values = k[m, pl.ds(0, span)], v[m, pl.ds(0, span)]
-            probs = probabilities(query, keys, t * tile, bias[m][:, :span])
+            probs = probabilities(query, keys, t * tile, lengths[m])
             dprobs = dot_t(grad, values)
             inner = jnp.sum(probs * dprobs, -1, keepdims=True)
             dscores = (probs * (dprobs - inner)).astype(low)
@@ -937,6 +1011,8 @@
         halves[h, 0] = dk_rows[:, h * half : (h + 1) * half]
         halves[h, 1] = dv_rows[:, h * half : (h + 1) * half]
     swap().start()
+    gather.drain()
+    parts = dbranch
     gradient(2, dq_rows[:, :chunk], normed)
     gradient(3, dq_rows[:, chunk:], normed)
 
@@ -948,9 +1024,7 @@
 
     for i in range(seqs, line - 1):
         ffn_sum.hop(i)
-    reduce = Reduce(p, split, parts, first, scratch[17 + n :])
-    for i in range(DEPTH):
-        reduce.send_across(i)
+    reduce = Reduce(p, parts, first, scratch[17 + n :])
     swap().wait_recv()
 
     def summed(which):
@@ -969,23 +1043,34 @@
     total_into(mine, mine, theirs)
     attn_chip().start()
     ffn_sum.finish()
+    for i in range(DEPTH):
+        reduce.send_across(i)
     for i in range(line - 1):
         reduce.b_hop(i)
+    valid = row_valid(p, lengths, rows)
+    result = tokens[...].astype(F32) + branch[...] + ffn_own[...]
+    mixed[...] = jnp.where(valid, result, jnp.zeros_like(result)).astype(low)
 
     def back(i):
         if i < n_sums:
-            whole, size, out = sums.at[i], part_rows, total_hbm.at[i]
+            whole, size, out = sums_in.at[i], part_rows, total_hbm.at[i // 2]
+            start = core * 2 * size + (i % 2) * size
         else:
             whole, size, out = mine, 3 * chunk, attn_hbm
-        at = pl.ds(pl.multiple_of(core * size, size), size)
+            start = core * size
+        at = pl.ds(pl.multiple_of(start, size), size)
         return (
             pltpu.make_async_copy(whole, out.at[at], keep_sem.at[i]),
             to_peer("grp", partner, whole, out.at[at], back_send.at[i], back_recv.at[i]),
         )
 
     def sum_up(i):
-        chip_copy(i).wait()
-        total_into(sums.at[i], sums.at[i], sums_in.at[i])
+        if i:
+            chip_copy(i).wait()
+        load_sum(i).wait()
+        total_into(sums_in.at[i], sums.at[i % 2], sums_in.at[i])
+        if i + 2 < n_sums:
+            load_sum(i + 2).start()
         start_all(back(i))
 
     def gain_copy(step, peer, origin):
@@ -1006,10 +1091,8 @@
             return total
 
         total = lax.fori_loop(0, rows // 16, body, jnp.zeros((16, parts.shape[2]), F32))
-        total = jnp.sum(total, 0, keepdims=True) / gain[...]
-        share = gain_held.shape[2]
+        total = jnp.sum(total, 0, keepdims=True) / gain_row(gains, 0)
         for b in range(count):
-            gain_held[b] = gain_parts[b]
             gain_held[b, 0:1] = total[:, b * share : (b + 1) * share]
         for step in range(1, count):
             gain_copy(step, lax.rem(p.me + step, count), p.me).start()
@@ -1030,12 +1113,14 @@
     reduce.send_across(DEPTH)
     gain_first()
     sum_up(0)
+    sum_up(1)
     reduce.hop(1)
     reduce.send_across(DEPTH + 1)
     gain_second()
+    sum_up(2)
+    sum_up(3)
     reduce.hop(2)
-    for i in range(1, n_sums):
-        sum_up(i)
+    sum_up(4)
     reduce.finish()
     for step in range(1, groups):
         gain_group(step, rank, lax.rem(rank + groups - step, groups)).wait_recv()
@@ -1043,12 +1128,15 @@
     for b in range(1, groups):
         total = total + gain_all[b]
     gain_out[...] = total
+    source = tokens[...].astype(F32)
+    inner = norm_grad(source, inverse_rms(source), gain_row(gains, 0), first[...])
+    input_grad[...] = (middle_grad[...] + inner).astype(low)
+    sum_up(5)
     attn_chip().wait()
     total_into(mine, mine, mine_in)
     start_all(back(n_sums))
     reduce.drain()
     ffn_sum.drain()
-    gather.drain()
     swap().wait_send()
     for b in range(3):
         to_partner(b).wait_send()
@@ -1061,54 +1149,59 @@
 
 
 def attention_grad(
-    own, bias, cosine, sine, gain, gain_parts, ffn_parts, normed, attended, q, k, v, wq, wkv, wo, sums,
-    groups, ident, split=112,
+    lengths, tokens, branch, cot, second, gains, cosine, sine, ffn_parts, normed, attended, q, k, v, wq, wkv, wo, sums, early,
+    groups, ident,
 ):
-    rows, width = own.shape
+    rows, width = tokens.shape
     count = normed.shape[0]
     line = count // 2
     seqs, total_slots, hd = q.shape
-    low = own.dtype
+    low = tokens.dtype
     vmem = pltpu.VMEM
-    tokens = count * rows
+    tall = count * rows
     half = hd // 2
+    sums = sums.reshape((-1,) + early.shape)
     n_sums, part_rows, _ = sums.shape
     shape = jax.ShapeDtypeStruct
     big = vmem((count, rows, width), low)
     head = vmem((seqs, total_slots, hd), low)
     weight = vmem((hd, width), low)
-    flat = vmem((tokens, hd), low)
+    flat = vmem((tall, hd), low)
     acc = vmem((total_slots, hd), F32)
     third = vmem((3 * half, width), low)
-    g = gain_parts.shape
+    g = gains.shape
+    block = vmem((rows, width), F32)
     return pl.pallas_call(
-        functools.partial(attention_grad_kernel, line, split, groups, seqs),
+        functools.partial(attention_grad_kernel, line, groups, seqs),
         out_shape=(
-            shape((rows, width), F32),
-            shape((rows, width), F32),
+            shape((rows, width), low),
+            shape((rows, width), low),
             shape(g[1:], F32),
-            shape((n_sums, 2 * part_rows, width), low),
+            shape((n_sums // 2, 4 * part_rows, width), low),
             shape((6 * half, width), low),
         ),
-        in_specs=[vm()] * 6 + [hbm()] * 10,
+        in_specs=[scalars()] + [vm()] * 7 + [hbm()] * 11,
         out_specs=(vm(), vm(), vm(), hbm(), hbm()),
         scratch_shapes=[
+            vmem((rows, width), low), block, block, block,
             big, big, flat, head, head, head, weight, vmem((2, hd, width), low), weight, head, acc, acc,
             flat, flat, flat,
-            vmem((2, 2, tokens, half), low), vmem((2, tokens, half), low), big, big,
-            vmem(sums.shape, low), vmem(sums.shape, low), vmem((3, half, width), low), third, third, third,
+            vmem((2, 2, tall, half), low), vmem((2, tall, half), low), big,
+            vmem((2,) + early.shape, low), vmem(sums.shape, low), vmem((3, half, width), low), third, third, third,
             vmem(g, F32), vmem(g, F32), vmem(g[1:], F32), vmem((groups,) + g[1:], F32),
         ]
         + gather_sems(count)
         + [
-            DMA((10,)), DMA((n_sums + 1,)), DMA((n_sums + 1,)), DMA, DMA, DMA((3,)), DMA((3,)),
+            DMA((12,)), DMA((n_sums + 1,)), DMA((n_sums + 1,)), DMA, DMA, DMA((3,)), DMA((3,)),
             DMA((n_sums + 1,)), DMA((n_sums + 1,)), DMA((n_sums + 1,)),
             DMA((count,)), DMA((count,)), DMA((groups,)), DMA((groups,)),
         ]
-        + Reduce.scratch(line, rows, split, width, low) * 2,
+        + Reduce.scratch(line, rows, width, low) * 2,
         compiler_params=params(ident),
         name="attention_grad",
-    )(own, bias, cosine, sine, gain, gain_parts, ffn_parts, normed, attended, q, k, v, wq, wkv, wo, sums)
+    )(
+        lengths, tokens, branch, cot, second, gains, cosine, sine, ffn_parts, normed, attended, q, k, v, wq, wkv, wo, sums, early
+    )
 
 
 epsilon = 1e-06
@@ -1442,26 +1535,18 @@
     low = jnp.bfloat16
     count = lax.axis_size("shard")
     groups = lax.axis_size("grp")
-    shard_rank = lax.axis_index("shard")
     seqs, seq_dev, model_width = tokens.shape
     rows = seqs * seq_dev
-    key_pos = jnp.arange(seq_dev * count, dtype=jnp.int32)
-    local_pos = shard_rank * seq_dev + jnp.arange(seq_dev, dtype=jnp.int32)
-    valid_rows = (local_pos[None, :] < lengths[:, None]).reshape(rows, 1)
-    bias = jnp.where(key_pos[None, None, :] < lengths[:, None, None], 0.0, -1.0)
     inverse_freq = theta_base ** (-(jnp.arange(0, HD, 2).astype(jnp.float32) / HD))
-    cot_low = jnp.where(valid_rows, cotangent.reshape(rows, model_width), jnp.zeros((), low))
-    share = prenorm_gain.shape[0]
-    own_gains = jnp.broadcast_to(
-        jnp.stack([prenorm_gain, midnorm_gain])[:, None, :], (2, 8, share)
-    ).reshape(16, share)
     tokens_low = tokens.reshape(rows, model_width)
+    cot_low = cotangent.reshape(rows, model_width)
     branch, gains, normed_first, cot_all, queries, keys, values, attended, kv_head, cosine, sine = (
         attention(
+            lengths,
             tokens_low,
             cot_low,
-            own_gains,
-            bias,
+            prenorm_gain[None, :],
+            midnorm_gain[None, :],
             inverse_freq[None, :],
             query_weight,
             key_weight,
@@ -1472,32 +1557,18 @@
             1,
         )
     )
-    gains = gains.astype(jnp.float32)
-    prenorm_f = gains[:, 0].reshape(-1)
-    midnorm_f = gains[:, 8].reshape(-1)
-    source = tokens_low.astype(jnp.float32)
-    middle = source + branch
-    scaled_second, inverse_second = norm_forward(middle, midnorm_f)
-    second_grad, ffn_parts, pair_sums, down_total = ffn(
-        scaled_second.astype(low), cot_all, gate_weight, up_weight, down_weight, groups, 2
+    second_grad, ffn_parts, pair_sums, early = ffn(
+        tokens_low, branch, gains, cot_all, gate_weight, up_weight, down_weight, groups, 2
     )
-    middle_part, midnorm_part = norm_backward(middle, inverse_second, midnorm_f, second_grad)
-    middle_grad = cot_low.astype(jnp.float32) + middle_part
-    gain_parts = jnp.concatenate(
-        [
-            jnp.zeros((count, 1, share), jnp.float32),
-            midnorm_part.reshape(count, 1, share),
-            jnp.zeros((count, 6, share), jnp.float32),
-        ],
-        1,
-    )
-    first_grad, ffn_part, gain_own, totals, attn_total = attention_grad(
-        middle_grad.astype(low),
-        bias,
+    mixed, input_gradient, gain_own, totals, attn_total = attention_grad(
+        lengths,
+        tokens_low,
+        branch,
+        cot_low,
+        second_grad,
+        gains,
         cosine,
         sine,
-        prenorm_f[None, :],
-        gain_parts,
         ffn_parts,
         normed_first,
         attended,
@@ -1508,18 +1579,10 @@
         kv_head,
         out_weight,
         pair_sums,
+        early,
         groups,
         3,
     )
-    mixed = jnp.where(valid_rows, middle + ffn_part, 0.0).astype(low)
-    inverse_first = lax.rsqrt(jnp.mean(source * source, -1, keepdims=True) + epsilon)
-    weighted = first_grad * prenorm_f
-    inner_sum = jnp.sum(weighted * source, -1, keepdims=True)
-    input_gradient = (
-        middle_grad
-        + inverse_first * weighted
-        - source * inverse_first * inverse_first * inverse_first * inner_sum / model_width
-    ).astype(low)
     head = query_weight.shape[0]
     kv_share = key_weight.shape[0]
     f32 = jnp.float32
@@ -1532,9 +1595,9 @@
         attn_total[2 * head + kv_share :].astype(f32),
         attn_total[:head].astype(f32),
         gain_own[1],
+        totals[1].astype(f32),
+        totals[2].astype(f32),
         totals[0].astype(f32),
-        totals[1].astype(f32),
-        down_total.astype(f32),
     )
 
 

time: 504 us -> 444 us (0.88)
  Pallas kernels: 459 us -> 421 us
  other arithmetic: 38.6 us -> 17.1 us
    pallas_call x3, Pallas kernels: 459 us -> 421 us  [the longest x1 163 us: attention_grad(): pl.pallas_call(functools.partial(attention_grad_kernel, line, groups, seq...]
    convert_element_type x5 -> x1, other arithmetic: 24.3 us -> 12.5 us  [local_heads(): totals[0].astype(f32)]
where the time goes in v5:
time: 444 us
  Pallas kernels  421 us (95%)
  other arithmetic  17.1 us (4%)
  local copies, waits for them, and re-layouts  5.38 us (1%)
    pallas_call x1, Pallas kernels, attention_grad(): pl.pallas_call(functools.partial(attention_grad_kernel, line, groups, seq...  163 us
    pallas_call x1, Pallas kernels, attention(): pl.pallas_call(functools.partial(attention_kernel, line, groups, seqs), o...  149 us
    pallas_call x1, Pallas kernels, ffn(): pl.pallas_call(functools.partial(ffn_kernel, line, groups), out_shape=(sh...  109 us
    convert_element_type x1, other arithmetic, local_heads(): totals[0].astype(f32)  12.5 us

profile of v5, /device:TPU:0, one launch (start us, length us, event | category | flops | bytes accessed | tf_op | source)
XLA Modules:
  0.0 443.7 jit_solution(11310350409483401604)
XLA Ops:
  0.6 1.2 broadcast_in_dim.7.pre_gain
  1.9 1.2 broadcast_in_dim.8.mid_gain
  3.1 0.5 negate_power_fusion.freq
  3.6 149.0 %attention.1 = (f32[128,2048]{1,0:T(8,128)}, f32[8,8,256]{2,1,0:T(8,128)}, bf16[8,128,2048]{2,1,0:T(8,128)(2,1)}, bf16[8,128,2048]{2,1,0:T(8,128)(2,1)}, bf16[2,...) custom-call(s32[2]{0:T(128)} %lengths.3, ...), custom_call_target="tpu_custom_call" | custom-call | tf_op jit(solution)/shard_map/attention/pallas_call | solution.py:650
  152.6 108.7 %ffn.1 = (f32[128,2048]{1,0:T(8,128)}, bf16[8,128,2048]{2,1,0:T(8,128)(2,1)}, bf16[3,512,2048]{2,1,0:T(8,128)(2,1)}, bf16[256,2048]{1,0:T(8,128)(2,1)}) custom-call(bf16[128,2048]{1,0:T(8,128)(2,1)} %bitcast.18, f32[128,2048]{1,0:T(8,128)} %get-tuple-element.31.branch, f32[8,8,256]{2,1,0:T(8,128)} %get-tuple-element.32.gains, ...), custom_call_target="tpu_custom_call" | custom-call | tf_op jit(solution)/shard_map/ffn/pallas_call | solution.py:824
  261.3 162.8 %attention_grad.1 = (bf16[128,2048]{1,0:T(8,128)(2,1)}, bf16[128,2048]{1,0:T(8,128)(2,1)}, f32[8,256]{1,0:T(8,128)}, bf16[3,1024,2048]{2,1,0:T(8,128)(2,1)}, bf16[768,2048]{1,0:T(8,128)(2,1)}) custom-call(s32[2]{0:T(128)} %lengths.3, bf16[128,2048]{1,0:T(8,128)(2,1)} %bitcast.19, f32[128,2048]{1,0:T(8,128)} %get-tuple-element.31.branch, ...), custom_call_target="tpu_custom_call" | custom-call | tf_op jit(solution)/shard_map/attention_grad/pallas_call | solution.py:1174
  424.1 0.0 copy-start
  424.1 12.5 %bitcast_convert_fusion = (f32[1024,2048]{1,0:T(8,128)}, f32[1024,2048]{1,0:T(8,128)}, f32[1024,2048]{1,0:T(8,128)}) fusion(bf16[3,1024,2048]{2,1,0:T(8,128)(2,1)} %get-tuple-element.50), kind=kLoop, calls=%fused_computation | loop fusion | flops 6291456 | bytes 37748736 | tf_op jit(solution)/shard_map/convert_element_type | solution.py:1600
  436.7 0.0 copy-done
  436.7 0.0 copy-start.2
  436.7 0.0 copy-start.1
  436.7 2.5 slice_convert_fusion
  439.2 1.6 slice_convert_fusion.2
  440.8 1.3 fusion
  442.1 0.0 copy-done.2
  442.1 0.8 copy.25
  442.9 0.0 copy-done.1
  442.9 0.8 copy.26
Async XLA Ops:
  424.1 12.5 %copy-start = (bf16[768,2048]{1,0:T(8,128)(2,1)S(1)}, bf16[768,2048]{1,0:T(8,128)(2,1)}, u32[]{:S(2)}) copy-start(bf16[768,2048]{1,0:T(8,128)(2,1)} %get-tuple-element.49) | copy-start | bytes 9437188
  436.7 5.4 %copy-start.2 = (bf16[128,2048]{1,0:T(8,128)(2,1)S(1)}, bf16[128,2048]{1,0:T(8,128)(2,1)}, u32[]{:S(2)}) copy-start(bf16[128,2048]{1,0:T(8,128)(2,1)} %get-tuple-element.46) | copy-start | bytes 1572868
  436.7 6.2 %copy-start.1 = (bf16[128,2048]{1,0:T(8,128)(2,1)S(1)}, bf16[128,2048]{1,0:T(8,128)(2,1)}, u32[]{:S(2)}) copy-start(bf16[128,2048]{1,0:T(8,128)(2,1)} %get-tuple-element.47) | copy-start | bytes 1572868

commit v6 on v5

--- a/solution.py
+++ b/solution.py
@@ -18,6 +18,8 @@
 F32 = jnp.float32
 DMA = pltpu.SemaphoreType.DMA
 REST = 16
+PIECE = 128
+EARLY = 3
 CHUNKS = 2
 
 
@@ -122,18 +124,24 @@
         self.copy(self.CROSS, origin, part).wait_recv()
 
     def start(self):
+        self.send_own()
+        self.pass_rest()
+
+    def send_own(self):
         p = self.p
-        self.keep = pltpu.make_async_copy(self.own, self.out.at[p.me], self.local_sem)
-        self.keep.start()
+        pltpu.make_async_copy(self.own, self.out.at[p.me], self.local_sem).start()
         for part in (self.last,) + tuple(range(self.last)):
             self.copy(self.CROSS, p.me, part, True).start()
         for part in range(self.last + 1):
             either(p.z < p.line - 1, lambda: self.copy(self.UP, p.me, part, True).start())
             either(p.z > 0, lambda: self.copy(self.DOWN, p.me, part, True).start())
+
+    def pass_rest(self):
+        p = self.p
         self.arrived(p.cross, self.last)
         either(p.z < p.line - 1, lambda: self.copy(self.UP, p.cross, self.last).start())
         either(p.z > 0, lambda: self.copy(self.DOWN, p.cross, self.last).start())
-        self.keep.wait()
+        pltpu.make_async_copy(self.own, self.out.at[p.me], self.local_sem).wait()
 
     def hop(self, k):
         p = self.p
@@ -495,6 +503,7 @@
         small_copy(step, lax.rem(p.me + step, count), p.me).start()
     gather = Gather(p, own, rows_all, *g1)
     gather.start()
+    cots = Gather(p, cot_own, cot_all, *g2)
     small_out[p.me] = small[...]
 
     def rows_of(quarter, column):
@@ -521,6 +530,7 @@
     sine[...] = jnp.sin(angle)
     cot = cot_raw[...]
     cot_own[...] = jnp.where(row_valid(p, lengths, cot.shape[0]), cot, jnp.zeros_like(cot))
+    gather.hop(1)
     for step in range(1, count):
         small_copy(step, p.me, lax.rem(p.me + count - step, count)).wait_recv()
     gain = gain_row(small_out, 0)
@@ -538,7 +548,6 @@
 
     @pl.loop(0, line)
     def _(i):
-        gather.hop(i + 1)
         d = p.near(i)
         gather.whole(d)
         x = rows_all[pl.ds(2 * d, 2)].reshape(pair, -1).astype(F32)
@@ -563,6 +572,8 @@
         put(q, turn_by(dot_t(n, wq[...]), c, s).astype(low))
         put(k, turn_by(dot_t(n, wkv[0]), c, s).astype(low))
         put(v, dot_t(n, wkv[1]).astype(low))
+        gather.hop(i + 2)
+        either(i == line - 3, cots.send_own)
 
     saves = [
         pltpu.make_async_copy(src, dst, save_sem.at[i])
@@ -579,8 +590,7 @@
         )
     ]
     start_all(saves)
-    cots = Gather(p, cot_own, cot_all, *g2)
-    cots.start()
+    cots.pass_rest()
     total_slots = q.shape[1]
     tile = min(256, total_slots)
 
@@ -769,7 +779,7 @@
 
     def chip_copy():
         return to_peer(
-            "grp", opposite, mine[0].at[pl.ds(0, quarter)], chip_in, chip_send, chip_recv
+            "grp", opposite, mine[0].at[pl.ds(0, chip_in.shape[0])], chip_in, chip_send, chip_recv
         )
 
     def save_pair(which):
@@ -827,7 +837,7 @@
             shape((rows, width), F32),
             shape(big, low),
             shape((3,) + half, low),
-            shape((units // 4, width), low),
+            shape((EARLY * PIECE, width), low),
         ),
         in_specs=[vm()] * 3 + [hbm()] * 4,
         out_specs=(vm(), hbm(), hbm(), hbm()),
@@ -877,14 +887,14 @@
                 (wq_hbm, wq),
                 (wkv_hbm, wkv),
                 (normed_hbm, normed),
-                (early_hbm, sums_in.at[0]),
+                (early_hbm, sums_in.at[pl.ds(0, EARLY)]),
             )
         )
     ]
     start_all(loads)
 
     def load_sum(i):
-        return pltpu.make_async_copy(sums_hbm.at[i], sums.at[i % 2], load_sem.at[10 + i % 2])
+        return pltpu.make_async_copy(sums_hbm.at[i], sums.at[lax.rem(i, 2)], load_sem.at[10 + lax.rem(i, 2)])
 
     load_sum(0).start()
     load_sum(1).start()
@@ -910,10 +920,14 @@
             "grp", opposite, sums_hbm.at[i], sums_in.at[i], chip_send.at[i], chip_recv.at[i]
         )
 
-    for i in range(1, n_sums):
+    gather.start()
+
+    @pl.loop(EARLY, n_sums)
+    def _(i):
         chip_copy(i).start()
-    gather.start()
+
     wait_all(loads)
+    ffn_sum = Reduce(p, ffn_parts, ffn_own, scratch[17 : 17 + n])
     rows = own.shape[0]
     pair = 2 * rows
     slots = rows // seqs
@@ -923,6 +937,12 @@
     @pl.loop(0, line)
     def _(i):
         gather.hop(i + 1)
+
+        @pl.when(i == line - 2)
+        def _():
+            for first_sends in range(DEPTH):
+                ffn_sum.send_across(first_sends)
+
         d = p.near(i)
         gather.whole(d)
         grad = dot_t(dbranch[pl.ds(2 * d, 2)].reshape(pair, -1), wo[...]).astype(low)
@@ -931,9 +951,6 @@
                 at = pl.ds(pl.multiple_of(d * 2 * slots + block * slots, slots), slots)
                 da[m, at] = grad[block * rows + m * slots : block * rows + (m + 1) * slots]
 
-    ffn_sum = Reduce(p, ffn_parts, ffn_own, scratch[17 : 17 + n])
-    for i in range(DEPTH):
-        ffn_sum.send_across(i)
     for i in range(line - 1):
         ffn_sum.b_hop(i)
 
@@ -1052,26 +1069,30 @@
     mixed[...] = jnp.where(valid, result, jnp.zeros_like(result)).astype(low)
 
     def back(i):
-        if i < n_sums:
-            whole, size, out = sums_in.at[i], part_rows, total_hbm.at[i // 2]
-            start = core * 2 * size + (i % 2) * size
-        else:
-            whole, size, out = mine, 3 * chunk, attn_hbm
-            start = core * size
-        at = pl.ds(pl.multiple_of(start, size), size)
+        per_half = n_sums // 3
+        start = core * per_half * part_rows + lax.rem(i, per_half) * part_rows
+        at = pl.ds(pl.multiple_of(start, part_rows), part_rows)
+        out = total_hbm.at[lax.div(i, per_half), at]
         return (
-            pltpu.make_async_copy(whole, out.at[at], keep_sem.at[i]),
-            to_peer("grp", partner, whole, out.at[at], back_send.at[i], back_recv.at[i]),
-        )
-
-    def sum_up(i):
-        if i:
-            chip_copy(i).wait()
-        load_sum(i).wait()
-        total_into(sums_in.at[i], sums.at[i % 2], sums_in.at[i])
-        if i + 2 < n_sums:
-            load_sum(i + 2).start()
-        start_all(back(i))
+            pltpu.make_async_copy(sums_in.at[i], out, keep_sem.at[i]),
+            to_peer("grp", partner, sums_in.at[i], out, back_send.at[i], back_recv.at[i]),
+        )
+
+    def back_attn():
+        out = attn_hbm.at[pl.ds(pl.multiple_of(core * 3 * chunk, chunk), 3 * chunk)]
+        return (
+            pltpu.make_async_copy(mine, out, keep_sem.at[n_sums]),
+            to_peer("grp", partner, mine, out, back_send.at[n_sums], back_recv.at[n_sums]),
+        )
+
+    def sum_up(first_piece, end):
+        @pl.loop(first_piece, end)
+        def _(i):
+            either(i >= EARLY, lambda: chip_copy(i).wait())
+            load_sum(i).wait()
+            total_into(sums_in.at[i], sums.at[lax.rem(i, 2)], sums_in.at[i])
+            either(i + 2 < n_sums, lambda: load_sum(i + 2).start())
+            start_all(back(i))
 
     def gain_copy(step, peer, origin):
         return to_peer(
@@ -1112,15 +1133,13 @@
     reduce.hop(0)
     reduce.send_across(DEPTH)
     gain_first()
-    sum_up(0)
-    sum_up(1)
+    sum_up(0, n_sums // 2)
     reduce.hop(1)
     reduce.send_across(DEPTH + 1)
     gain_second()
-    sum_up(2)
-    sum_up(3)
+    sum_up(n_sums // 2, n_sums - 3)
     reduce.hop(2)
-    sum_up(4)
+    sum_up(n_sums - 3, n_sums)
     reduce.finish()
     for step in range(1, groups):
         gain_group(step, rank, lax.rem(rank + groups - step, groups)).wait_recv()
@@ -1131,10 +1150,9 @@
     source = tokens[...].astype(F32)
     inner = norm_grad(source, inverse_rms(source), gain_row(gains, 0), first[...])
     input_grad[...] = (middle_grad[...] + inner).astype(low)
-    sum_up(5)
     attn_chip().wait()
     total_into(mine, mine, mine_in)
-    start_all(back(n_sums))
+    start_all(back_attn())
     reduce.drain()
     ffn_sum.drain()
     swap().wait_send()
@@ -1144,8 +1162,12 @@
         gain_copy(step, lax.rem(p.me + step, count), p.me).wait_send()
     for step in range(1, groups):
         gain_group(step, lax.rem(rank + step, groups), rank).wait_send()
-    for i in range(n_sums + 1):
+
+    @pl.loop(0, n_sums)
+    def _(i):
         wait_all(back(i))
+
+    wait_all(back_attn())
 
 
 def attention_grad(
@@ -1160,7 +1182,8 @@
     vmem = pltpu.VMEM
     tall = count * rows
     half = hd // 2
-    sums = sums.reshape((-1,) + early.shape)
+    sums = sums.reshape(-1, PIECE, width)
+    early = early.reshape(-1, PIECE, width)
     n_sums, part_rows, _ = sums.shape
     shape = jax.ShapeDtypeStruct
     big = vmem((count, rows, width), low)
@@ -1177,7 +1200,7 @@
             shape((rows, width), low),
             shape((rows, width), low),
             shape(g[1:], F32),
-            shape((n_sums // 2, 4 * part_rows, width), low),
+            shape((3, n_sums // 3 * 2 * part_rows, width), low),
             shape((6 * half, width), low),
         ),
         in_specs=[scalars()] + [vm()] * 7 + [hbm()] * 11,
@@ -1187,7 +1210,7 @@
             big, big, flat, head, head, head, weight, vmem((2, hd, width), low), weight, head, acc, acc,
             flat, flat, flat,
             vmem((2, 2, tall, half), low), vmem((2, tall, half), low), big,
-            vmem((2,) + early.shape, low), vmem(sums.shape, low), vmem((3, half, width), low), third, third, third,
+            vmem((2,) + sums.shape[1:], low), vmem(sums.shape, low), vmem((3, half, width), low), third, third, third,
             vmem(g, F32), vmem(g, F32), vmem(g[1:], F32), vmem((groups,) + g[1:], F32),
         ]
         + gather_sems(count)

time: 444 us -> 443 us (level)
    pallas_call x1, Pallas kernels: 163 us -> 170 us  [attention_grad(): pl.pallas_call(functools.partial(attention_grad_kernel, line, groups, seq...]
    pallas_call x1, Pallas kernels: 149 us -> 144 us  [attention(): pl.pallas_call(functools.partial(attention_kernel, line, groups, seqs), o...]
where the time goes in v6:
time: 443 us
  Pallas kernels  420 us (95%)
  other arithmetic  17.1 us (4%)
  local copies, waits for them, and re-layouts  5.38 us (1%)
    pallas_call x1, Pallas kernels, attention_grad(): pl.pallas_call(functools.partial(attention_grad_kernel, line, groups, seq...  170 us
    pallas_call x1, Pallas kernels, attention(): pl.pallas_call(functools.partial(attention_kernel, line, groups, seqs), o...  144 us
    pallas_call x1, Pallas kernels, ffn(): pl.pallas_call(functools.partial(ffn_kernel, line, groups), out_shape=(sh...  106 us
    convert_element_type x1, other arithmetic, local_heads(): totals[0].astype(f32)  12.5 us

profile of v6, /device:TPU:0, one launch (start us, length us, event | category | flops | bytes accessed | tf_op | source)
XLA Modules:
  0.0 442.8 jit_solution(2706550381377998792)
XLA Ops:
  0.6 1.2 broadcast_in_dim.7.pre_gain
  1.9 1.2 broadcast_in_dim.8.mid_gain
  3.1 0.5 negate_power_fusion.freq
  3.6 143.9 %attention.1 = (f32[128,2048]{1,0:T(8,128)}, f32[8,8,256]{2,1,0:T(8,128)}, bf16[8,128,2048]{2,1,0:T(8,128)(2,1)}, bf16[8,128,2048]{2,1,0:T(8,128)(2,1)}, bf16[2,...) custom-call(s32[2]{0:T(128)} %lengths.3, ...), custom_call_target="tpu_custom_call" | custom-call | tf_op jit(solution)/shard_map/attention/pallas_call | solution.py:660
  147.5 105.7 %ffn.1 = (f32[128,2048]{1,0:T(8,128)}, bf16[8,128,2048]{2,1,0:T(8,128)(2,1)}, bf16[3,512,2048]{2,1,0:T(8,128)(2,1)}, bf16[384,2048]{1,0:T(8,128)(2,1)}) custom-call(bf16[128,2048]{1,0:T(8,128)(2,1)} %bitcast.19, f32[128,2048]{1,0:T(8,128)} %get-tuple-element.31.branch, f32[8,8,256]{2,1,0:T(8,128)} %get-tuple-element.32.gains, ...), custom_call_target="tpu_custom_call" | custom-call | tf_op jit(solution)/shard_map/ffn/pallas_call | solution.py:834
  253.2 169.9 %attention_grad.1 = (bf16[128,2048]{1,0:T(8,128)(2,1)}, bf16[128,2048]{1,0:T(8,128)(2,1)}, f32[8,256]{1,0:T(8,128)}, bf16[3,1024,2048]{2,1,0:T(8,128)(2,1)}, bf16[768,2048]{1,0:T(8,128)(2,1)}) custom-call(s32[2]{0:T(128)} %lengths.3, bf16[128,2048]{1,0:T(8,128)(2,1)} %bitcast.20, f32[128,2048]{1,0:T(8,128)} %get-tuple-element.31.branch, ...), custom_call_target="tpu_custom_call" | custom-call | tf_op jit(solution)/shard_map/attention_grad/pallas_call | solution.py:1197
  423.2 0.0 copy-start
  423.2 12.5 %bitcast_convert_fusion = (f32[1024,2048]{1,0:T(8,128)}, f32[1024,2048]{1,0:T(8,128)}, f32[1024,2048]{1,0:T(8,128)}) fusion(bf16[3,1024,2048]{2,1,0:T(8,128)(2,1)} %get-tuple-element.50), kind=kLoop, calls=%fused_computation | loop fusion | flops 6291456 | bytes 37748736 | tf_op jit(solution)/shard_map/convert_element_type | solution.py:1623
  435.7 0.0 copy-done
  435.7 0.0 copy-start.2
  435.7 0.0 copy-start.1
  435.7 2.5 slice_convert_fusion
  438.3 1.6 slice_convert_fusion.2
  439.8 1.3 fusion
  441.2 0.0 copy-done.2
  441.2 0.8 copy.25
  442.0 0.0 copy-done.1
  442.0 0.8 copy.26
Async XLA Ops:
  423.2 12.5 %copy-start = (bf16[768,2048]{1,0:T(8,128)(2,1)S(1)}, bf16[768,2048]{1,0:T(8,128)(2,1)}, u32[]{:S(2)}) copy-start(bf16[768,2048]{1,0:T(8,128)(2,1)} %get-tuple-element.49) | copy-start | bytes 9437188
  435.7 5.4 %copy-start.2 = (bf16[128,2048]{1,0:T(8,128)(2,1)S(1)}, bf16[128,2048]{1,0:T(8,128)(2,1)}, u32[]{:S(2)}) copy-start(bf16[128,2048]{1,0:T(8,128)(2,1)} %get-tuple-element.46) | copy-start | bytes 1572868
  435.7 6.2 %copy-start.1 = (bf16[128,2048]{1,0:T(8,128)(2,1)S(1)}, bf16[128,2048]{1,0:T(8,128)(2,1)}, u32[]{:S(2)}) copy-start(bf16[128,2048]{1,0:T(8,128)(2,1)} %get-tuple-element.47) | copy-start | bytes 1572868

commit v7 on v6

--- a/solution.py
+++ b/solution.py
@@ -737,8 +737,6 @@
     reduce = Reduce(p, parts, second, scratch[9:])
     for i in range(DEPTH):
         reduce.send_across(i)
-    for i in range(line - 1):
-        reduce.b_hop(i)
 
     units = hidden.shape[1]
     quarter = units // 4
@@ -755,7 +753,7 @@
             stage_recv.at[which, j],
         )
 
-    def gradient(which, left, right):
+    def gradient(which, left, right, between=None):
         def block(q):
             cols = pl.ds(pl.multiple_of(q * quarter, quarter), quarter)
             return t_dot(left[:, cols], right[...].reshape(left.shape[0], -1)).astype(low)
@@ -767,6 +765,9 @@
             stage[j] = block(2 * (1 - core) + j)
             to_partner(which, j).start()
 
+        if between is not None:
+            between()
+
         @pl.loop(0, 2)
         def _(j):
             at = pl.ds(pl.multiple_of(j * quarter, quarter), quarter)
@@ -785,7 +786,11 @@
     def save_pair(which):
         return pltpu.make_async_copy(mine[which], pair_hbm.at[which], out_sem.at[which])
 
-    gradient(0, hidden, cot)
+    def rest_hops():
+        for i in range(line - 1):
+            reduce.b_hop(i)
+
+    gradient(0, hidden, cot, rest_hops)
     reduce.hop(0)
     reduce.send_across(DEPTH)
     add_theirs(0)
@@ -960,23 +965,23 @@
         return to_peer(
             "grp",
             partner,
-            stage.at[b % 3],
-            theirs.at[pl.ds((b % 3) * chunk, chunk)],
-            stage_send.at[b % 3],
-            stage_recv.at[b % 3],
+            stage.at[b // 2],
+            theirs.at[pl.ds(b // 2 * chunk, chunk)],
+            stage_send.at[b // 2],
+            stage_recv.at[b // 2],
         )
 
     def gradient(b, left, right):
         value = t_dot(left, right[...].reshape(left.shape[0], -1)).astype(low)
-        keep = core == b // 3
+        keep = core == b % 2
 
         @pl.when(keep)
         def _():
-            mine[pl.ds((b % 3) * chunk, chunk)] = value
+            mine[pl.ds(b // 2 * chunk, chunk)] = value
 
         @pl.when(jnp.logical_not(keep))
         def _():
-            stage[b % 3] = value
+            stage[b // 2] = value
             to_partner(b).start()
 
     total_slots = q.shape[1]
@@ -1033,6 +1038,40 @@
     gradient(2, dq_rows[:, :chunk], normed)
     gradient(3, dq_rows[:, chunk:], normed)
 
+    spans = (pl.ds(0, 2 * chunk), pl.ds(2 * chunk, chunk))
+
+    def attn_chip(part):
+        return to_peer(
+            "grp",
+            opposite,
+            mine.at[spans[part]],
+            mine_in.at[spans[part]],
+            chip_send.at[n_sums + part],
+            chip_recv.at[n_sums + part],
+        )
+
+    def attn_pair(part, blocks):
+        for b in blocks:
+            to_partner(2 * b).wait_recv()
+        at = mine.at[spans[part]]
+        total_into(at, at, theirs.at[spans[part]])
+        attn_chip(part).start()
+
+    def back_attn(part):
+        size = 2 * chunk if part == 0 else chunk
+        start = core * 3 * chunk + part * 2 * chunk
+        out = attn_hbm.at[pl.ds(pl.multiple_of(start, chunk), size)]
+        at = mine.at[spans[part]]
+        sems = keep_sem.at[n_sums + part], back_send.at[n_sums + part], back_recv.at[n_sums + part]
+        return pltpu.make_async_copy(at, out, sems[0]), to_peer("grp", partner, at, out, *sems[1:])
+
+    def attn_total(part):
+        attn_chip(part).wait()
+        at = mine.at[spans[part]]
+        total_into(at, at, mine_in.at[spans[part]])
+        start_all(back_attn(part))
+
+
     @pl.loop(0, line)
     def _(d):
         at = pl.ds(pl.multiple_of(d * pair, pair), pair)
@@ -1041,29 +1080,17 @@
 
     for i in range(seqs, line - 1):
         ffn_sum.hop(i)
+    attn_pair(0, (0, 1))
+    ffn_sum.finish()
     reduce = Reduce(p, parts, first, scratch[17 + n :])
-    swap().wait_recv()
-
-    def summed(which):
-        return (halves[p.y, which].astype(F32) + half_in[which].astype(F32)).astype(low)
-
-    gradient(4, summed(0), normed)
-    gradient(5, summed(1), normed)
-
-    def attn_chip():
-        return to_peer(
-            "grp", opposite, mine, mine_in, chip_send.at[n_sums], chip_recv.at[n_sums]
-        )
-
-    for b in range(3):
-        to_partner(b).wait_recv()
-    total_into(mine, mine, theirs)
-    attn_chip().start()
-    ffn_sum.finish()
     for i in range(DEPTH):
         reduce.send_across(i)
     for i in range(line - 1):
         reduce.b_hop(i)
+
+    def summed(which):
+        return (halves[p.y, which].astype(F32) + half_in[which].astype(F32)).astype(low)
+
     valid = row_valid(p, lengths, rows)
     result = tokens[...].astype(F32) + branch[...] + ffn_own[...]
     mixed[...] = jnp.where(valid, result, jnp.zeros_like(result)).astype(low)
@@ -1076,13 +1103,6 @@
         return (
             pltpu.make_async_copy(sums_in.at[i], out, keep_sem.at[i]),
             to_peer("grp", partner, sums_in.at[i], out, back_send.at[i], back_recv.at[i]),
-        )
-
-    def back_attn():
-        out = attn_hbm.at[pl.ds(pl.multiple_of(core * 3 * chunk, chunk), 3 * chunk)]
-        return (
-            pltpu.make_async_copy(mine, out, keep_sem.at[n_sums]),
-            to_peer("grp", partner, mine, out, back_send.at[n_sums], back_recv.at[n_sums]),
         )
 
     def sum_up(first_piece, end):
@@ -1130,8 +1150,12 @@
         for step in range(1, groups):
             gain_group(step, lax.rem(rank + step, groups), rank).start()
 
+    swap().wait_recv()
+    gradient(4, summed(0), normed)
+    gradient(5, summed(1), normed)
     reduce.hop(0)
     reduce.send_across(DEPTH)
+    attn_pair(1, (2,))
     gain_first()
     sum_up(0, n_sums // 2)
     reduce.hop(1)
@@ -1140,6 +1164,7 @@
     sum_up(n_sums // 2, n_sums - 3)
     reduce.hop(2)
     sum_up(n_sums - 3, n_sums)
+    attn_total(0)
     reduce.finish()
     for step in range(1, groups):
         gain_group(step, rank, lax.rem(rank + groups - step, groups)).wait_recv()
@@ -1150,14 +1175,12 @@
     source = tokens[...].astype(F32)
     inner = norm_grad(source, inverse_rms(source), gain_row(gains, 0), first[...])
     input_grad[...] = (middle_grad[...] + inner).astype(low)
-    attn_chip().wait()
-    total_into(mine, mine, mine_in)
-    start_all(back_attn())
+    attn_total(1)
     reduce.drain()
     ffn_sum.drain()
     swap().wait_send()
     for b in range(3):
-        to_partner(b).wait_send()
+        to_partner(2 * b).wait_send()
     for step in range(1, count):
         gain_copy(step, lax.rem(p.me + step, count), p.me).wait_send()
     for step in range(1, groups):
@@ -1167,7 +1190,8 @@
     def _(i):
         wait_all(back(i))
 
-    wait_all(back_attn())
+    for part in range(2):
+        wait_all(back_attn(part))
 
 
 def attention_grad(
@@ -1215,8 +1239,8 @@
         ]
         + gather_sems(count)
         + [
-            DMA((12,)), DMA((n_sums + 1,)), DMA((n_sums + 1,)), DMA, DMA, DMA((3,)), DMA((3,)),
-            DMA((n_sums + 1,)), DMA((n_sums + 1,)), DMA((n_sums + 1,)),
+            DMA((12,)), DMA((n_sums + 2,)), DMA((n_sums + 2,)), DMA, DMA, DMA((3,)), DMA((3,)),
+            DMA((n_sums + 2,)), DMA((n_sums + 2,)), DMA((n_sums + 2,)),
             DMA((count,)), DMA((count,)), DMA((groups,)), DMA((groups,)),
         ]
         + Reduce.scratch(line, rows, width, low) * 2,
@@ -1606,17 +1630,16 @@
         groups,
         3,
     )
-    head = query_weight.shape[0]
-    kv_share = key_weight.shape[0]
     f32 = jnp.float32
+    blocks = attn_total.reshape(2, 3, key_weight.shape[0], model_width).astype(f32)
     return (
         mixed.reshape(tokens.shape),
         input_gradient.reshape(tokens.shape),
         gain_own[0],
-        attn_total[head : 2 * head].astype(f32),
-        attn_total[2 * head : 2 * head + kv_share].astype(f32),
-        attn_total[2 * head + kv_share :].astype(f32),
-        attn_total[:head].astype(f32),
+        blocks[:, 1].reshape(query_weight.shape),
+        blocks[0, 2],
+        blocks[1, 2],
+        blocks[:, 0].reshape(out_weight.shape),
         gain_own[1],
         totals[1].astype(f32),
         totals[2].astype(f32),

time: 443 us -> 437 us (0.986)
  Pallas kernels: 420 us -> 412 us
    pallas_call x1, Pallas kernels: 170 us -> 159 us  [attention_grad(): pl.pallas_call(functools.partial(attention_grad_kernel, line, groups, seq...]
where the time goes in v7:
time: 437 us; the launch traced here: 436 us
  Pallas kernels  412 us (94%)
  other arithmetic  13.9 us (3%)
  local copies, waits for them, and re-layouts  9.46 us (2%)
    pallas_call x1, Pallas kernels, attention_grad(): pl.pallas_call(functools.partial(attention_grad_kernel, line, groups, seq...  159 us
    pallas_call x1, Pallas kernels, attention(): pl.pallas_call(functools.partial(attention_kernel, line, groups, seqs), o...  144 us
    pallas_call x1, Pallas kernels, ffn(): pl.pallas_call(functools.partial(ffn_kernel, line, groups), out_shape=(sh...  109 us
    convert_element_type x1, other arithmetic, local_heads(): totals[0].astype(f32)  12.5 us

profile of v7, /device:TPU:0, one launch (start us, length us, event | category | flops | bytes accessed | tf_op | source)
XLA Modules:
  0.0 436.5 jit_solution(16302944422504229226)
XLA Ops:
  0.6 1.2 broadcast_in_dim.7.pre_gain
  1.9 1.2 broadcast_in_dim.8.mid_gain
  3.1 0.5 negate_power_fusion.freq
  3.6 144.1 %attention.1 = (f32[128,2048]{1,0:T(8,128)}, f32[8,8,256]{2,1,0:T(8,128)}, bf16[8,128,2048]{2,1,0:T(8,128)(2,1)}, bf16[8,128,2048]{2,1,0:T(8,128)(2,1)}, bf16[2,...) custom-call(s32[2]{0:T(128)} %lengths.3, ...), custom_call_target="tpu_custom_call" | custom-call | tf_op jit(solution)/shard_map/attention/pallas_call | solution.py:660
  147.7 109.2 %ffn.1 = (f32[128,2048]{1,0:T(8,128)}, bf16[8,128,2048]{2,1,0:T(8,128)(2,1)}, bf16[3,512,2048]{2,1,0:T(8,128)(2,1)}, bf16[384,2048]{1,0:T(8,128)(2,1)}) custom-call(bf16[128,2048]{1,0:T(8,128)(2,1)} %bitcast.29, f32[128,2048]{1,0:T(8,128)} %get-tuple-element.31.branch, f32[8,8,256]{2,1,0:T(8,128)} %get-tuple-element.32.gains, ...), custom_call_target="tpu_custom_call" | custom-call | tf_op jit(solution)/shard_map/ffn/pallas_call | solution.py:839
  257.0 159.1 %attention_grad.1 = (bf16[128,2048]{1,0:T(8,128)(2,1)}, bf16[128,2048]{1,0:T(8,128)(2,1)}, f32[8,256]{1,0:T(8,128)}, bf16[3,1024,2048]{2,1,0:T(8,128)(2,1)}, bf16[768,2048]{1,0:T(8,128)(2,1)}) custom-call(s32[2]{0:T(128)} %lengths.3, bf16[128,2048]{1,0:T(8,128)(2,1)} %bitcast.30, f32[128,2048]{1,0:T(8,128)} %get-tuple-element.31.branch, ...), custom_call_target="tpu_custom_call" | custom-call | tf_op jit(solution)/shard_map/attention_grad/pallas_call | solution.py:1221
  416.1 0.0 copy-start
  416.1 12.5 %bitcast_convert_fusion = (f32[1024,2048]{1,0:T(8,128)}, f32[1024,2048]{1,0:T(8,128)}, f32[1024,2048]{1,0:T(8,128)}) fusion(bf16[3,1024,2048]{2,1,0:T(8,128)(2,1)} %get-tuple-element.50), kind=kLoop, calls=%fused_computation | loop fusion | flops 6291456 | bytes 37748736 | tf_op jit(solution)/shard_map/convert_element_type | solution.py:1646
  428.6 0.0 copy-done
  428.6 0.8 convert.4
  429.4 1.5 slice_bitcast_fusion
  431.0 0.0 copy-start.2
  431.0 0.0 copy-start.1
  431.0 2.5 fusion
  433.5 1.3 fusion.1
  434.9 0.0 copy-done.2
  434.9 0.8 copy.25
  435.7 0.0 copy-done.1
  435.7 0.8 copy.26
Async XLA Ops:
  416.1 12.5 %copy-start = (bf16[768,2048]{1,0:T(8,128)(2,1)S(1)}, bf16[768,2048]{1,0:T(8,128)(2,1)}, u32[]{:S(2)}) copy-start(bf16[768,2048]{1,0:T(8,128)(2,1)} %get-tuple-element.49) | copy-start | bytes 9437188
  431.0 3.9 copy-start.2
  431.0 4.7 %copy-start.1 = (bf16[128,2048]{1,0:T(8,128)(2,1)S(1)}, bf16[128,2048]{1,0:T(8,128)(2,1)}, u32[]{:S(2)}) copy-start(bf16[128,2048]{1,0:T(8,128)(2,1)} %get-tuple-element.47) | copy-start | bytes 1572868

commit v8 on v7

--- a/solution.py
+++ b/solution.py
@@ -7,6 +7,7 @@
 from jax.experimental import pallas as pl
 from jax.experimental.pallas import tpu as pltpu
 from jax.sharding import PartitionSpec as P
+import numpy as np
 
 NH = 8
 KVH = 4
@@ -286,28 +287,31 @@
         either(d < p.z, lambda: go(False))
 
     def hop(self, i):
+        for c in range(CHUNKS):
+            self.step(i, c)
+
+    def step(self, i, c):
         p = self.p
         d = p.far(i)
-        for c in range(CHUNKS):
-            self.cross_copy(d, c).wait_recv()
-            at = self.pieces[c]
-            mine = self.parts.at[2 * d + p.y, at]
-            held = self.cross_in.at[d, at]
-
-            def go(up):
-                first = p.low_end if up else p.high_end
-                came = self.up_in if up else self.down_in
-                either(first, lambda: total_into(held, mine, held))
-
-                @pl.when(jnp.logical_not(first))
-                def _():
-                    self.line_copy(up, d, c).wait_recv()
-                    total_into(held, mine, held, came.at[d, at])
-
-                self.line_copy(up, d, c).start()
-
-            either(d > p.z, lambda: go(True))
-            either(d < p.z, lambda: go(False))
+        self.cross_copy(d, c).wait_recv()
+        at = self.pieces[c]
+        mine = self.parts.at[2 * d + p.y, at]
+        held = self.cross_in.at[d, at]
+
+        def go(up):
+            first = p.low_end if up else p.high_end
+            came = self.up_in if up else self.down_in
+            either(first, lambda: total_into(held, mine, held))
+
+            @pl.when(jnp.logical_not(first))
+            def _():
+                self.line_copy(up, d, c).wait_recv()
+                total_into(held, mine, held, came.at[d, at])
+
+            self.line_copy(up, d, c).start()
+
+        either(d > p.z, lambda: go(True))
+        either(d < p.z, lambda: go(False))
 
     def close(self, dst, mine, ups, downs):
         p = self.p
@@ -491,8 +495,8 @@
     p.greet(groups)
 
     small[...] = jnp.zeros_like(small)
-    small[0:1] = pre_gain[...].astype(F32)
-    small[1:2] = mid_gain[...].astype(F32)
+    small[0:1] = pre_gain[...].astype(F32)[None, :]
+    small[1:2] = mid_gain[...].astype(F32)[None, :]
 
     def small_copy(step, peer, origin):
         return to_peer(
@@ -647,7 +651,7 @@
     rows, width = own.shape
     seqs = lengths.shape[0]
     total_slots = count * rows // seqs
-    small = (8, pre_gain.shape[1])
+    small = (8, pre_gain.shape[0])
     line = count // 2
     low = own.dtype
     v = pltpu.VMEM
@@ -690,7 +694,7 @@
     line, groups,
     tokens, branch, gains, cot_hbm, gate_hbm, up_hbm, down_hbm,
     second, ffn_hbm, pair_hbm, chip_in,
-    own, normed, cot, gate_w, up_w, down_w, hidden, gate_g, up_g, parts, stage, theirs,
+    own, rights, gate_up, down_w, lefts, parts, stage, theirs,
     *scratch,
 ):
     p = Place(line)
@@ -699,6 +703,10 @@
     partner = rank + 1 - 2 * core
     opposite = lax.rem(rank + 2, groups)
     (load_sem, out_sem, stage_send, stage_recv, chip_send, chip_recv) = scratch[3:9]
+    units = down_w.shape[0]
+    gate_w, up_w = gate_up.at[pl.ds(0, units)], gate_up.at[pl.ds(units, units)]
+    cot, normed = rights.at[0], rights.at[1]
+    hidden, gate_g, up_g = lefts.at[0], lefts.at[1], lefts.at[2]
     loads = [
         pltpu.make_async_copy(src, dst, load_sem.at[i])
         for i, (src, dst) in enumerate(
@@ -738,71 +746,70 @@
     for i in range(DEPTH):
         reduce.send_across(i)
 
-    units = hidden.shape[1]
+    for i in range(line - 1):
+        reduce.b_hop(i)
+
     quarter = units // 4
     half = units // 2
-    mine = (up_w.at[pl.ds(0, half)], gate_w.at[pl.ds(0, half)], gate_w.at[pl.ds(half, half)])
+
+    def mine(which):
+        start = lax.rem(which + 2, 3) * half
+        return gate_up.at[pl.ds(pl.multiple_of(start, half), half)]
 
     def to_partner(which, j):
         return to_peer(
             "grp",
             partner,
             stage.at[j],
-            theirs.at[which, pl.ds(j * quarter, quarter)],
+            theirs.at[which, pl.ds(pl.multiple_of(j * quarter, quarter), quarter)],
             stage_send.at[j],
             stage_recv.at[which, j],
         )
 
-    def gradient(which, left, right, between=None):
+    def chip_copy():
+        return to_peer(
+            "grp",
+            opposite,
+            gate_up.at[pl.ds(2 * half, chip_in.shape[0])],
+            chip_in,
+            chip_send,
+            chip_recv,
+        )
+
+    def save_pair(which):
+        return pltpu.make_async_copy(mine(which), pair_hbm.at[which], out_sem.at[which])
+
+    @pl.loop(0, 3)
+    def _(which):
+        right = rights.at[jnp.minimum(which, 1)]
+
         def block(q):
             cols = pl.ds(pl.multiple_of(q * quarter, quarter), quarter)
-            return t_dot(left[:, cols], right[...].reshape(left.shape[0], -1)).astype(low)
+            left = lefts[which, :, cols]
+            return t_dot(left, right[...].reshape(left.shape[0], -1)).astype(low)
 
         @pl.loop(0, 2)
         def _(j):
-            if which:
-                to_partner(which - 1, j).wait_send()
+            either(which > 0, lambda: to_partner(which - 1, j).wait_send())
             stage[j] = block(2 * (1 - core) + j)
             to_partner(which, j).start()
 
-        if between is not None:
-            between()
+        reduce.step(which, 0)
 
         @pl.loop(0, 2)
         def _(j):
             at = pl.ds(pl.multiple_of(j * quarter, quarter), quarter)
-            mine[which][at] = block(2 * core + j)
-
-    def add_theirs(which):
+            mine(which)[at] = block(2 * core + j)
+
+        for c in range(1, CHUNKS):
+            reduce.step(which, c)
+        either(which + DEPTH < line, lambda: reduce.send_across(which + DEPTH))
         for j in range(2):
             to_partner(which, j).wait_recv()
-        total_into(mine[which], mine[which], theirs.at[which])
-
-    def chip_copy():
-        return to_peer(
-            "grp", opposite, mine[0].at[pl.ds(0, chip_in.shape[0])], chip_in, chip_send, chip_recv
-        )
-
-    def save_pair(which):
-        return pltpu.make_async_copy(mine[which], pair_hbm.at[which], out_sem.at[which])
-
-    def rest_hops():
-        for i in range(line - 1):
-            reduce.b_hop(i)
-
-    gradient(0, hidden, cot, rest_hops)
-    reduce.hop(0)
-    reduce.send_across(DEPTH)
-    add_theirs(0)
-    chip_copy().start()
-    save_pair(0).start()
-    gradient(1, gate_g, normed)
-    reduce.hop(1)
-    reduce.send_across(DEPTH + 1)
-    add_theirs(1)
-    save_pair(1).start()
-    gradient(2, up_g, normed)
-    reduce.hop(2)
+        total_into(mine(which), mine(which), theirs.at[which])
+        either(which == 0, lambda: chip_copy().start())
+        save_pair(which).start()
+
     gather.drain()
 
     @pl.loop(0, line)
@@ -812,8 +819,6 @@
 
     ffn_save = pltpu.make_async_copy(normed, ffn_hbm, out_sem.at[3])
     ffn_save.start()
-    add_theirs(2)
-    save_pair(2).start()
     reduce.finish()
     for j in range(2):
         to_partner(2, j).wait_send()
@@ -847,10 +852,8 @@
         in_specs=[vm()] * 3 + [hbm()] * 4,
         out_specs=(vm(), hbm(), hbm(), hbm()),
         scratch_shapes=[v((rows, width), low)]
-        + [v(big, low)] * 2
-        + [v((units, width), low)] * 3
-        + [v((tall, units), low)] * 3
-        + [v(big, low), v((2, units // 4, width), low), v((3,) + half, low)]
+        + [v((2,) + big, low), v((2 * units, width), low), v((units, width), low)]
+        + [v((3, tall, units), low), v(big, low), v((2, units // 4, width), low), v((3,) + half, low)]
         + gather_sems(count)
         + [DMA((4,)), DMA((4,)), DMA((2,)), DMA((3, 2)), DMA, DMA]
         + Reduce.scratch(line, rows, width, low),
@@ -1584,7 +1587,7 @@
     groups = lax.axis_size("grp")
     seqs, seq_dev, model_width = tokens.shape
     rows = seqs * seq_dev
-    inverse_freq = theta_base ** (-(jnp.arange(0, HD, 2).astype(jnp.float32) / HD))
+    inverse_freq = jnp.asarray(theta_base ** (-np.arange(0, HD, 2) / HD), jnp.float32)
     tokens_low = tokens.reshape(rows, model_width)
     cot_low = cotangent.reshape(rows, model_width)
     branch, gains, normed_first, cot_all, queries, keys, values, attended, kv_head, cosine, sine = (
@@ -1592,8 +1595,8 @@
             lengths,
             tokens_low,
             cot_low,
-            prenorm_gain[None, :],
-            midnorm_gain[None, :],
+            prenorm_gain,
+            midnorm_gain,
             inverse_freq[None, :],
             query_weight,
             key_weight,

time: 437 us -> 432 us (0.989)
  no operation moved by 1% of the time
where the time goes in v8:
time: 432 us; the launch traced here: 431 us
  Pallas kernels  410 us (95%)
  other arithmetic  13.3 us (3%)
  local copies, waits for them, and re-layouts  7.02 us (2%)
    pallas_call x1, Pallas kernels, attention_grad(): pl.pallas_call(functools.partial(attention_grad_kernel, line, groups, seq...  160 us
    pallas_call x1, Pallas kernels, attention(): pl.pallas_call(functools.partial(attention_kernel, line, groups, seqs), o...  144 us
    pallas_call x1, Pallas kernels, ffn(): pl.pallas_call(functools.partial(ffn_kernel, line, groups), out_shape=(sh...  105 us
    convert_element_type x1, other arithmetic, local_heads(): totals[0].astype(f32)  12.5 us

profile of v8, /device:TPU:0, one launch (start us, length us, event | category | flops | bytes accessed | tf_op | source)
XLA Modules:
  0.0 430.7 jit_solution(9902218020063776520)
XLA Ops:
  0.6 144.1 %attention.1 = (f32[128,2048]{1,0:T(8,128)}, f32[8,8,256]{2,1,0:T(8,128)}, bf16[8,128,2048]{2,1,0:T(8,128)(2,1)}, bf16[8,128,2048]{2,1,0:T(8,128)(2,1)}, bf16[2,...) custom-call(s32[2]{0:T(128)} %lengths.3, ...), custom_call_target="tpu_custom_call" | custom-call | tf_op jit(solution)/shard_map/attention/pallas_call | solution.py:664
  144.8 105.0 %ffn.1 = (f32[128,2048]{1,0:T(8,128)}, bf16[8,128,2048]{2,1,0:T(8,128)(2,1)}, bf16[3,512,2048]{2,1,0:T(8,128)(2,1)}, bf16[384,2048]{1,0:T(8,128)(2,1)}) custom-call(bf16[128,2048]{1,0:T(8,128)(2,1)} %bitcast.29, f32[128,2048]{1,0:T(8,128)} %get-tuple-element.31.branch, f32[8,8,256]{2,1,0:T(8,128)} %get-tuple-element.32.gains, ...), custom_call_target="tpu_custom_call" | custom-call | tf_op jit(solution)/shard_map/ffn/pallas_call | solution.py:844
  249.8 160.5 %attention_grad.1 = (bf16[128,2048]{1,0:T(8,128)(2,1)}, bf16[128,2048]{1,0:T(8,128)(2,1)}, f32[8,256]{1,0:T(8,128)}, bf16[3,1024,2048]{2,1,0:T(8,128)(2,1)}, bf16[768,2048]{1,0:T(8,128)(2,1)}) custom-call(s32[2]{0:T(128)} %lengths.3, bf16[128,2048]{1,0:T(8,128)(2,1)} %bitcast.30, f32[128,2048]{1,0:T(8,128)} %get-tuple-element.31.branch, ...), custom_call_target="tpu_custom_call" | custom-call | tf_op jit(solution)/shard_map/attention_grad/pallas_call | solution.py:1224
  410.3 0.0 copy-start
  410.3 12.5 %bitcast_convert_fusion = (f32[1024,2048]{1,0:T(8,128)}, f32[1024,2048]{1,0:T(8,128)}, f32[1024,2048]{1,0:T(8,128)}) fusion(bf16[3,1024,2048]{2,1,0:T(8,128)(2,1)} %get-tuple-element.50), kind=kLoop, calls=%fused_computation | loop fusion | flops 6291456 | bytes 37748736 | tf_op jit(solution)/shard_map/convert_element_type | solution.py:1649
  422.8 0.0 copy-done
  422.8 0.8 convert.4
  423.7 1.5 slice_bitcast_fusion
  425.2 0.0 copy-start.2
  425.2 0.0 copy-start.1
  425.2 2.5 fusion
  427.7 1.3 fusion.1
  429.1 0.0 copy-done.2
  429.1 0.8 copy.26
  429.9 0.0 copy-done.1
  429.9 0.8 copy.27
Async XLA Ops:
  410.3 12.5 %copy-start = (bf16[768,2048]{1,0:T(8,128)(2,1)S(1)}, bf16[768,2048]{1,0:T(8,128)(2,1)}, u32[]{:S(2)}) copy-start(bf16[768,2048]{1,0:T(8,128)(2,1)} %get-tuple-element.49) | copy-start | bytes 9437188
  425.2 3.9 copy-start.2
  425.2 4.7 %copy-start.1 = (bf16[128,2048]{1,0:T(8,128)(2,1)S(1)}, bf16[128,2048]{1,0:T(8,128)(2,1)}, u32[]{:S(2)}) copy-start(bf16[128,2048]{1,0:T(8,128)(2,1)} %get-tuple-element.47) | copy-start | bytes 1572868

commit v9 on v8

--- a/solution.py
+++ b/solution.py
@@ -743,11 +743,8 @@
         parts[pl.ds(2 * d, 2)] = part.astype(low).reshape(2, rows, -1)
 
     reduce = Reduce(p, parts, second, scratch[9:])
-    for i in range(DEPTH):
+    for i in range(line):
         reduce.send_across(i)
-
-    for i in range(line - 1):
-        reduce.b_hop(i)
 
     quarter = units // 4
     half = units // 2
@@ -794,21 +791,34 @@
             stage[j] = block(2 * (1 - core) + j)
             to_partner(which, j).start()
 
-        reduce.step(which, 0)
+        @pl.when(which == 0)
+        def _():
+            for i in range(line - 1):
+                reduce.b_hop(i)
+
+        at_end = p.low_end | p.high_end
+        either(at_end, lambda: reduce.step(which, 0))
 
         @pl.loop(0, 2)
         def _(j):
             at = pl.ds(pl.multiple_of(j * quarter, quarter), quarter)
             mine(which)[at] = block(2 * core + j)
 
-        for c in range(1, CHUNKS):
-            reduce.step(which, c)
-        either(which + DEPTH < line, lambda: reduce.send_across(which + DEPTH))
+        @pl.when(at_end)
+        def _():
+            for c in range(1, CHUNKS):
+                reduce.step(which, c)
+
         for j in range(2):
             to_partner(which, j).wait_recv()
         total_into(mine(which), mine(which), theirs.at[which])
         either(which == 0, lambda: chip_copy().start())
         save_pair(which).start()
+
+        @pl.when(jnp.logical_not(at_end))
+        def _():
+            for c in range(CHUNKS):
+                reduce.step(which, c)
 
     gather.drain()
 

time: 432 us -> 427 us (0.988)
    pallas_call x1, Pallas kernels: 160 us -> 152 us  [attention_grad(): pl.pallas_call(functools.partial(attention_grad_kernel, line, groups, seq...]
    pallas_call x1, Pallas kernels: 105 us -> 109 us  [ffn(): pl.pallas_call(functools.partial(ffn_kernel, line, groups), out_shape=(sh...]
where the time goes in v9:
time: 427 us
  Pallas kernels  406 us (95%)
  other arithmetic  13.3 us (3%)
  local copies, waits for them, and re-layouts  7.02 us (2%)
    pallas_call x1, Pallas kernels, attention_grad(): pl.pallas_call(functools.partial(attention_grad_kernel, line, groups, seq...  152 us
    pallas_call x1, Pallas kernels, attention(): pl.pallas_call(functools.partial(attention_kernel, line, groups, seqs), o...  144 us
    pallas_call x1, Pallas kernels, ffn(): pl.pallas_call(functools.partial(ffn_kernel, line, groups), out_shape=(sh...  109 us
    convert_element_type x1, other arithmetic, local_heads(): totals[0].astype(f32)  12.5 us

profile of v9, /device:TPU:0, one launch (start us, length us, event | category | flops | bytes accessed | tf_op | source)
XLA Modules:
  0.0 426.8 jit_solution(5832670180728045967)
XLA Ops:
  0.6 144.1 %attention.1 = (f32[128,2048]{1,0:T(8,128)}, f32[8,8,256]{2,1,0:T(8,128)}, bf16[8,128,2048]{2,1,0:T(8,128)(2,1)}, bf16[8,128,2048]{2,1,0:T(8,128)(2,1)}, bf16[2,...) custom-call(s32[2]{0:T(128)} %lengths.3, ...), custom_call_target="tpu_custom_call" | custom-call | tf_op jit(solution)/shard_map/attention/pallas_call | solution.py:664
  144.8 109.4 %ffn.1 = (f32[128,2048]{1,0:T(8,128)}, bf16[8,128,2048]{2,1,0:T(8,128)(2,1)}, bf16[3,512,2048]{2,1,0:T(8,128)(2,1)}, bf16[384,2048]{1,0:T(8,128)(2,1)}) custom-call(bf16[128,2048]{1,0:T(8,128)(2,1)} %bitcast.29, f32[128,2048]{1,0:T(8,128)} %get-tuple-element.31.branch, f32[8,8,256]{2,1,0:T(8,128)} %get-tuple-element.32.gains, ...), custom_call_target="tpu_custom_call" | custom-call | tf_op jit(solution)/shard_map/ffn/pallas_call | solution.py:854
  254.2 152.2 %attention_grad.1 = (bf16[128,2048]{1,0:T(8,128)(2,1)}, bf16[128,2048]{1,0:T(8,128)(2,1)}, f32[8,256]{1,0:T(8,128)}, bf16[3,1024,2048]{2,1,0:T(8,128)(2,1)}, bf16[768,2048]{1,0:T(8,128)(2,1)}) custom-call(s32[2]{0:T(128)} %lengths.3, bf16[128,2048]{1,0:T(8,128)(2,1)} %bitcast.30, f32[128,2048]{1,0:T(8,128)} %get-tuple-element.31.branch, ...), custom_call_target="tpu_custom_call" | custom-call | tf_op jit(solution)/shard_map/attention_grad/pallas_call | solution.py:1234
  406.4 0.0 copy-start
  406.4 12.5 %bitcast_convert_fusion = (f32[1024,2048]{1,0:T(8,128)}, f32[1024,2048]{1,0:T(8,128)}, f32[1024,2048]{1,0:T(8,128)}) fusion(bf16[3,1024,2048]{2,1,0:T(8,128)(2,1)} %get-tuple-element.50), kind=kLoop, calls=%fused_computation | loop fusion | flops 6291456 | bytes 37748736 | tf_op jit(solution)/shard_map/convert_element_type | solution.py:1659
  418.9 0.0 copy-done
  418.9 0.8 convert.4
  419.8 1.5 slice_bitcast_fusion
  421.3 0.0 copy-start.2
  421.3 0.0 copy-start.1
  421.3 2.5 fusion
  423.9 1.3 fusion.1
  425.2 0.0 copy-done.2
  425.2 0.8 copy.26
  426.0 0.0 copy-done.1
  426.0 0.8 copy.27
Async XLA Ops:
  406.4 12.5 %copy-start = (bf16[768,2048]{1,0:T(8,128)(2,1)S(1)}, bf16[768,2048]{1,0:T(8,128)(2,1)}, u32[]{:S(2)}) copy-start(bf16[768,2048]{1,0:T(8,128)(2,1)} %get-tuple-element.49) | copy-start | bytes 9437188
  421.3 3.9 copy-start.2
  421.3 4.7 %copy-start.1 = (bf16[128,2048]{1,0:T(8,128)(2,1)S(1)}, bf16[128,2048]{1,0:T(8,128)(2,1)}, u32[]{:S(2)}) copy-start(bf16[128,2048]{1,0:T(8,128)(2,1)} %get-tuple-element.47) | copy-start | bytes 1572868

commit v10 on v9

--- a/solution.py
+++ b/solution.py
@@ -24,9 +24,9 @@
 CHUNKS = 2
 
 
-def pieces(rows):
-    size = -(-(rows - REST) // (16 * CHUNKS)) * 16
-    cuts = [min(i * size, rows - REST) for i in range(CHUNKS + 1)] + [rows]
+def pieces(rows, rest=REST):
+    size = -(-(rows - rest) // (16 * CHUNKS)) * 16
+    cuts = [min(i * size, rows - rest) for i in range(CHUNKS + 1)] + [rows]
     return [pl.ds(a, b - a) for a, b in zip(cuts, cuts[1:])]
 
 
@@ -102,10 +102,10 @@
 class Gather:
     UP, DOWN, CROSS = 0, 1, 2
 
-    def __init__(self, place, own, out, local_sem, send_sem, recv_sem):
+    def __init__(self, place, own, out, local_sem, send_sem, recv_sem, rest=REST):
         self.p, self.own, self.out = place, own, out
         self.local_sem, self.send_sem, self.recv_sem = local_sem, send_sem, recv_sem
-        self.pieces = pieces(own.shape[0])
+        self.pieces = pieces(own.shape[0], rest)
         self.last = len(self.pieces) - 1
 
     def copy(self, way, origin, part, own=False):
@@ -505,7 +505,7 @@
 
     for step in range(1, count):
         small_copy(step, lax.rem(p.me + step, count), p.me).start()
-    gather = Gather(p, own, rows_all, *g1)
+    gather = Gather(p, own, rows_all, *g1, rest=2 * REST)
     gather.start()
     cots = Gather(p, cot_own, cot_all, *g2)
     small_out[p.me] = small[...]
@@ -724,23 +724,34 @@
     pair = 2 * rows
     low = own.dtype
 
-    @pl.loop(0, line)
+    def branch_rows(block, count):
+        size = count * rows
+        x = normed[pl.ds(block, count)].reshape(size, -1)
+        g = dot_t(x, gate_w[...])
+        u = dot_t(x, up_w[...])
+        dh = dot_t(cot[pl.ds(block, count)].reshape(size, -1), down_w[...])
+        s = 1.0 / (1.0 + jnp.exp(-g))
+        silu = g * s
+        at = pl.ds(pl.multiple_of(block * rows, rows), size)
+        hidden[at] = (silu * u).astype(low)
+        up_g[at] = (dh * silu).astype(low)
+        gate_g[at] = (dh * u * s * (1.0 + g * (1.0 - s))).astype(low)
+        part = dot(gate_g[at], gate_w[...]) + dot(up_g[at], up_w[...])
+        parts[pl.ds(block, count)] = part.astype(low).reshape(count, rows, -1)
+
+    @pl.loop(0, line - 1)
     def _(i):
         gather.hop(i + 1)
         d = p.near(i)
         gather.whole(d)
-        x = normed[pl.ds(2 * d, 2)].reshape(pair, -1)
-        g = dot_t(x, gate_w[...])
-        u = dot_t(x, up_w[...])
-        dh = dot_t(cot[pl.ds(2 * d, 2)].reshape(pair, -1), down_w[...])
-        s = 1.0 / (1.0 + jnp.exp(-g))
-        silu = g * s
-        at = pl.ds(pl.multiple_of(d * pair, pair), pair)
-        hidden[at] = (silu * u).astype(low)
-        up_g[at] = (dh * silu).astype(low)
-        gate_g[at] = (dh * u * s * (1.0 + g * (1.0 - s))).astype(low)
-        part = dot(gate_g[at], gate_w[...]) + dot(up_g[at], up_w[...])
-        parts[pl.ds(2 * d, 2)] = part.astype(low).reshape(2, rows, -1)
+        branch_rows(2 * d, 2)
+
+    last = p.far(0)
+
+    @pl.loop(0, 2)
+    def _(i):
+        either(i == 1, lambda: gather.whole(last))
+        branch_rows(2 * last + lax.rem(p.y + i, 2), 1)
 
     reduce = Reduce(p, parts, second, scratch[9:])
     for i in range(line):
@@ -876,7 +887,7 @@
     line, groups, seqs,
     lengths, tokens, branch, cot, second, gains, cosine, sine,
     ffn_hbm, normed_hbm, attended_hbm, q_hbm, k_hbm, v_hbm, wq_hbm, wkv_hbm, wo_hbm, sums_hbm, early_hbm,
-    mixed, input_grad, gain_out, total_hbm, attn_hbm,
+    mixed, input_grad, gain_out, total_hbm, wide_hbm, narrow_hbm,
     own, middle_grad, first, ffn_own, dbranch, normed, attended, q, k, v, wq, wkv, wo, da, dk_acc, dv_acc, dq_rows, dk_rows, dv_rows,
     halves, half_in, ffn_parts, sums, sums_in, stage, mine, theirs, mine_in, gain_held, gain_in, gain_sum, gain_all,
     *scratch,
@@ -1070,19 +1081,22 @@
         total_into(at, at, theirs.at[spans[part]])
         attn_chip(part).start()
 
-    def back_attn(part):
-        size = 2 * chunk if part == 0 else chunk
-        start = core * 3 * chunk + part * 2 * chunk
-        out = attn_hbm.at[pl.ds(pl.multiple_of(start, chunk), size)]
-        at = mine.at[spans[part]]
-        sems = keep_sem.at[n_sums + part], back_send.at[n_sums + part], back_recv.at[n_sums + part]
+    def back_attn(slot):
+        if slot < 2:
+            out = wide_hbm.at[slot, pl.ds(pl.multiple_of(core * chunk, chunk), chunk)]
+        else:
+            out = narrow_hbm.at[core]
+        at = mine.at[pl.ds(slot * chunk, chunk)]
+        n_slot = n_sums + slot
+        sems = keep_sem.at[n_slot], back_send.at[n_slot], back_recv.at[n_slot]
         return pltpu.make_async_copy(at, out, sems[0]), to_peer("grp", partner, at, out, *sems[1:])
 
     def attn_total(part):
         attn_chip(part).wait()
         at = mine.at[spans[part]]
         total_into(at, at, mine_in.at[spans[part]])
-        start_all(back_attn(part))
+        for slot in (0, 1) if part == 0 else (2,):
+            start_all(back_attn(slot))
 
 
     @pl.loop(0, line)
@@ -1203,8 +1217,8 @@
     def _(i):
         wait_all(back(i))
 
-    for part in range(2):
-        wait_all(back_attn(part))
+    for slot in range(3):
+        wait_all(back_attn(slot))
 
 
 def attention_grad(
@@ -1238,10 +1252,11 @@
             shape((rows, width), low),
             shape(g[1:], F32),
             shape((3, n_sums // 3 * 2 * part_rows, width), low),
-            shape((6 * half, width), low),
+            shape((2, 2 * half, width), low),
+            shape((2, half, width), low),
         ),
         in_specs=[scalars()] + [vm()] * 7 + [hbm()] * 11,
-        out_specs=(vm(), vm(), vm(), hbm(), hbm()),
+        out_specs=(vm(), vm(), vm(), hbm(), hbm(), hbm()),
         scratch_shapes=[
             vmem((rows, width), low), block, block, block,
             big, big, flat, head, head, head, weight, vmem((2, hd, width), low), weight, head, acc, acc,
@@ -1253,7 +1268,7 @@
         + gather_sems(count)
         + [
             DMA((12,)), DMA((n_sums + 2,)), DMA((n_sums + 2,)), DMA, DMA, DMA((3,)), DMA((3,)),
-            DMA((n_sums + 2,)), DMA((n_sums + 2,)), DMA((n_sums + 2,)),
+            DMA((n_sums + 3,)), DMA((n_sums + 3,)), DMA((n_sums + 3,)),
             DMA((count,)), DMA((count,)), DMA((groups,)), DMA((groups,)),
         ]
         + Reduce.scratch(line, rows, width, low) * 2,
@@ -1620,7 +1635,7 @@
     second_grad, ffn_parts, pair_sums, early = ffn(
         tokens_low, branch, gains, cot_all, gate_weight, up_weight, down_weight, groups, 2
     )
-    mixed, input_gradient, gain_own, totals, attn_total = attention_grad(
+    mixed, input_gradient, gain_own, totals, wide, narrow = attention_grad(
         lengths,
         tokens_low,
         branch,
@@ -1644,15 +1659,14 @@
         3,
     )
     f32 = jnp.float32
-    blocks = attn_total.reshape(2, 3, key_weight.shape[0], model_width).astype(f32)
     return (
         mixed.reshape(tokens.shape),
         input_gradient.reshape(tokens.shape),
         gain_own[0],
-        blocks[:, 1].reshape(query_weight.shape),
-        blocks[0, 2],
-        blocks[1, 2],
-        blocks[:, 0].reshape(out_weight.shape),
+        wide[1].astype(f32),
+        narrow[0].astype(f32),
+        narrow[1].astype(f32),
+        wide[0].astype(f32),
         gain_own[1],
         totals[1].astype(f32),
         totals[2].astype(f32),

time: 427 us -> 428 us (level)
    pallas_call x1, Pallas kernels: 109 us -> 114 us  [ffn(): pl.pallas_call(functools.partial(ffn_kernel, line, groups), out_shape=(sh...]
where the time goes in v10:
time: 428 us
  Pallas kernels  408 us (95%)
  other arithmetic  16.2 us (4%)
    pallas_call x1, Pallas kernels, attention_grad(): pl.pallas_call(functools.partial(attention_grad_kernel, line, groups, seq...  152 us
    pallas_call x1, Pallas kernels, attention(): pl.pallas_call(functools.partial(attention_kernel, line, groups, seqs), o...  141 us
    pallas_call x1, Pallas kernels, ffn(): pl.pallas_call(functools.partial(ffn_kernel, line, groups), out_shape=(sh...  114 us
    convert_element_type x1, other arithmetic, local_heads(): totals[0].astype(f32)  12.1 us

profile of v10, /device:TPU:0, one launch (start us, length us, event | category | flops | bytes accessed | tf_op | source)
XLA Modules:
  0.0 427.7 jit_solution(8234245549808427569)
XLA Ops:
  0.6 141.4 %attention.1 = (f32[128,2048]{1,0:T(8,128)}, f32[8,8,256]{2,1,0:T(8,128)}, bf16[8,128,2048]{2,1,0:T(8,128)(2,1)}, bf16[8,128,2048]{2,1,0:T(8,128)(2,1)}, bf16[2,...) custom-call(s32[2]{0:T(128)} %lengths.3, ...), custom_call_target="tpu_custom_call" | custom-call | tf_op jit(solution)/shard_map/attention/pallas_call | solution.py:664
  142.0 114.0 %ffn.1 = (f32[128,2048]{1,0:T(8,128)}, bf16[8,128,2048]{2,1,0:T(8,128)(2,1)}, bf16[3,512,2048]{2,1,0:T(8,128)(2,1)}, bf16[384,2048]{1,0:T(8,128)(2,1)}) custom-call(bf16[128,2048]{1,0:T(8,128)(2,1)} %bitcast.31, f32[128,2048]{1,0:T(8,128)} %get-tuple-element.32.branch, f32[8,8,256]{2,1,0:T(8,128)} %get-tuple-element.33.gains, ...), custom_call_target="tpu_custom_call" | custom-call | tf_op jit(solution)/shard_map/ffn/pallas_call | solution.py:865
  256.0 152.5 %attention_grad.1 = (bf16[128,2048]{1,0:T(8,128)(2,1)}, bf16[128,2048]{1,0:T(8,128)(2,1)}, f32[8,256]{1,0:T(8,128)}, bf16[3,1024,2048]{2,1,0:T(8,128)(2,1)}, bf1...) custom-call(s32[2]{0:T(128)} %lengths.3, bf16[128,2048]{1,0:T(8,128)(2,1)} %bitcast.32, ...), custom_call_target="tpu_custom_call" | custom-call | tf_op jit(solution)/shard_map/attention_grad/pallas_call | solution.py:1248
  408.5 0.0 copy-start
  408.5 12.1 %bitcast_convert_fusion = (f32[1024,2048]{1,0:T(8,128)}, f32[1024,2048]{1,0:T(8,128)}, f32[1024,2048]{1,0:T(8,128)}) fusion(bf16[3,1024,2048]{2,1,0:T(8,128)(2,1)} %get-tuple-element.52), kind=kLoop, calls=%fused_computation | loop fusion | flops 6291456 | bytes 37748736 | tf_op jit(solution)/shard_map/convert_element_type | solution.py:1673
  420.6 0.0 copy-start.1
  420.6 0.0 copy-done
  420.6 0.0 copy-start.3
  420.7 0.0 copy-start.2
  420.7 2.5 bitcast_convert_fusion.3
  423.2 0.0 copy-done.1
  423.2 1.6 bitcast_convert_fusion.5
  424.8 1.3 fusion
  426.1 0.0 copy-done.3
  426.1 0.8 copy.26
  426.9 0.0 copy-done.2
  426.9 0.8 copy.27
Async XLA Ops:
  408.5 12.1 %copy-start = (bf16[2,256,2048]{2,1,0:T(8,128)(2,1)S(1)}, bf16[2,256,2048]{2,1,0:T(8,128)(2,1)}, u32[]{:S(2)}) copy-start(bf16[2,256,2048]{2,1,0:T(8,128)(2,1)} %get-tuple-element.50) | copy-start | bytes 6291460
  420.6 2.6 copy-start.1
  420.6 5.5 %copy-start.3 = (bf16[128,2048]{1,0:T(8,128)(2,1)S(1)}, bf16[128,2048]{1,0:T(8,128)(2,1)}, u32[]{:S(2)}) copy-start(bf16[128,2048]{1,0:T(8,128)(2,1)} %get-tuple-element.47) | copy-start | bytes 1572868
  420.7 6.2 %copy-start.2 = (bf16[128,2048]{1,0:T(8,128)(2,1)S(1)}, bf16[128,2048]{1,0:T(8,128)(2,1)}, u32[]{:S(2)}) copy-start(bf16[128,2048]{1,0:T(8,128)(2,1)} %get-tuple-element.48) | copy-start | bytes 1572868

commit v11 on v10

--- a/solution.py
+++ b/solution.py
@@ -79,6 +79,13 @@
         return self.near(self.line - 1 - i)
 
     def greet(self, groups):
+        self.arrive(groups)
+        self.meet(groups)
+
+    def meet(self, groups):
+        pl.semaphore_wait(pltpu.get_barrier_semaphore(), 2 * self.line + groups - 2)
+
+    def arrive(self, groups):
         barrier = pltpu.get_barrier_semaphore()
         count = 2 * self.line
         rank = lax.axis_index("grp")
@@ -96,7 +103,6 @@
                 device_id={"grp": lax.rem(rank + step, groups)},
                 device_id_type=MESH,
             )
-        pl.semaphore_wait(barrier, count + groups - 2)
 
 
 class Gather:
@@ -491,12 +497,13 @@
             )
         )
     ]
+    p.arrive(groups)
     start_all(loads)
-    p.greet(groups)
 
     small[...] = jnp.zeros_like(small)
     small[0:1] = pre_gain[...].astype(F32)[None, :]
     small[1:2] = mid_gain[...].astype(F32)[None, :]
+    p.meet(groups)
 
     def small_copy(step, peer, origin):
         return to_peer(
@@ -710,48 +717,46 @@
     loads = [
         pltpu.make_async_copy(src, dst, load_sem.at[i])
         for i, (src, dst) in enumerate(
-            ((gate_hbm, gate_w), (up_hbm, up_w), (cot_hbm, cot), (down_hbm, down_w))
+            ((cot_hbm, cot), (down_hbm, down_w), (gate_hbm, gate_w), (up_hbm, up_w))
         )
     ]
+    p.arrive(groups)
     start_all(loads)
     middle = tokens[...].astype(F32) + branch[...]
     own[...] = (middle * inverse_rms(middle) * gain_row(gains, 1)).astype(own.dtype)
-    p.greet(groups)
+    p.meet(groups)
     gather = Gather(p, own, normed, *scratch[:3])
-    gather.start()
-    wait_all(loads)
+    gather.send_own()
+    wait_all(loads[:2])
     rows = own.shape[0]
     pair = 2 * rows
     low = own.dtype
 
-    def branch_rows(block, count):
-        size = count * rows
-        x = normed[pl.ds(block, count)].reshape(size, -1)
+    @pl.loop(0, line)
+    def _(d):
+        at = pl.ds(pl.multiple_of(d * pair, pair), pair)
+        gate_g[at] = dot_t(cot[pl.ds(2 * d, 2)].reshape(pair, -1), down_w[...]).astype(low)
+
+    gather.pass_rest()
+    wait_all(loads[2:])
+
+    @pl.loop(0, line)
+    def _(i):
+        gather.hop(i + 1)
+        d = p.near(i)
+        gather.whole(d)
+        x = normed[pl.ds(2 * d, 2)].reshape(pair, -1)
         g = dot_t(x, gate_w[...])
         u = dot_t(x, up_w[...])
-        dh = dot_t(cot[pl.ds(block, count)].reshape(size, -1), down_w[...])
         s = 1.0 / (1.0 + jnp.exp(-g))
         silu = g * s
-        at = pl.ds(pl.multiple_of(block * rows, rows), size)
+        at = pl.ds(pl.multiple_of(d * pair, pair), pair)
+        dh = gate_g[at].astype(F32)
         hidden[at] = (silu * u).astype(low)
         up_g[at] = (dh * silu).astype(low)
         gate_g[at] = (dh * u * s * (1.0 + g * (1.0 - s))).astype(low)
         part = dot(gate_g[at], gate_w[...]) + dot(up_g[at], up_w[...])
-        parts[pl.ds(block, count)] = part.astype(low).reshape(count, rows, -1)
-
-    @pl.loop(0, line - 1)
-    def _(i):
-        gather.hop(i + 1)
-        d = p.near(i)
-        gather.whole(d)
-        branch_rows(2 * d, 2)
-
-    last = p.far(0)
-
-    @pl.loop(0, 2)
-    def _(i):
-        either(i == 1, lambda: gather.whole(last))
-        branch_rows(2 * last + lax.rem(p.y + i, 2), 1)
+        parts[pl.ds(2 * d, 2)] = part.astype(low).reshape(2, rows, -1)
 
     reduce = Reduce(p, parts, second, scratch[9:])
     for i in range(line):
@@ -920,6 +925,7 @@
             )
         )
     ]
+    p.arrive(groups)
     start_all(loads)
 
     def load_sum(i):
@@ -939,7 +945,7 @@
     for b in range(count):
         gain_held[b] = jnp.zeros(gain_held.shape[1:], F32)
         gain_held[b, 1:2] = mid_total[:, b * share : (b + 1) * share]
-    p.greet(groups)
+    p.meet(groups)
     gather = Gather(p, own, dbranch, *scratch[:3])
     n_sums = sums_hbm.shape[0]
     part_rows = sums.shape[1]
@@ -1107,21 +1113,6 @@
 
     for i in range(seqs, line - 1):
         ffn_sum.hop(i)
-    attn_pair(0, (0, 1))
-    ffn_sum.finish()
-    reduce = Reduce(p, parts, first, scratch[17 + n :])
-    for i in range(DEPTH):
-        reduce.send_across(i)
-    for i in range(line - 1):
-        reduce.b_hop(i)
-
-    def summed(which):
-        return (halves[p.y, which].astype(F32) + half_in[which].astype(F32)).astype(low)
-
-    valid = row_valid(p, lengths, rows)
-    result = tokens[...].astype(F32) + branch[...] + ffn_own[...]
-    mixed[...] = jnp.where(valid, result, jnp.zeros_like(result)).astype(low)
-
     def back(i):
         per_half = n_sums // 3
         start = core * per_half * part_rows + lax.rem(i, per_half) * part_rows
@@ -1177,14 +1168,30 @@
         for step in range(1, groups):
             gain_group(step, lax.rem(rank + step, groups), rank).start()
 
+    sum_up(0, n_sums // 3)
+    attn_pair(0, (0, 1))
+    gain_first()
+    ffn_sum.finish()
+    reduce = Reduce(p, parts, first, scratch[17 + n :])
+    for i in range(DEPTH):
+        reduce.send_across(i)
+    for i in range(line - 1):
+        reduce.b_hop(i)
+
+    def summed(which):
+        return (halves[p.y, which].astype(F32) + half_in[which].astype(F32)).astype(low)
+
+    valid = row_valid(p, lengths, rows)
+    result = tokens[...].astype(F32) + branch[...] + ffn_own[...]
+    mixed[...] = jnp.where(valid, result, jnp.zeros_like(result)).astype(low)
+
     swap().wait_recv()
     gradient(4, summed(0), normed)
     gradient(5, summed(1), normed)
     reduce.hop(0)
     reduce.send_across(DEPTH)
     attn_pair(1, (2,))
-    gain_first()
-    sum_up(0, n_sums // 2)
+    sum_up(n_sums // 3, n_sums // 2)
     reduce.hop(1)
     reduce.send_across(DEPTH + 1)
     gain_second()
@@ -1193,6 +1200,7 @@
     sum_up(n_sums - 3, n_sums)
     attn_total(0)
     reduce.finish()
+    attn_total(1)
     for step in range(1, groups):
         gain_group(step, rank, lax.rem(rank + groups - step, groups)).wait_recv()
     total = gain_all[0]
@@ -1202,7 +1210,6 @@
     source = tokens[...].astype(F32)
     inner = norm_grad(source, inverse_rms(source), gain_row(gains, 0), first[...])
     input_grad[...] = (middle_grad[...] + inner).astype(low)
-    attn_total(1)
     reduce.drain()
     ffn_sum.drain()
     swap().wait_send()

time: 428 us -> 419 us (0.979)
  Pallas kernels: 408 us -> 398 us
    pallas_call x1, Pallas kernels: 114 us -> 108 us  [ffn(): pl.pallas_call(functools.partial(ffn_kernel, line, groups), out_shape=(sh...]
where the time goes in v11:
time: 419 us; the launch traced here: 418 us
  Pallas kernels  398 us (95%)
  other arithmetic  16.2 us (4%)
    pallas_call x1, Pallas kernels, attention_grad(): pl.pallas_call(functools.partial(attention_grad_kernel, line, groups, seq...  149 us
    pallas_call x1, Pallas kernels, attention(): pl.pallas_call(functools.partial(attention_kernel, line, groups, seqs), o...  141 us
    pallas_call x1, Pallas kernels, ffn(): pl.pallas_call(functools.partial(ffn_kernel, line, groups), out_shape=(sh...  108 us
    convert_element_type x1, other arithmetic, local_heads(): totals[0].astype(f32)  12.1 us

profile of v11, /device:TPU:0, one launch (start us, length us, event | category | flops | bytes accessed | tf_op | source)
XLA Modules:
  0.0 418.2 jit_solution(11609382994425174117)
XLA Ops:
  0.6 141.4 %attention.1 = (f32[128,2048]{1,0:T(8,128)}, f32[8,8,256]{2,1,0:T(8,128)}, bf16[8,128,2048]{2,1,0:T(8,128)(2,1)}, bf16[8,128,2048]{2,1,0:T(8,128)(2,1)}, bf16[2,...) custom-call(s32[2]{0:T(128)} %lengths.3, ...), custom_call_target="tpu_custom_call" | custom-call | tf_op jit(solution)/shard_map/attention/pallas_call | solution.py:671
  142.0 107.7 %ffn.1 = (f32[128,2048]{1,0:T(8,128)}, bf16[8,128,2048]{2,1,0:T(8,128)(2,1)}, bf16[3,512,2048]{2,1,0:T(8,128)(2,1)}, bf16[384,2048]{1,0:T(8,128)(2,1)}) custom-call(bf16[128,2048]{1,0:T(8,128)(2,1)} %bitcast.31, f32[128,2048]{1,0:T(8,128)} %get-tuple-element.32.branch, f32[8,8,256]{2,1,0:T(8,128)} %get-tuple-element.33.gains, ...), custom_call_target="tpu_custom_call" | custom-call | tf_op jit(solution)/shard_map/ffn/pallas_call | solution.py:870
  249.7 149.3 %attention_grad.1 = (bf16[128,2048]{1,0:T(8,128)(2,1)}, bf16[128,2048]{1,0:T(8,128)(2,1)}, f32[8,256]{1,0:T(8,128)}, bf16[3,1024,2048]{2,1,0:T(8,128)(2,1)}, bf1...) custom-call(s32[2]{0:T(128)} %lengths.3, bf16[128,2048]{1,0:T(8,128)(2,1)} %bitcast.32, ...), custom_call_target="tpu_custom_call" | custom-call | tf_op jit(solution)/shard_map/attention_grad/pallas_call | solution.py:1255
  399.0 0.0 copy-start
  399.0 12.1 %bitcast_convert_fusion = (f32[1024,2048]{1,0:T(8,128)}, f32[1024,2048]{1,0:T(8,128)}, f32[1024,2048]{1,0:T(8,128)}) fusion(bf16[3,1024,2048]{2,1,0:T(8,128)(2,1)} %get-tuple-element.52), kind=kLoop, calls=%fused_computation | loop fusion | flops 6291456 | bytes 37748736 | tf_op jit(solution)/shard_map/convert_element_type | solution.py:1680
  411.2 0.0 copy-start.1
  411.2 0.0 copy-done
  411.2 0.0 copy-start.3
  411.2 0.0 copy-start.2
  411.2 2.5 bitcast_convert_fusion.3
  413.7 0.0 copy-done.1
  413.7 1.6 bitcast_convert_fusion.5
  415.3 1.3 fusion
  416.6 0.0 copy-done.3
  416.6 0.8 copy.26
  417.4 0.0 copy-done.2
  417.4 0.8 copy.27
Async XLA Ops:
  399.0 12.1 %copy-start = (bf16[2,256,2048]{2,1,0:T(8,128)(2,1)S(1)}, bf16[2,256,2048]{2,1,0:T(8,128)(2,1)}, u32[]{:S(2)}) copy-start(bf16[2,256,2048]{2,1,0:T(8,128)(2,1)} %get-tuple-element.50) | copy-start | bytes 6291460
  411.2 2.6 copy-start.1
  411.2 5.5 %copy-start.3 = (bf16[128,2048]{1,0:T(8,128)(2,1)S(1)}, bf16[128,2048]{1,0:T(8,128)(2,1)}, u32[]{:S(2)}) copy-start(bf16[128,2048]{1,0:T(8,128)(2,1)} %get-tuple-element.47) | copy-start | bytes 1572868
  411.2 6.2 %copy-start.2 = (bf16[128,2048]{1,0:T(8,128)(2,1)S(1)}, bf16[128,2048]{1,0:T(8,128)(2,1)}, u32[]{:S(2)}) copy-start(bf16[128,2048]{1,0:T(8,128)(2,1)} %get-tuple-element.48) | copy-start | bytes 1572868

commit v12 on v11

--- a/solution.py
+++ b/solution.py
@@ -103,6 +103,23 @@
                 device_id={"grp": lax.rem(rank + step, groups)},
                 device_id_type=MESH,
             )
+
+
+    def arrive_near(self, ranks):
+        barrier = pltpu.get_barrier_semaphore()
+
+        def signal(**peer):
+            pl.semaphore_signal(barrier, inc=1, device_id=peer, device_id_type=MESH)
+
+        signal(shard=self.cross)
+        either(self.z > 0, lambda: signal(shard=self.me - 2))
+        either(self.z < self.line - 1, lambda: signal(shard=self.me + 2))
+        for rank in ranks:
+            signal(grp=rank)
+
+    def meet_near(self, ranks):
+        ends = jnp.where(self.z > 0, 1, 0) + jnp.where(self.z < self.line - 1, 1, 0)
+        pl.semaphore_wait(pltpu.get_barrier_semaphore(), 1 + len(ranks) + ends)
 
 
 class Gather:
@@ -720,11 +737,11 @@
             ((cot_hbm, cot), (down_hbm, down_w), (gate_hbm, gate_w), (up_hbm, up_w))
         )
     ]
-    p.arrive(groups)
+    p.arrive_near((partner, opposite))
     start_all(loads)
     middle = tokens[...].astype(F32) + branch[...]
     own[...] = (middle * inverse_rms(middle) * gain_row(gains, 1)).astype(own.dtype)
-    p.meet(groups)
+    p.meet_near((partner, opposite))
     gather = Gather(p, own, normed, *scratch[:3])
     gather.send_own()
     wait_all(loads[:2])

time: 419 us -> 418 us (level)
  no operation moved by 1% of the time
where the time goes in v12:
time: 418 us
  Pallas kernels  398 us (95%)
  other arithmetic  16.2 us (4%)
    pallas_call x1, Pallas kernels, attention_grad(): pl.pallas_call(functools.partial(attention_grad_kernel, line, groups, seq...  149 us
    pallas_call x1, Pallas kernels, attention(): pl.pallas_call(functools.partial(attention_kernel, line, groups, seqs), o...  141 us
    pallas_call x1, Pallas kernels, ffn(): pl.pallas_call(functools.partial(ffn_kernel, line, groups), out_shape=(sh...  107 us
    convert_element_type x1, other arithmetic, local_heads(): totals[0].astype(f32)  12.1 us

profile of v12, /device:TPU:0, one launch (start us, length us, event | category | flops | bytes accessed | tf_op | source)
XLA Modules:
  0.0 417.7 jit_solution(11936124080899707879)
XLA Ops:
  0.6 141.2 %attention.1 = (f32[128,2048]{1,0:T(8,128)}, f32[8,8,256]{2,1,0:T(8,128)}, bf16[8,128,2048]{2,1,0:T(8,128)(2,1)}, bf16[8,128,2048]{2,1,0:T(8,128)(2,1)}, bf16[2,...) custom-call(s32[2]{0:T(128)} %lengths.3, ...), custom_call_target="tpu_custom_call" | custom-call | tf_op jit(solution)/shard_map/attention/pallas_call | solution.py:688
  141.8 107.1 %ffn.1 = (f32[128,2048]{1,0:T(8,128)}, bf16[8,128,2048]{2,1,0:T(8,128)(2,1)}, bf16[3,512,2048]{2,1,0:T(8,128)(2,1)}, bf16[384,2048]{1,0:T(8,128)(2,1)}) custom-call(bf16[128,2048]{1,0:T(8,128)(2,1)} %bitcast.31, f32[128,2048]{1,0:T(8,128)} %get-tuple-element.32.branch, f32[8,8,256]{2,1,0:T(8,128)} %get-tuple-element.33.gains, ...), custom_call_target="tpu_custom_call" | custom-call | tf_op jit(solution)/shard_map/ffn/pallas_call | solution.py:887
  249.0 149.5 %attention_grad.1 = (bf16[128,2048]{1,0:T(8,128)(2,1)}, bf16[128,2048]{1,0:T(8,128)(2,1)}, f32[8,256]{1,0:T(8,128)}, bf16[3,1024,2048]{2,1,0:T(8,128)(2,1)}, bf1...) custom-call(s32[2]{0:T(128)} %lengths.3, bf16[128,2048]{1,0:T(8,128)(2,1)} %bitcast.32, ...), custom_call_target="tpu_custom_call" | custom-call | tf_op jit(solution)/shard_map/attention_grad/pallas_call | solution.py:1272
  398.5 0.0 copy-start
  398.5 12.1 %bitcast_convert_fusion = (f32[1024,2048]{1,0:T(8,128)}, f32[1024,2048]{1,0:T(8,128)}, f32[1024,2048]{1,0:T(8,128)}) fusion(bf16[3,1024,2048]{2,1,0:T(8,128)(2,1)} %get-tuple-element.52), kind=kLoop, calls=%fused_computation | loop fusion | flops 6291456 | bytes 37748736 | tf_op jit(solution)/shard_map/convert_element_type | solution.py:1697
  410.6 0.0 copy-start.1
  410.6 0.0 copy-done
  410.6 0.0 copy-start.3
  410.6 0.0 copy-start.2
  410.6 2.5 bitcast_convert_fusion.3
  413.2 0.0 copy-done.1
  413.2 1.6 bitcast_convert_fusion.5
  414.7 1.3 fusion
  416.1 0.0 copy-done.3
  416.1 0.8 copy.26
  416.9 0.0 copy-done.2
  416.9 0.8 copy.27
Async XLA Ops:
  398.5 12.1 %copy-start = (bf16[2,256,2048]{2,1,0:T(8,128)(2,1)S(1)}, bf16[2,256,2048]{2,1,0:T(8,128)(2,1)}, u32[]{:S(2)}) copy-start(bf16[2,256,2048]{2,1,0:T(8,128)(2,1)} %get-tuple-element.50) | copy-start | bytes 6291460
  410.6 2.6 copy-start.1
  410.6 5.5 %copy-start.3 = (bf16[128,2048]{1,0:T(8,128)(2,1)S(1)}, bf16[128,2048]{1,0:T(8,128)(2,1)}, u32[]{:S(2)}) copy-start(bf16[128,2048]{1,0:T(8,128)(2,1)} %get-tuple-element.47) | copy-start | bytes 1572868
  410.6 6.2 %copy-start.2 = (bf16[128,2048]{1,0:T(8,128)(2,1)S(1)}, bf16[128,2048]{1,0:T(8,128)(2,1)}, u32[]{:S(2)}) copy-start(bf16[128,2048]{1,0:T(8,128)(2,1)} %get-tuple-element.48) | copy-start | bytes 1572868

commit v13 on v12

--- a/solution.py
+++ b/solution.py
@@ -809,6 +809,12 @@
     def save_pair(which):
         return pltpu.make_async_copy(mine(which), pair_hbm.at[which], out_sem.at[which])
 
+    def core_sum(which):
+        for j in range(2):
+            to_partner(which, j).wait_recv()
+        total_into(mine(which), mine(which), theirs.at[which])
+        save_pair(which).start()
+
     @pl.loop(0, 3)
     def _(which):
         right = rights.at[jnp.minimum(which, 1)]
@@ -829,6 +835,8 @@
             for i in range(line - 1):
                 reduce.b_hop(i)
 
+        either(which > 1, lambda: core_sum(which - 1))
+
         at_end = p.low_end | p.high_end
         either(at_end, lambda: reduce.step(which, 0))
 
@@ -842,17 +850,17 @@
             for c in range(1, CHUNKS):
                 reduce.step(which, c)
 
-        for j in range(2):
-            to_partner(which, j).wait_recv()
-        total_into(mine(which), mine(which), theirs.at[which])
-        either(which == 0, lambda: chip_copy().start())
-        save_pair(which).start()
+        @pl.when(which == 0)
+        def _():
+            core_sum(0)
+            chip_copy().start()
 
         @pl.when(jnp.logical_not(at_end))
         def _():
             for c in range(CHUNKS):
                 reduce.step(which, c)
 
+    core_sum(2)
     gather.drain()
 
     @pl.loop(0, line)

time: 418 us -> 417 us (level)
  no operation moved by 1% of the time
where the time goes in v13:
time: 417 us
  Pallas kernels  397 us (95%)
  other arithmetic  16.2 us (4%)
    pallas_call x1, Pallas kernels, attention_grad(): pl.pallas_call(functools.partial(attention_grad_kernel, line, groups, seq...  150 us
    pallas_call x1, Pallas kernels, attention(): pl.pallas_call(functools.partial(attention_kernel, line, groups, seqs), o...  141 us
    pallas_call x1, Pallas kernels, ffn(): pl.pallas_call(functools.partial(ffn_kernel, line, groups), out_shape=(sh...  106 us
    convert_element_type x1, other arithmetic, local_heads(): totals[0].astype(f32)  12.1 us

profile of v13, /device:TPU:0, one launch (start us, length us, event | category | flops | bytes accessed | tf_op | source)
XLA Modules:
  0.0 416.9 jit_solution(2063179788434966734)
XLA Ops:
  0.6 141.2 %attention.1 = (f32[128,2048]{1,0:T(8,128)}, f32[8,8,256]{2,1,0:T(8,128)}, bf16[8,128,2048]{2,1,0:T(8,128)(2,1)}, bf16[8,128,2048]{2,1,0:T(8,128)(2,1)}, bf16[2,...) custom-call(s32[2]{0:T(128)} %lengths.3, ...), custom_call_target="tpu_custom_call" | custom-call | tf_op jit(solution)/shard_map/attention/pallas_call | solution.py:688
  141.8 106.2 %ffn.1 = (f32[128,2048]{1,0:T(8,128)}, bf16[8,128,2048]{2,1,0:T(8,128)(2,1)}, bf16[3,512,2048]{2,1,0:T(8,128)(2,1)}, bf16[384,2048]{1,0:T(8,128)(2,1)}) custom-call(bf16[128,2048]{1,0:T(8,128)(2,1)} %bitcast.31, f32[128,2048]{1,0:T(8,128)} %get-tuple-element.32.branch, f32[8,8,256]{2,1,0:T(8,128)} %get-tuple-element.33.gains, ...), custom_call_target="tpu_custom_call" | custom-call | tf_op jit(solution)/shard_map/ffn/pallas_call | solution.py:895
  248.0 149.6 %attention_grad.1 = (bf16[128,2048]{1,0:T(8,128)(2,1)}, bf16[128,2048]{1,0:T(8,128)(2,1)}, f32[8,256]{1,0:T(8,128)}, bf16[3,1024,2048]{2,1,0:T(8,128)(2,1)}, bf1...) custom-call(s32[2]{0:T(128)} %lengths.3, bf16[128,2048]{1,0:T(8,128)(2,1)} %bitcast.32, ...), custom_call_target="tpu_custom_call" | custom-call | tf_op jit(solution)/shard_map/attention_grad/pallas_call | solution.py:1280
  397.7 0.0 copy-start
  397.7 12.1 %bitcast_convert_fusion = (f32[1024,2048]{1,0:T(8,128)}, f32[1024,2048]{1,0:T(8,128)}, f32[1024,2048]{1,0:T(8,128)}) fusion(bf16[3,1024,2048]{2,1,0:T(8,128)(2,1)} %get-tuple-element.52), kind=kLoop, calls=%fused_computation | loop fusion | flops 6291456 | bytes 37748736 | tf_op jit(solution)/shard_map/convert_element_type | solution.py:1705
  409.8 0.0 copy-start.1
  409.8 0.0 copy-done
  409.8 0.0 copy-start.3
  409.8 0.0 copy-start.2
  409.8 2.5 bitcast_convert_fusion.3
  412.4 0.0 copy-done.1
  412.4 1.6 bitcast_convert_fusion.5
  413.9 1.3 fusion
  415.3 0.0 copy-done.3
  415.3 0.8 copy.26
  416.1 0.0 copy-done.2
  416.1 0.8 copy.27
Async XLA Ops:
  397.7 12.1 %copy-start = (bf16[2,256,2048]{2,1,0:T(8,128)(2,1)S(1)}, bf16[2,256,2048]{2,1,0:T(8,128)(2,1)}, u32[]{:S(2)}) copy-start(bf16[2,256,2048]{2,1,0:T(8,128)(2,1)} %get-tuple-element.50) | copy-start | bytes 6291460
  409.8 2.6 copy-start.1
  409.8 5.5 %copy-start.3 = (bf16[128,2048]{1,0:T(8,128)(2,1)S(1)}, bf16[128,2048]{1,0:T(8,128)(2,1)}, u32[]{:S(2)}) copy-start(bf16[128,2048]{1,0:T(8,128)(2,1)} %get-tuple-element.47) | copy-start | bytes 1572868
  409.8 6.2 %copy-start.2 = (bf16[128,2048]{1,0:T(8,128)(2,1)S(1)}, bf16[128,2048]{1,0:T(8,128)(2,1)}, u32[]{:S(2)}) copy-start(bf16[128,2048]{1,0:T(8,128)(2,1)} %get-tuple-element.48) | copy-start | bytes 1572868

commit v14 on v13

--- a/solution.py
+++ b/solution.py
@@ -1193,9 +1193,9 @@
         for step in range(1, groups):
             gain_group(step, lax.rem(rank + step, groups), rank).start()
 
+    gain_first()
     sum_up(0, n_sums // 3)
     attn_pair(0, (0, 1))
-    gain_first()
     ffn_sum.finish()
     reduce = Reduce(p, parts, first, scratch[17 + n :])
     for i in range(DEPTH):
@@ -1215,8 +1215,8 @@
     gradient(5, summed(1), normed)
     reduce.hop(0)
     reduce.send_across(DEPTH)
+    sum_up(n_sums // 3, n_sums // 2)
     attn_pair(1, (2,))
-    sum_up(n_sums // 3, n_sums // 2)
     reduce.hop(1)
     reduce.send_across(DEPTH + 1)
     gain_second()

time: 417 us -> 417 us (level)
  no operation moved by 1% of the time
where the time goes in v14:
time: 417 us
  Pallas kernels  397 us (95%)
  other arithmetic  16.2 us (4%)
    pallas_call x1, Pallas kernels, attention_grad(): pl.pallas_call(functools.partial(attention_grad_kernel, line, groups, seq...  150 us
    pallas_call x1, Pallas kernels, attention(): pl.pallas_call(functools.partial(attention_kernel, line, groups, seqs), o...  141 us
    pallas_call x1, Pallas kernels, ffn(): pl.pallas_call(functools.partial(ffn_kernel, line, groups), out_shape=(sh...  106 us
    convert_element_type x1, other arithmetic, local_heads(): totals[0].astype(f32)  12.1 us

profile of v14, /device:TPU:0, one launch (start us, length us, event | category | flops | bytes accessed | tf_op | source)
XLA Modules:
  0.0 416.9 jit_solution(1429388298560981609)
XLA Ops:
  0.6 141.2 %attention.1 = (f32[128,2048]{1,0:T(8,128)}, f32[8,8,256]{2,1,0:T(8,128)}, bf16[8,128,2048]{2,1,0:T(8,128)(2,1)}, bf16[8,128,2048]{2,1,0:T(8,128)(2,1)}, bf16[2,...) custom-call(s32[2]{0:T(128)} %lengths.3, ...), custom_call_target="tpu_custom_call" | custom-call | tf_op jit(solution)/shard_map/attention/pallas_call | solution.py:688
  141.8 106.2 %ffn.1 = (f32[128,2048]{1,0:T(8,128)}, bf16[8,128,2048]{2,1,0:T(8,128)(2,1)}, bf16[3,512,2048]{2,1,0:T(8,128)(2,1)}, bf16[384,2048]{1,0:T(8,128)(2,1)}) custom-call(bf16[128,2048]{1,0:T(8,128)(2,1)} %bitcast.31, f32[128,2048]{1,0:T(8,128)} %get-tuple-element.32.branch, f32[8,8,256]{2,1,0:T(8,128)} %get-tuple-element.33.gains, ...), custom_call_target="tpu_custom_call" | custom-call | tf_op jit(solution)/shard_map/ffn/pallas_call | solution.py:895
  248.0 149.6 %attention_grad.1 = (bf16[128,2048]{1,0:T(8,128)(2,1)}, bf16[128,2048]{1,0:T(8,128)(2,1)}, f32[8,256]{1,0:T(8,128)}, bf16[3,1024,2048]{2,1,0:T(8,128)(2,1)}, bf1...) custom-call(s32[2]{0:T(128)} %lengths.3, bf16[128,2048]{1,0:T(8,128)(2,1)} %bitcast.32, ...), custom_call_target="tpu_custom_call" | custom-call | tf_op jit(solution)/shard_map/attention_grad/pallas_call | solution.py:1280
  397.7 0.0 copy-start
  397.7 12.1 %bitcast_convert_fusion = (f32[1024,2048]{1,0:T(8,128)}, f32[1024,2048]{1,0:T(8,128)}, f32[1024,2048]{1,0:T(8,128)}) fusion(bf16[3,1024,2048]{2,1,0:T(8,128)(2,1)} %get-tuple-element.52), kind=kLoop, calls=%fused_computation | loop fusion | flops 6291456 | bytes 37748736 | tf_op jit(solution)/shard_map/convert_element_type | solution.py:1705
  409.8 0.0 copy-start.1
  409.8 0.0 copy-done
  409.8 0.0 copy-start.3
  409.8 0.0 copy-start.2
  409.8 2.5 bitcast_convert_fusion.3
  412.4 0.0 copy-done.1
  412.4 1.6 bitcast_convert_fusion.5
  413.9 1.3 fusion
  415.3 0.0 copy-done.3
  415.3 0.8 copy.26
  416.1 0.0 copy-done.2
  416.1 0.8 copy.27
Async XLA Ops:
  397.7 12.1 %copy-start = (bf16[2,256,2048]{2,1,0:T(8,128)(2,1)S(1)}, bf16[2,256,2048]{2,1,0:T(8,128)(2,1)}, u32[]{:S(2)}) copy-start(bf16[2,256,2048]{2,1,0:T(8,128)(2,1)} %get-tuple-element.50) | copy-start | bytes 6291460
  409.8 2.6 copy-start.1
  409.8 5.5 %copy-start.3 = (bf16[128,2048]{1,0:T(8,128)(2,1)S(1)}, bf16[128,2048]{1,0:T(8,128)(2,1)}, u32[]{:S(2)}) copy-start(bf16[128,2048]{1,0:T(8,128)(2,1)} %get-tuple-element.47) | copy-start | bytes 1572868
  409.8 6.2 %copy-start.2 = (bf16[128,2048]{1,0:T(8,128)(2,1)S(1)}, bf16[128,2048]{1,0:T(8,128)(2,1)}, u32[]{:S(2)}) copy-start(bf16[128,2048]{1,0:T(8,128)(2,1)} %get-tuple-element.48) | copy-start | bytes 1572868
